TPU v7x, 32 devices: a whole 2x2x4 slice. The times are simulated.
32 devices in a mesh: dp: 8 (over z, x), blk: 4 (over y, core).
Axes of the slice: x: 2, y: 2, z: 4, core: 2. Of those that a mesh axis runs over, the one named last changes fastest.
Arguments:
- block_input: float32 [73728, 512], P('dp', 'blk'), may hold values from -6 to 6
- cotangent: float32 [73728, 512], P('dp', 'blk'), may hold values from -6 to 6
- item_sides: int32 [8], P('dp'), may hold values from 48 to 96, as said below
- item_modes: int32 [8], P('dp'), may hold values from 12 to 32, as said below
- ln1_gain: float32 [512], P('blk'), may hold values from 0.1 to 1.9
- ln1_bias: float32 [512], P('blk'), may hold values from -3 to 3
- spec_w1: float32 [2, 8, 64, 64], P(None, 'blk'), may hold values from -0.5 to 0.5
- spec_b1: float32 [2, 8, 64], P(None, 'blk'), may hold values from -3 to 3
- spec_w2: float32 [2, 8, 64, 64], P(None, 'blk'), may hold values from -0.5 to 0.5
- spec_b2: float32 [2, 8, 64], P(None, 'blk'), may hold values from -3 to 3
- ln2_gain: float32 [512], P('blk'), may hold values from 0.1 to 1.9
- ln2_bias: float32 [512], P('blk'), may hold values from -3 to 3
- mlp_w1: float32 [512, 2048], P(None, 'blk'), may hold values from -0.25 to 0.25
- mlp_b1: float32 [2048], P('blk'), may hold values from -3 to 3
- mlp_w2: float32 [2048, 512], P('blk'), may hold values from -0.125 to 0.125
- mlp_b2: float32 [512], P('blk'), may hold values from -3 to 3
Outputs:
- block_output: float32 [73728, 512], P('dp', 'blk')
- input_grad: float32 [73728, 512], P('dp', 'blk')
- ln1_gain_grad: float32 [512], P('blk')
- ln1_bias_grad: float32 [512], P('blk')
- spec_w1_grad: float32 [2, 8, 64, 64], P(None, 'blk')
- spec_b1_grad: float32 [2, 8, 64], P(None, 'blk')
- spec_w2_grad: float32 [2, 8, 64, 64], P(None, 'blk')
- spec_b2_grad: float32 [2, 8, 64], P(None, 'blk')
- ln2_gain_grad: float32 [512], P('blk')
- ln2_bias_grad: float32 [512], P('blk')
- mlp_w1_grad: float32 [512, 2048], P(None, 'blk')
- mlp_b1_grad: float32 [2048], P('blk')
- mlp_w2_grad: float32 [2048, 512], P('blk')
- mlp_b2_grad: float32 [512], P('blk')
Inputs may be any that keep to these rules, and one draw needn't show every extreme that they name: `item_sides`: each item's side is 48, 72 or 96; at least one item has side 96. `item_modes`: an item of side s keeps m between max(1, s // 4) and min(32, s // 2); an item of side 96 with m = 32 is present.
All inputs are finite; a program needn't handle non-finite values.
Results may differ from a plain program's by a relative error of at most 0.0028.
Values sent between devices are 32-bit elements; how exact they have to be, the bound alone decides.
No kernel may reach another device: no remote copies, remote signals or barrier semaphores. Data moves between devices by JAX's collectives and lax.ppermute only.
A program may use at most 320 MiB of HBM per device.

v0:
```python
import math

import jax
import jax.numpy as jnp
from jax import lax
from jax.sharding import PartitionSpec as P

C = 512
MODES = 32
SMAX = 96


EPS = 1e-05
SHRINK = 0.01


def contract(form, left, right):
    return jnp.einsum(form, left, right, precision=lax.Precision.HIGHEST)


def tables(item_sides, item_modes):
    frequency = jnp.arange(2 * MODES - 1, dtype=jnp.int32) - (MODES - 1)
    cells = jnp.arange(SMAX, dtype=jnp.int32)
    extent = item_sides[:, None, None]
    phase = frequency[None, :, None] * cells[None, None, :] % extent
    keep = (jnp.abs(frequency)[None, :, None] < item_modes[:, None, None]) & (
        cells[None, None, :] < extent
    )
    length = extent.astype(jnp.float32)
    angle = 2.0 * math.pi * phase.astype(jnp.float32) / length
    scale = lax.rsqrt(length)
    cosine = jnp.where(keep, jnp.cos(angle) * scale, jnp.zeros_like(angle))
    sine = jnp.where(keep, -jnp.sin(angle) * scale, jnp.zeros_like(angle))
    return (cosine, sine)


def cell_mask(item_sides):
    cells = jnp.arange(SMAX, dtype=jnp.int32)
    extent = item_sides[:, None, None]
    inside = (cells[None, :, None] < extent) & (cells[None, None, :] < extent)
    return inside.astype(jnp.float32)


def shrink(value):
    return jnp.where(
        value > SHRINK,
        value - SHRINK,
        jnp.where(value < -SHRINK, value + SHRINK, jnp.zeros_like(value)),
    )


def gelu_exact(value):
    return jax.nn.gelu(value, approximate=False)


def complex_layer(real_in, imag_in, weight, bias):
    real_out = (
        contract("...bc,bcd->...bd", real_in, weight[0])
        - contract("...bc,bcd->...bd", imag_in, weight[1])
        + bias[0]
    )
    imag_out = (
        contract("...bc,bcd->...bd", real_in, weight[1])
        + contract("...bc,bcd->...bd", imag_in, weight[0])
        + bias[1]
    )
    return (real_out, imag_out)


def spectral(field, cosine, sine, first_w, first_b, second_w, second_b):
    real_a = contract("qjn,qnmc->qjmc", cosine, field)
    imag_a = contract("qjn,qnmc->qjmc", sine, field)
    real_x = contract("qkm,qjmc->qjkc", cosine, real_a) - contract("qkm,qjmc->qjkc", sine, imag_a)
    imag_x = contract("qkm,qjmc->qjkc", cosine, imag_a) + contract("qkm,qjmc->qjkc", sine, real_a)
    split = real_x.shape[:-1] + (first_w.shape[1], first_w.shape[2])
    real_h, imag_h = complex_layer(real_x.reshape(split), imag_x.reshape(split), first_w, first_b)
    real_h, imag_h = (gelu_exact(real_h), gelu_exact(imag_h))
    real_o, imag_o = complex_layer(real_h, imag_h, second_w, second_b)
    real_z = shrink(real_o).reshape(real_x.shape)
    imag_z = shrink(imag_o).reshape(real_x.shape)
    real_b = contract("qkm,qjkc->qjmc", cosine, real_z) + contract("qkm,qjkc->qjmc", sine, imag_z)
    imag_b = contract("qkm,qjkc->qjmc", cosine, imag_z) - contract("qkm,qjkc->qjmc", sine, real_z)
    return contract("qjn,qjmc->qnmc", cosine, real_b) + contract("qjn,qjmc->qnmc", sine, imag_b)


def dot_rows(left, right):
    return jnp.dot(left, right, precision=lax.Precision.HIGHEST)


def dot_leading(left, right):
    return lax.dot_general(left, right, (((0,), (0,)), ((), ())), precision=lax.Precision.HIGHEST)


def dot_trailing(left, right):
    return lax.dot_general(left, right, (((1,), (1,)), ((), ())), precision=lax.Precision.HIGHEST)


def norm_forward(value, gain, bias):
    total = lax.psum(jnp.sum(value, axis=1), "blk")
    centered = value - (total / C)[:, None]
    spread = lax.psum(jnp.sum(centered * centered, axis=1), "blk") / C
    inverse = lax.rsqrt(spread + EPS)
    normal = centered * inverse[:, None]
    return (normal * gain + bias, normal, inverse)


def norm_backward(grad_out, normal, inverse, gain):
    scaled = grad_out * gain
    first, second = lax.psum((jnp.sum(scaled, axis=1), jnp.sum(scaled * normal, axis=1)), "blk")
    grad_in = inverse[:, None] * (scaled - first[:, None] / C - normal * second[:, None] / C)
    return (grad_in, jnp.sum(grad_out * normal, axis=0), jnp.sum(grad_out, axis=0))


def per_device(
    block_input,
    cotangent,
    item_sides,
    item_modes,
    ln1_gain,
    ln1_bias,
    spec_w1,
    spec_b1,
    spec_w2,
    spec_b2,
    ln2_gain,
    ln2_bias,
    mlp_w1,
    mlp_b1,
    mlp_w2,
    mlp_b2,
):
    cosine, sine = tables(item_sides, item_modes)
    valid = cell_mask(item_sides).reshape(-1, 1)
    num_rows, local_width = block_input.shape
    inputs = block_input * valid
    normed, normal_one, inverse_one = norm_forward(inputs, ln1_gain, ln1_bias)

    def mixing(field, first_w, first_b, second_w, second_b):
        return spectral(field, cosine, sine, first_w, first_b, second_w, second_b)

    field = normed.reshape(1, SMAX, SMAX, local_width)
    mixed, mixing_pull = jax.vjp(mixing, field, spec_w1, spec_b1, spec_w2, spec_b2)
    middle = inputs + mixed.reshape(num_rows, local_width) + normed
    grad_out = cotangent * valid
    grad_bias_out = jnp.sum(grad_out, axis=0)
    second, normal_two, inverse_two = norm_forward(middle, ln2_gain, ln2_bias)
    second_full = lax.all_gather(second, "blk", axis=1, tiled=True)
    pre_act = dot_rows(second_full, mlp_w1) + mlp_b1
    hidden, gelu_pull = jax.vjp(gelu_exact, pre_act)
    partial_out = dot_rows(hidden, mlp_w2)
    branch = lax.psum_scatter(partial_out, "blk", scatter_dimension=1, tiled=True)
    grad_full = lax.all_gather(grad_out, "blk", axis=1, tiled=True)
    grad_proj_out = dot_leading(hidden, grad_full)
    grad_pre = gelu_pull(dot_trailing(grad_full, mlp_w2))[0]
    grad_bias_in = jnp.sum(grad_pre, axis=0)
    grad_proj_in = dot_leading(second_full, grad_pre)
    grad_second = lax.psum_scatter(
        dot_trailing(grad_pre, mlp_w1), "blk", scatter_dimension=1, tiled=True
    )
    grad_norm_two, grad_gain_two, grad_shift_two = norm_backward(
        grad_second, normal_two, inverse_two, ln2_gain
    )
    block_output = (middle + branch + mlp_b2) * valid
    grad_middle = grad_out + grad_norm_two
    mixing_grads = mixing_pull(grad_middle.reshape(1, SMAX, SMAX, local_width))
    grad_field, grad_first_w, grad_first_b, grad_second_w, grad_second_b = mixing_grads
    grad_normed = grad_field.reshape(num_rows, local_width) + grad_middle
    grad_norm_one, grad_gain_one, grad_shift_one = norm_backward(
        grad_normed, normal_one, inverse_one, ln1_gain
    )
    input_grad = (grad_middle + grad_norm_one) * valid
    summed = lax.psum(
        (
            grad_gain_one,
            grad_shift_one,
            grad_first_w,
            grad_first_b,
            grad_second_w,
            grad_second_b,
            grad_gain_two,
            grad_shift_two,
            grad_proj_in,
            grad_bias_in,
            grad_proj_out,
            grad_bias_out,
        ),
        "dp",
    )
    grad_gain_one, grad_shift_one, grad_first_w, grad_first_b, grad_second_w, grad_second_b = (
        summed[0],
        summed[1],
        summed[2],
        summed[3],
        summed[4],
        summed[5],
    )
    grad_gain_two, grad_shift_two, grad_proj_in, grad_bias_in, grad_proj_out, grad_bias_out = (
        summed[6],
        summed[7],
        summed[8],
        summed[9],
        summed[10],
        summed[11],
    )
    return (
        block_output,
        input_grad,
        grad_gain_one,
        grad_shift_one,
        grad_first_w,
        grad_first_b,
        grad_second_w,
        grad_second_b,
        grad_gain_two,
        grad_shift_two,
        grad_proj_in,
        grad_bias_in,
        grad_proj_out,
        grad_bias_out,
    )


def solution(mesh):
    in_specs = (
        P("dp", "blk"),
        P("dp", "blk"),
        P("dp"),
        P("dp"),
        P("blk"),
        P("blk"),
        P(None, "blk", None, None),
        P(None, "blk", None),
        P(None, "blk", None, None),
        P(None, "blk", None),
        P("blk"),
        P("blk"),
        P(None, "blk"),
        P("blk"),
        P("blk", None),
        P("blk"),
    )
    out_specs = (
        P("dp", "blk"),
        P("dp", "blk"),
        P("blk"),
        P("blk"),
        P(None, "blk", None, None),
        P(None, "blk", None),
        P(None, "blk", None, None),
        P(None, "blk", None),
        P("blk"),
        P("blk"),
        P(None, "blk"),
        P("blk"),
        P("blk", None),
        P("blk"),
    )
    return jax.shard_map(
        per_device, mesh=mesh, in_specs=in_specs, out_specs=out_specs, check_vma=False
    )
```

profile of v0, /device:TPU:0, one launch (start us, length us, event | category | flops | bytes accessed | tf_op | source)
XLA Modules:
  0.0 1436.6 jit_solution(9488161537855846429)
XLA Ops:
  9.1 6.8 multiply_reduce_fusion.8
  16.0 13.2 psum.140
  29.2 7.6 multiply_reduce_fusion.5
  36.8 10.5 psum.141
  47.4 7.2 fusion.698
  60.9 6.7 fusion.15
  92.4 7.0 copy.97
  103.6 7.1 copy.99
  110.6 8.9 fusion.261
  119.5 6.6 convolution_add_fusion
  126.1 13.1 fusion.82
  139.3 14.2 fusion.84
  153.5 6.7 fusion.256
  160.3 6.8 convolution_subtract_fusion
  167.1 15.0 %fusion.78 = (f32[1,63,63,2,64]{4,2,1,3,0:T(8,128)S(1)}, f32[2,64,1,63,63]{1,4,3,0,2:T(8,128)}) fusion(f32[2,64]{1,0:T(2,128)S(1)} %get-tuple-element.51, f32[2,63,63,64]{3,2,1,0:T(8,128)S(1)} %fusion.82, f32[2,2,64,64]{3,2,1,0:T(8,128)S(1)} %copy-done.50, f32[2,64]{1,0:T(2,128)S(1)} %get-tuple-element.52, f32[2,63,63,64]{3,2,1,0:T(8,128)S(1)} %convolution_subtract_fusion), kind=kOutput, calls=%fused_computation.130 | convolution fusion | flops 427254912 | bytes 12389376 | tf_op jit(solution)/shard_map/jvp(...bc,bcd->...bd)/dot_general | solution.py:18
  196.5 17.1 %fusion.79 = (f32[1,63,63,2,64]{4,2,1,3,0:T(8,128)S(1)}, f32[2,64,1,63,63]{1,4,3,0,2:T(8,128)}) fusion(f32[2,64]{1,0:T(2,128)S(1)} %get-tuple-element.50, f32[2,63,63,64]{3,2,1,0:T(8,128)} %fusion.84, f32[2,2,64,64]{3,2,1,0:T(8,128)S(1)} %copy-done.50, f32[2,64]{1,0:T(2,128)S(1)} %get-tuple-element.52, f32[2,63,63,64]{3,2,1,0:T(8,128)S(1)} %copy-done.17), kind=kOutput, calls=%fused_computation.132 | convolution fusion | flops 427254912 | bytes 10292736 | tf_op jit(solution)/shard_map/jvp(...bc,bcd->...bd)/dot_general | solution.py:18
  260.2 10.5 psum.142
  275.4 10.5 psum.143
  286.5 8.3 multiply_add_fusion.2
  295.7 122.9 %all-gather.3.cloned.1.call-done = f32[9216,512]{1,0:T(8,128)} async-done(((f32[9216,128]{1,0:T(8,128)}), f32[9216,512]{1,0:T(8,128)}) %all-gather.3.cloned.1.call-update) | async-done | bytes 18874384 | tf_op jit(solution)/shard_map/all_gather | solution.py:147
  418.6 35.4 %fusion.703 = f32[9216,512]{1,0:T(8,128)} fusion(f32[9216,512]{1,0:T(8,128)} %all-gather.3.cloned.1.call-done, f32[512,512]{1,0:T(8,128)S(1)} %copy-done.23), kind=kOutput, calls=%fused_computation.736 | convolution fusion | flops 28991029248 | bytes 38797312 | tf_op jit(solution)/shard_map/dot_general | solution.py:87
  453.9 89.4 %all-gather.5.cloned.1.call-done = f32[9216,512]{1,0:T(8,128)} async-done(((f32[9216,128]{1,0:T(8,128)}), f32[9216,512]{1,0:T(8,128)}) %all-gather.5.cloned.1.call-update) | async-done | bytes 18874384 | tf_op jit(solution)/shard_map/all_gather | solution.py:152
  543.3 77.3 %fusion.699 = (f32[512]{0:T(512)}, f32[9216,512]{1,0:T(8,128)S(1)}, f32[9216,512]{1,0:T(8,128)}) fusion(f32[9216,512]{1,0:T(8,128)} %fusion.703, f32[512]{0:T(512)S(1)} %copy-done.54, f32[9216,512]{1,0:T(8,128)} %all-gather.5.cloned.1.call-done, f32[512,512]{1,0:T(8,128)S(1)} %copy-done), kind=kOutput, calls=%fused_computation.733 | convolution fusion | flops 29335486464 | bytes 76550144 | tf_op jit(solution)/shard_map/dot_general | solution.py:95
  620.6 6.5 copy-done.2
  627.1 33.8 %fusion.704 = f32[9216,512]{1,0:T(8,128)} fusion(f32[9216,512]{1,0:T(8,128)S(1)} %get-tuple-element.41, f32[512,512]{1,0:T(8,128)S(1)} %copy-done.23), kind=kOutput, calls=%fused_computation.737 | convolution fusion | flops 28991029248 | bytes 38797312 | tf_op jit(solution)/shard_map/dot_general | solution.py:95
  660.9 139.6 %reduce-scatter.5.cloned.1.call-done = f32[9216,128]{1,0:T(8,128)} async-done(((f32[9216,512]{1,0:T(8,128)}), f32[9216,128]{1,0:T(8,128)}) %reduce-scatter.5.cloned.1.call-update) | async-done | bytes 4718608 | tf_op jit(solution)/shard_map/reduce_scatter | solution.py:157
  800.5 10.3 multiply_reduce_fusion
  810.9 36.4 %fusion.7 = f32[9216,512]{1,0:T(8,128)} fusion(f32[512,512]{1,0:T(8,128)S(1)} %copy-done, f32[9216,512]{1,0:T(8,128)} %get-tuple-element.42, f32[9216,512]{1,0:T(8,128)} %fusion.703, f32[512]{0:T(512)S(1)} %copy-done.54), kind=kOutput, calls=%fused_computation.22 | convolution fusion | flops 29005185024 | bytes 57673728 | tf_op jit(solution)/shard_map/dot_general | solution.py:87
  847.4 35.3 %fusion.705 = f32[512,512]{1,0:T(8,128)} fusion(f32[9216,512]{1,0:T(8,128)} %all-gather.3.cloned.1.call-done, f32[9216,512]{1,0:T(8,128)} %copy-done.2), kind=kOutput, calls=%fused_computation.738 | convolution fusion | flops 28991029248 | bytes 38797312 | tf_op jit(solution)/shard_map/dot_general | solution.py:91
  882.7 37.2 %fusion.6 = f32[512,512]{1,0:T(8,128)} fusion(f32[9216,512]{1,0:T(8,128)} %all-gather.5.cloned.1.call-done, f32[9216,512]{1,0:T(8,128)} %get-tuple-element.42, f32[9216,512]{1,0:T(8,128)} %fusion.703, f32[512]{0:T(512)S(1)} %copy-done.54), kind=kOutput, calls=%fused_computation.21 | convolution fusion | flops 29005185024 | bytes 57673728 | tf_op jit(solution)/shard_map/dot_general | solution.py:91
  920.7 66.3 %reduce-scatter.3.cloned.1.call-done = f32[9216,128]{1,0:T(8,128)} async-done(((f32[9216,512]{1,0:T(8,128)}), f32[9216,128]{1,0:T(8,128)}) %reduce-scatter.3.cloned.1.call-update) | async-done | bytes 4718608 | tf_op jit(solution)/shard_map/reduce_scatter | solution.py:151
  987.0 13.3 multiply_add_fusion.1
  1000.3 6.6 fusion.203
  1007.0 6.8 fusion.11
  1044.1 8.3 fusion.701
  1052.5 16.5 %fusion.218 = f32[1,2,64,64]{3,2,1,0:T(8,128)} fusion(f32[1,63,63,2,64]{4,2,1,3,0:T(8,128)S(1)} %get-tuple-element.44, f32[2,64]{1,0:T(2,128)S(1)} %copy-done.63, f32[2,63,63,64]{3,2,1,0:T(8,128)S(1)} %copy-done.15), kind=kOutput, calls=%fused_computation.272 | convolution fusion | flops 423190656 | bytes 4097536 | tf_op jit(solution)/shard_map/transpose(jvp(...bc,bcd->...bd))/dot_general | solution.py:18
  1069.0 16.7 %fusion.223 = f32[1,2,64,64]{3,2,1,0:T(8,128)} fusion(f32[1,63,63,2,64]{4,2,1,3,0:T(8,128)S(1)} %get-tuple-element.44, f32[2,64]{1,0:T(2,128)S(1)} %copy-done.61, f32[2,63,63,64]{3,2,1,0:T(8,128)S(1)} %copy-done.18), kind=kOutput, calls=%fused_computation.273 | convolution fusion | flops 423190656 | bytes 4097536 | tf_op jit(solution)/shard_map/transpose(jvp(...bc,bcd->...bd))/dot_general | solution.py:18
  1085.7 16.3 %fusion.234 = f32[1,2,64,64]{3,2,1,0:T(8,128)S(1)} fusion(f32[1,63,63,2,64]{4,2,1,3,0:T(8,128)S(1)} %get-tuple-element.63, f32[2,64]{1,0:T(2,128)S(1)} %copy-done.63, f32[2,63,63,64]{3,2,1,0:T(8,128)S(1)} %copy-done.15), kind=kOutput, calls=%fused_computation.276 | convolution fusion | flops 423698688 | bytes 4097536 | tf_op jit(solution)/shard_map/transpose(jvp(...bc,bcd->...bd))/dot_general | solution.py:18
  1102.0 16.6 %fusion.239 = f32[1,2,64,64]{3,2,1,0:T(8,128)S(1)} fusion(f32[1,63,63,2,64]{4,2,1,3,0:T(8,128)S(1)} %get-tuple-element.63, f32[2,64]{1,0:T(2,128)S(1)} %copy-done.61, f32[2,63,63,64]{3,2,1,0:T(8,128)S(1)} %copy-done.18), kind=kOutput, calls=%fused_computation.277 | convolution fusion | flops 423190656 | bytes 4097536 | tf_op jit(solution)/shard_map/transpose(jvp(...bc,bcd->...bd))/dot_general | solution.py:18
  1127.0 14.2 fusion.29
  1149.4 13.5 fusion.58
  1162.9 10.2 fusion.24
  1214.2 10.4 fusion.51
  1247.9 6.5 fusion.151
  1265.9 9.4 multiply_reduce_fusion.1
  1276.9 22.4 %all-reduce.12 = (f32[128]{0:T(128)}, f32[128]{0:T(128)}, f32[2,2,64]{2,1,0:T(2,128)}, f32[2,2,64]{2,1,0:T(2,128)}, f32[128]{0:T(128)}, /*index=5*/f32[128]{0:T(128)}, f32[512]{0:T(512)}, f32[128]{0:T(128)}) all-reduce(f32[128]{0:T(128)S(1)} %get-tuple-element.14, ...), channel_id=1, replica_groups=mesh['dp'=8,'blk'=4] {'dp'}, use_global_device_ids=true, to_apply=%region_19.20 | all-reduce | flops 1664 | bytes 13312 | tf_op jit(solution)/shard_map/psum | solution.py:172
  1305.8 12.9 add_multiply_fusion
  1318.6 103.2 %all-reduce.20.cloned.1.call-done = (f32[2,2,64,64]{3,2,1,0:T(8,128)}, f32[2,2,64,64]{3,2,1,0:T(8,128)}, f32[512,512]{1,0:T(8,128)}, f32[512,512]{1,0:T(8,128)}) async-done(((f32[2,2,64,64]{3,2,1,0:T(8,128)}, f32[2,2,64,64]{3,2,1,0:T(8,128)}, f32[512,512]{1,0:T(8,128)}, f32[512,512]{1,0:T(8,128)}), (f32[2,2,64,64]{3,2,1,0:T(8,128)}, f32[2,2,64,64]{3,2,1,0:T(8,128)}, f32[512,512]{1,0:T(8,128)}, ...) | async-done | bytes 2228240 | tf_op jit(solution)/shard_map/psum | solution.py:172
  (255 shorter events, 241.4 us)
Async XLA Ops:
  7.2 536.1 %copy-start = (f32[512,512]{1,0:T(8,128)S(1)}, f32[512,512]{1,0:T(8,128)}, u32[]{:S(2)}) copy-start(f32[512,512]{1,0:T(8,128)} %param.30) | copy-start | bytes 3145732
  7.2 411.4 %all-gather.3.cloned.1.call-start = ((), (), s32[]{:S(2)}) async-start(), calls=%async_computation.2 | async-start | bytes 23592960 | tf_op jit(solution)/shard_map/all_gather | solution.py:147
  7.3 235.5 %copy-start.44 = (s32[63]{0:T(128)}, s32[63]{0:T(128)S(1)}, u32[]{:S(2)}) copy-start(s32[63]{0:T(128)S(1)} %iota_add_fusion) | copy-start | bytes 760
  8.7 234.1 %copy-start.41 = (pred[96]{0:T(512)(128)(4,1)}, pred[96]{0:T(512)(128)(4,1)S(1)}, u32[]{:S(2)}) copy-start(pred[96]{0:T(512)(128)(4,1)S(1)} %iota_compare_fusion) | copy-start | bytes 292
  8.7 234.0 %copy-start.47 = (pred[63]{0:T(512)(128)(4,1)}, pred[63]{0:T(512)(128)(4,1)S(1)}, u32[]{:S(2)}) copy-start(pred[63]{0:T(512)(128)(4,1)S(1)} %abs_compare_fusion.1) | copy-start | bytes 193
  9.1 38.3 %copy-start.25 = (f32[9216]{0:T(1024)}, f32[9216]{0:T(1024)S(1)}, u32[]{:S(2)}) copy-start(f32[9216]{0:T(1024)S(1)} %and_convert_fusion) | copy-start | bytes 110596
  9.1 38.3 %copy-start.55 = (f32[128]{0:T(128)S(1)}, f32[128]{0:T(128)}, u32[]{:S(2)}) copy-start(f32[128]{0:T(128)} %param.20) | copy-start | bytes 1540
  9.1 38.3 %copy-start.66 = (f32[128]{0:T(128)S(1)}, f32[128]{0:T(128)}, u32[]{:S(2)}) copy-start(f32[128]{0:T(128)} %param.21) | copy-start | bytes 1540
  29.1 25.5 %copy-start.31 = (f32[9216]{0:T(1024)}, f32[9216]{0:T(1024)S(1)}, u32[]{:S(2)}) copy-start(f32[9216]{0:T(1024)S(1)} %broadcast_multiply_fusion.4) | copy-start | bytes 110596
  76.4 62.9 %copy-start.62 = (f32[2,64]{1,0:T(2,128)}, f32[2,64]{1,0:T(2,128)S(1)}, u32[]{:S(2)}) copy-start(f32[2,64]{1,0:T(2,128)S(1)} %get-tuple-element.53) | copy-start | bytes 1540
  76.4 120.1 %copy-start.60 = (f32[2,64]{1,0:T(2,128)}, f32[2,64]{1,0:T(2,128)S(1)}, u32[]{:S(2)}) copy-start(f32[2,64]{1,0:T(2,128)S(1)} %get-tuple-element.52) | copy-start | bytes 1540
  126.1 13.2 copy-start.14
  139.3 14.2 copy-start.6
  167.0 15.0 %copy-start.16 = (f32[2,63,63,64]{3,2,1,0:T(8,128)}, f32[2,63,63,64]{3,2,1,0:T(8,128)S(1)}, u32[]{:S(2)}) copy-start(f32[2,63,63,64]{3,2,1,0:T(8,128)S(1)} %convolution_subtract_fusion) | copy-start | bytes 6096388
  236.3 15.5 %slice-start = ((s8[4718592]{0:T(1024)(128)(4,1)}), s8[4194304]{0:T(1024)(128)(4,1)S(1)}, s32[]{:S(2)}) async-start(s8[4718592]{0:T(1024)(128)(4,1)} %bitcast.888), calls=%async_computation.9 | async-start | bytes 8388608
  257.1 29.4 %copy-start.58 = (f32[128]{0:T(128)S(1)}, f32[128]{0:T(128)}, u32[]{:S(2)}) copy-start(f32[128]{0:T(128)} %param.26) | copy-start | bytes 1540
  257.1 29.4 %copy-start.74 = (f32[128]{0:T(128)S(1)}, f32[128]{0:T(128)}, u32[]{:S(2)}) copy-start(f32[128]{0:T(128)} %param.27) | copy-start | bytes 1540
  270.7 24.1 %copy-start.34 = (f32[9216]{0:T(1024)}, f32[9216]{0:T(1024)S(1)}, u32[]{:S(2)}) copy-start(f32[9216]{0:T(1024)S(1)} %broadcast_multiply_fusion.3) | copy-start | bytes 110596
  294.8 123.8 %copy-start.23 = (f32[512,512]{1,0:T(8,128)S(1)}, f32[512,512]{1,0:T(8,128)}, u32[]{:S(2)}) copy-start(f32[512,512]{1,0:T(8,128)} %param.28) | copy-start | bytes 3145732
  294.8 248.4 %all-gather.5.cloned.1.call-start = ((), (), s32[]{:S(2)}) async-start(), calls=%async_computation.4 | async-start | bytes 23592960 | tf_op jit(solution)/shard_map/all_gather | solution.py:152
  295.6 247.7 %copy-start.54 = (f32[512]{0:T(512)S(1)}, f32[512]{0:T(512)}, u32[]{:S(2)}) copy-start(f32[512]{0:T(512)} %param.29) | copy-start | bytes 6148
  295.6 504.9 %reduce-scatter.5.cloned.1.call-start = ((), (), s32[]{:S(2)}) async-start(), calls=%async_computation.5 | async-start | bytes 23592960 | tf_op jit(solution)/shard_map/reduce_scatter | solution.py:157
  660.9 139.7 %copy-start.35 = (f32[9216]{0:T(1024)S(1)}, f32[9216]{0:T(1024)}, u32[]{:S(2)}) copy-start(f32[9216]{0:T(1024)} %copy-done.34) | copy-start | bytes 110596
  660.9 139.7 %copy-start.40 = (f32[9216]{0:T(1024)S(1)}, f32[9216]{0:T(1024)}, u32[]{:S(2)}) copy-start(f32[9216]{0:T(1024)} %copy-done.39) | copy-start | bytes 110596
  660.9 139.7 %copy-start.59 = (f32[128]{0:T(128)S(1)}, f32[128]{0:T(128)}, u32[]{:S(2)}) copy-start(f32[128]{0:T(128)} %param.26) | copy-start | bytes 1540
  660.9 259.0 %all-reduce.24.cloned.1.call-start = ((), (), s32[]{:S(2)}) async-start(), calls=%async_computation.8 | async-start | bytes 147456 | tf_op jit(solution)/shard_map/psum | solution.py:109
  810.8 176.1 %reduce-scatter.3.cloned.1.call-start = ((), (), s32[]{:S(2)}) async-start(), calls=%async_computation.3 | async-start | bytes 23592960 | tf_op jit(solution)/shard_map/reduce_scatter | solution.py:151
  847.3 457.7 %all-reduce.22.cloned.1.call-start = ((), (), s32[]{:S(2)}) async-start(), calls=%async_computation.7 | async-start | bytes 147456 | tf_op jit(solution)/shard_map/psum | solution.py:109
  882.7 104.3 %copy-start.27 = (f32[9216]{0:T(1024)S(1)}, f32[9216]{0:T(1024)}, u32[]{:S(2)}) copy-start(f32[9216]{0:T(1024)} %copy-done.25) | copy-start | bytes 110596
  882.7 104.3 %copy-start.75 = (f32[128]{0:T(128)S(1)}, f32[128]{0:T(128)}, u32[]{:S(2)}) copy-start(f32[128]{0:T(128)} %param.31) | copy-start | bytes 1540
  987.0 13.3 copy-start.42
  987.0 13.4 copy-start.45
  987.0 13.4 copy-start.48
  1000.3 13.5 copy-start.3
  1007.0 13.3 copy-start.11
  1052.5 16.5 %copy-start.18 = (f32[2,63,63,64]{3,2,1,0:T(8,128)S(1)}, f32[2,63,63,64]{3,2,1,0:T(8,128)}, u32[]{:S(2)}) copy-start(f32[2,63,63,64]{3,2,1,0:T(8,128)} %copy-done.16) | copy-start | bytes 6096388
  1052.5 16.5 %copy-start.61 = (f32[2,64]{1,0:T(2,128)S(1)}, f32[2,64]{1,0:T(2,128)}, u32[]{:S(2)}) copy-start(f32[2,64]{1,0:T(2,128)} %copy-done.60) | copy-start | bytes 1540
  1102.0 16.6 %copy-start.51 = (f32[2,2,64,64]{3,2,1,0:T(8,128)S(1)}, f32[2,2,64,64]{3,2,1,0:T(8,128)}, u32[]{:S(2)}) copy-start(f32[2,2,64,64]{3,2,1,0:T(8,128)} %param.24) | copy-start | bytes 196612
  1127.0 14.2 copy-start.5
  1141.3 49.1 %copy-start.8 = (f32[2,64,1,63,63]{1,4,3,0,2:T(8,128)}, f32[2,64,1,63,63]{1,4,3,0,2:T(8,128)S(1)}, u32[]{:S(2)}) copy-start(f32[2,64,1,63,63]{1,4,3,0,2:T(8,128)S(1)} %get-tuple-element.58) | copy-start | bytes 6096388
  1214.2 10.4 copy-start.20
  1247.9 15.7 %slice-start.4 = ((s8[4718592]{0:T(1024)(128)(4,1)}), s8[4194304]{0:T(1024)(128)(4,1)S(1)}, s32[]{:S(2)}) async-start(s8[4718592]{0:T(1024)(128)(4,1)} %bitcast.894), calls=%async_computation.13 | async-start | bytes 8388608
  1265.8 11.0 copy-start.68
  1265.9 11.0 copy-start.69
  1265.9 11.0 copy-start.70
  1265.9 11.0 copy-start.71
  1275.4 146.5 %all-reduce.20.cloned.1.call-start = ((), (), s32[]{:S(2)}) async-start(), calls=%async_computation.6 | async-start | bytes 4718592 | tf_op jit(solution)/shard_map/psum | solution.py:172
  1305.7 123.8 %copy-start.1 = (f32[512,512]{1,0:T(8,128)S(1)}, f32[512,512]{1,0:T(8,128)}, u32[]{:S(2)}) copy-start(f32[512,512]{1,0:T(8,128)} %param.30) | copy-start | bytes 3145732
  (41 other events, 241.5 us)
Sparse Core Ops, SparseCore 0:
  295.0 123.5 all-gather.2
  420.7 122.5 all-gather.4
  661.0 139.4 reduce-scatter.4
  810.9 29.4 all-reduce.23
  847.4 139.4 reduce-scatter.2
  1275.5 29.4 all-reduce.21
  1310.0 111.7 all-reduce.19
where the time goes:
time: 1440 us
  matrix products  605 us (42%)
  waiting for transfers between devices  528 us (37%)
  other arithmetic  123 us (9%)
  local copies, waits for them, and re-layouts  95.4 us (7%)
  blocking collectives  67.1 us (5%)
  between operations  17.2 us (1%)
    dot_general x48, matrix products, contract(): return jnp.einsum(form, left, right, precision=lax.Precision.HIGHEST)  350 us
    reduce_scatter x1, waiting for transfers between devices, per_device(): lax.psum_scatter(dot_trailing(grad_pre, mlp_w1), 'blk', scatter_dimension...  140 us
    all_gather x1, waiting for transfers between devices, per_device(): second_full = lax.all_gather(second, 'blk', axis=1, tiled=True)  123 us
    dot_general x2, matrix products, dot_trailing(): lax.dot_general(left, right, (((1,), (1,)), ((), ())), precision=lax.Prec...  111 us
    psum x1, waiting for transfers between devices, per_device(): lax.psum((grad_gain_one, grad_shift_one, grad_first_w, grad_first_b, grad...  103 us
    all_gather x1, waiting for transfers between devices, per_device(): grad_full = lax.all_gather(grad_out, 'blk', axis=1, tiled=True)  89.4 us
    dot_general x2, matrix products, dot_leading(): lax.dot_general(left, right, (((0,), (0,)), ((), ())), precision=lax.Prec...  72.6 us
    dot_general x2, matrix products, dot_rows(): return jnp.dot(left, right, precision=lax.Precision.HIGHEST)  71.8 us
  transfers between devices with their start and end apart: 7, of which 6 were waited for; matrix products, arithmetic and copies ran while one was open for 11% of the time, Pallas kernels for 0%

commit v1 on v0

v1 whole, which is shorter than its diff:
```python
import functools
import math

import jax
import jax.numpy as jnp
from jax import lax
from jax.experimental import pallas as pl
from jax.experimental.pallas import tpu as pltpu
from jax.sharding import PartitionSpec as P

C = 512
MODES = 32
SMAX = 96
LANES = 128
FREQ = 64
PARTS = 4
CHUNKS = 3
SLABS = SMAX // (PARTS * CHUNKS)
PIECE = SLABS * SMAX
GROUP = PARTS * SLABS
STEPS = SMAX // SLABS
TILE = 256
HID = 512

EPS = 1e-05
SHRINK = 0.01
F32 = jnp.float32
BF16 = jnp.bfloat16
NN = (((1,), (0,)), ((), ()))
NT = (((1,), (1,)), ((), ()))
TN = (((0,), (0,)), ((), ()))
LIMIT = 56 * 1024 * 1024


def mm(left, right, dims=NN):
    return lax.dot_general(left, right, dims, preferred_element_type=F32)


def split2(value):
    high = value.astype(BF16)
    return high, (value - high.astype(F32)).astype(BF16)


def split3(value):
    high = value.astype(BF16)
    rest = value - high.astype(F32)
    mid = rest.astype(BF16)
    return high, mid, (rest - mid.astype(F32)).astype(BF16)


def left6(value):
    one, two, three = split3(value)
    return jnp.concatenate([one, one, two, one, two, three], axis=1)


def right6(value):
    one, two, three = split3(value)
    return jnp.concatenate([one, two, one, three, two, one], axis=0)


def left3(value):
    one, two = split2(value)
    return jnp.concatenate([one, one, two], axis=1)


def right3(value):
    one, two = split2(value)
    return jnp.concatenate([one, two, one], axis=0)


def phi_pair(value):
    cdf = 0.5 + 0.5 * lax.erf(value * math.sqrt(0.5))
    pdf = jnp.exp(value * value * -0.5) * (1.0 / math.sqrt(2.0 * math.pi))
    return cdf, pdf


def pad_rows(value):
    return jnp.concatenate([value, jnp.zeros((LANES - SMAX, value.shape[1]), F32)], axis=0)


def fold_rows(value):
    return jnp.sum(value.reshape(-1, 8, value.shape[-1]), axis=0)


def spread(row):
    return jnp.broadcast_to(row, (LANES, LANES)).T[:SMAX]


def call(body, out_shape, in_specs, out_specs, grid=(), scratch=(), aliases=None, cost=None):
    flops, moved = cost or (0, 0)
    return pl.pallas_call(
        body,
        out_shape=out_shape,
        grid=grid,
        in_specs=in_specs,
        out_specs=out_specs,
        scratch_shapes=list(scratch),
        input_output_aliases=aliases or {},
        compiler_params=pltpu.CompilerParams(vmem_limit_bytes=LIMIT),
        cost_estimate=pl.CostEstimate(flops=flops, bytes_accessed=moved, transcendentals=0),
    )


SMEM = pl.BlockSpec(memory_space=pltpu.SMEM)
VMEM = pl.BlockSpec(memory_space=pltpu.VMEM)
ANY = pl.BlockSpec(memory_space=pl.ANY)


def whole(shape):
    zeros = (0,) * len(shape)
    return pl.BlockSpec(shape, lambda *_: zeros)


def sds(shape, dtype=F32):
    return jax.ShapeDtypeStruct(shape, dtype)


def table(item_sides, item_modes):
    row = lax.broadcasted_iota(jnp.int32, (LANES, LANES), 0)
    cell = lax.broadcasted_iota(jnp.int32, (LANES, LANES), 1)
    index = row % FREQ
    frequency = index - (MODES - 1)
    extent = item_sides[0]
    phase = frequency * cell % extent
    keep = (jnp.abs(frequency) < item_modes[0]) & (cell < extent) & (index < 2 * MODES - 1)
    length = extent.astype(F32)
    angle = 2.0 * math.pi * phase.astype(F32) / length
    wave = jnp.where(row < FREQ, jnp.cos(angle), -jnp.sin(angle)) * lax.rsqrt(length)
    return jnp.where(keep, wave, jnp.zeros_like(wave))


def big_weight(weight, out):
    out[...] = jnp.zeros_like(out)
    for block in range(2):
        rows = pl.ds(block * 64, 64)
        later = pl.ds(128 + block * 64, 64)
        out[rows, rows] = weight[0, block]
        out[rows, later] = weight[1, block]
        out[later, rows] = -weight[1, block]
        out[later, later] = weight[0, block]


def prepare_body(f_ref, w1_ref, w2_ref, f6, g6, ft3, gt3, w1c, w2c, w1t, w2t, big):
    forward = f_ref[...]
    turned = jnp.concatenate([-forward[FREQ:], forward[:FREQ]], axis=0)
    f6[...] = left6(forward)
    g6[...] = left6(jnp.concatenate([forward, turned], axis=1))
    back = forward.T
    ft3[...] = left3(back)
    gt3[...] = left3(jnp.concatenate([back, turned.T], axis=0))
    for source, straight, across in ((w1_ref, w1c, w1t), (w2_ref, w2c, w2t)):
        big_weight(source, big)
        straight[...] = right6(big[...])
        across[...] = right3(big[...].T)


def prepare(forward, spec_w1, spec_w2):
    shapes = [
        sds((128, 768), BF16),
        sds((128, 1536), BF16),
        sds((128, 384), BF16),
        sds((256, 384), BF16),
        sds((1536, 256), BF16),
        sds((1536, 256), BF16),
        sds((768, 256), BF16),
        sds((768, 256), BF16),
    ]
    return call(
        prepare_body,
        shapes,
        [VMEM] * 3,
        [VMEM] * 8,
        scratch=[pltpu.VMEM((256, 256), F32)],
        cost=(10**6, 3 * 10**6),
    )(forward, spec_w1, spec_w2)


def slab_mask(first, side):
    cell = lax.broadcasted_iota(jnp.int32, (SMAX, LANES), 0)
    return (cell < side) & (first < side)


def moments_body(side_ref, x_ref, out_ref):
    step = pl.program_id(0)
    side = side_ref[0]
    for slab in range(SLABS):
        inside = slab_mask(step * SLABS + slab, side)
        value = pad_rows(jnp.where(inside, x_ref[slab], 0.0)).T
        mean = jnp.sum(value, axis=0, keepdims=True) * (1.0 / LANES)
        centered = value - mean
        out_ref[0, pl.ds(slab, 1), :] = mean
        out_ref[1, pl.ds(slab, 1), :] = jnp.sum(centered * centered, axis=0, keepdims=True)


def moments(side, x):
    return call(
        moments_body,
        sds((2, SMAX, LANES)),
        [SMEM, pl.BlockSpec((SLABS, SMAX, LANES), lambda i: (i, 0, 0))],
        pl.BlockSpec((2, SLABS, LANES), lambda i: (0, i, 0)),
        grid=(STEPS,),
        cost=(10**7, 5 * 10**6),
    )(side, x)


def cotangent_body(side_ref, own_ref, g_ref, *outs):
    side = side_ref[0]
    own = own_ref[0]
    total = outs[PARTS]
    total[...] = jnp.zeros_like(total)
    for chunk in range(CHUNKS):
        for part in range(PARTS):

            def one(slab, carry, chunk=chunk, part=part):
                first = chunk * GROUP + (own ^ part) * SLABS + slab
                value = jnp.where(slab_mask(first, side), g_ref[first], 0.0)
                outs[part][chunk, slab] = value
                return carry + fold_rows(value)

            total[...] += lax.fori_loop(0, SLABS, one, jnp.zeros((8, LANES), F32))


def cotangent_pieces(side, own, g):
    shapes = [sds((CHUNKS, SLABS, SMAX, LANES))] * PARTS + [sds((8, LANES))]
    return call(
        cotangent_body,
        shapes,
        [SMEM, SMEM, VMEM],
        [VMEM] * 5,
        cost=(10**7, 10**7),
    )(side, own, g)


def row_stats(stats):
    means = [stats[part, 0] for part in range(PARTS)]
    mean = (means[0] + means[1] + means[2] + means[3]) * (1.0 / PARTS)
    total = stats[0, 1] + stats[1, 1] + stats[2, 1] + stats[3, 1]
    for part in range(PARTS):
        gap = means[part] - mean
        total = total + LANES * (gap * gap)
    spread_ = total * (1.0 / C) + EPS
    inverse = lax.rsqrt(spread_)
    inverse = inverse * (1.5 - 0.5 * spread_ * inverse * inverse)
    return mean, inverse


def first_body(side_ref, x_ref, stats_ref, gain_ref, bias_ref, f6_ref, b_ref, xn_ref, xhat_ref, r_ref):
    step = pl.program_id(0)
    side = side_ref[0]
    mean, inverse = row_stats(stats_ref)
    r_ref[...] = inverse
    gain, bias = gain_ref[...], bias_ref[...]
    for pair in range(SLABS // 2):
        columns = []
        for slab in (2 * pair, 2 * pair + 1):
            value = jnp.where(slab_mask(step * SLABS + slab, side), x_ref[slab], 0.0)
            centered = value - spread(mean[slab : slab + 1])
            normal = centered * spread(inverse[slab : slab + 1])
            normed = normal * gain + bias
            xhat_ref[slab] = normal
            xn_ref[slab] = value + normed
            columns.append(pad_rows(normed))
        out = mm(f6_ref[...], right6(jnp.concatenate(columns, axis=1)))
        b_ref[2 * pair] = out[:, :LANES]
        b_ref[2 * pair + 1] = out[:, LANES:]


def first_stage(side, x, stats, gain, bias, f6):
    field = pl.BlockSpec((SLABS, SMAX, LANES), lambda i: (i, 0, 0))
    return call(
        first_body,
        [sds((SMAX, LANES, LANES)), sds((SMAX, SMAX, LANES)), sds((SMAX, SMAX, LANES)), sds((SMAX, LANES))],
        [
            SMEM,
            field,
            pl.BlockSpec((PARTS, 2, SLABS, LANES), lambda i: (0, 0, i, 0)),
            whole((1, LANES)),
            whole((1, LANES)),
            whole((128, 768)),
        ],
        [
            pl.BlockSpec((SLABS, LANES, LANES), lambda i: (i, 0, 0)),
            field,
            field,
            pl.BlockSpec((SLABS, LANES), lambda i: (i, 0)),
        ],
        grid=(STEPS,),
        cost=(2 * 10**9, 2 * 10**7),
    )(side, x, stats, gain, bias, f6)


def gather_columns(re_ref, im_ref, first):
    zeros = jnp.zeros((LANES - SMAX, LANES), F32)
    columns = []
    for j in range(first, first + 4):
        columns.append(jnp.concatenate([re_ref[:, j, :], zeros, im_ref[:, j, :], zeros], axis=0))
    return jnp.concatenate(columns, axis=1)


def to_rows(out):
    rows = []
    for j in range(4):
        lanes = slice(j * LANES, (j + 1) * LANES)
        rows.append(jnp.concatenate([out[:FREQ, lanes], out[FREQ:, lanes]], axis=1))
    return jnp.concatenate(rows, axis=0)


def to_columns(rows):
    columns = []
    for j in range(4):
        part = rows[j * FREQ : (j + 1) * FREQ]
        columns.append(jnp.concatenate([part[:, :LANES], part[:, LANES:]], axis=0))
    return jnp.concatenate(columns, axis=1)


def scatter_columns(re_ref, im_ref, first, out):
    for j in range(4):
        lanes = slice(j * LANES, (j + 1) * LANES)
        re_ref[:, first + j, :] = out[:SMAX, lanes]
        im_ref[:, first + j, :] = out[LANES : LANES + SMAX, lanes]


def shrink(value):
    return jnp.where(
        value > SHRINK,
        value - SHRINK,
        jnp.where(value < -SHRINK, value + SHRINK, jnp.zeros_like(value)),
    )


def mix_body(re_ref, im_ref, g6_ref, w1_ref, b1_ref, w2_ref, b2_ref, gt3_ref, bre, bim, a_out, p_out, o_out):
    for half in range(2):
        rows = pl.ds(half * TILE, TILE)
        spectrum = to_rows(mm(g6_ref[...], right6(gather_columns(re_ref, im_ref, 4 * half))))
        a_out[rows, :] = spectrum
        pre = mm(left6(spectrum), w1_ref[...]) + b1_ref[...]
        p_out[rows, :] = pre
        cdf = 0.5 + 0.5 * lax.erf(pre * math.sqrt(0.5))
        out = mm(left6(pre * cdf), w2_ref[...]) + b2_ref[...]
        o_out[rows, :] = out
        scatter_columns(bre, bim, 4 * half, mm(gt3_ref[...], right3(to_columns(shrink(out)))))


def mix_forward(b, g6, w1c, bias1, w2c, bias2, gt3):
    re = pl.BlockSpec((SMAX, 8, LANES), lambda j: (0, j, 0))
    im = pl.BlockSpec((SMAX, 8, LANES), lambda j: (0, 8 + j, 0))
    out = pl.BlockSpec((SMAX, 8, LANES), lambda j: (0, j, 0))
    rows = pl.BlockSpec((512, 256), lambda j: (j, 0))
    half = sds((SMAX, FREQ, LANES))
    return call(
        mix_body,
        [half, half] + [sds((4096, 256))] * 3,
        [
            re,
            im,
            whole((128, 1536)),
            whole((1536, 256)),
            whole((1, 256)),
            whole((1536, 256)),
            whole((1, 256)),
            whole((256, 384)),
        ],
        [out, out, rows, rows, rows],
        grid=(8,),
        cost=(10**10, 3 * 10**7),
    )(b, b, g6, w1c, bias1, w2c, bias2, gt3)


def last_body(own_ref, re_ref, im_ref, xn_ref, ft3_ref, *outs):
    own = own_ref[0]
    for part in range(PARTS):
        base = (own ^ part) * SLABS
        for pair in range(SLABS // 2):
            slabs = (base + 2 * pair, base + 2 * pair + 1)
            columns = [jnp.concatenate([re_ref[s], im_ref[s]], axis=0) for s in slabs]
            out = mm(ft3_ref[...], right3(jnp.concatenate(columns, axis=1)))[:SMAX]
            for index, s in enumerate(slabs):
                outs[part][2 * pair + index] = xn_ref[s] + out[:, index * LANES : (index + 1) * LANES]


def last_stage(own, bre, bim, xn, ft3, chunk):
    half = pl.BlockSpec((GROUP, FREQ, LANES), lambda i: (chunk, 0, 0))
    return call(
        last_body,
        [sds((SLABS, SMAX, LANES))] * PARTS,
        [SMEM, half, half, pl.BlockSpec((GROUP, SMAX, LANES), lambda i: (chunk, 0, 0)), whole((128, 384))],
        [whole((SLABS, SMAX, LANES))] * PARTS,
        grid=(1,),
        cost=(10**9, 5 * 10**6),
    )(own, bre, bim, xn, ft3)


def weights_body(w1_ref, w2_ref, w1h, w1l, w2h, w2l):
    w1h[...], w1l[...] = split2(w1_ref[...])
    w2h[...], w2l[...] = split2(w2_ref[...])


def split_weights(w1, w2):
    block = pl.BlockSpec((1, 512, 512), lambda i: (i, 0, 0))
    return call(
        weights_body,
        [sds((4, 512, 512), BF16)] * 4,
        [block] * 2,
        [block] * 4,
        grid=(4,),
        cost=(10**7, 16 * 10**6),
    )(w1, w2)


def feed_body(*refs):
    own_ref = refs[0]
    x_refs, g_refs = refs[1:5], refs[5:9]
    w1h, w1l, w2h, w2l, b1_ref, gain_ref, bias_ref = refs[9:16]
    refs = refs[16 + (len(refs) - 16 - 26) :]
    dx_refs, out_refs = refs[0:4], refs[4:8]
    hh, hl, ph, plo, nh, nl, gh, gl, db1, small = refs[8:18]
    n_h, n_l, g_h, g_l, xhat, scale, dn, acc = refs[18:26]
    step = pl.program_id(0)
    own = own_ref[0]
    last = pl.num_programs(0) - 1

    def lanes(part):
        return pl.ds(pl.multiple_of((own ^ part) * LANES, LANES), LANES)

    @pl.when(step == 0)
    def _():
        for part in range(PARTS):
            acc[:, lanes(part)] = g_refs[part][...]
            dn[:, lanes(part)] = x_refs[part][...]

        def norm(tile, carry):
            rows = pl.ds(tile * TILE, TILE)
            grad = acc[rows, :]
            high, low = split2(grad)
            g_h[rows, :] = high
            g_l[rows, :] = low
            gh[rows, :] = high
            gl[rows, :] = low
            value = dn[rows, :]
            centered = value - jnp.mean(value, axis=1, keepdims=True)
            spread_ = jnp.mean(centered * centered, axis=1, keepdims=True) + EPS
            inverse = lax.rsqrt(spread_)
            inverse = inverse * (1.5 - 0.5 * spread_ * inverse * inverse)
            normal = centered * inverse
            xhat[rows, :] = normal
            scale[rows, :] = jnp.broadcast_to(inverse, (TILE, LANES))
            high, low = split2(normal * gain_ref[...] + bias_ref[...])
            n_h[rows, :] = high
            n_l[rows, :] = low
            nh[rows, :] = high
            nl[rows, :] = low
            dn[rows, :] = jnp.zeros((TILE, C), F32)
            acc[rows, :] = jnp.zeros((TILE, C), F32)
            return carry

        lax.fori_loop(0, PIECE // TILE, norm, 0)

    def tile_step(tile, carry):
        rows = pl.ds(tile * TILE, TILE)
        a_h, a_l = n_h[rows, :], n_l[rows, :]
        pre = mm(a_h, w1h[0]) + mm(a_l, w1h[0]) + mm(a_h, w1l[0]) + b1_ref[0]
        c_h, c_l = g_h[rows, :], g_l[rows, :]
        dh = mm(c_h, w2h[0], NT) + mm(c_l, w2h[0], NT) + mm(c_h, w2l[0], NT)
        cdf, pdf = phi_pair(pre)
        high, low = split2(pre * cdf)
        hh[rows, :] = high
        hl[rows, :] = low
        acc[rows, :] += mm(high, w2h[0]) + mm(low, w2h[0]) + mm(high, w2l[0])
        grad = dh * (cdf + pre * pdf)
        high, low = split2(grad)
        ph[rows, :] = high
        plo[rows, :] = low
        dn[rows, :] += mm(high, w1h[0], NT) + mm(low, w1h[0], NT) + mm(high, w1l[0], NT)
        return carry + fold_rows(grad)

    db1[0] = lax.fori_loop(0, PIECE // TILE, tile_step, jnp.zeros((8, HID), F32))

    @pl.when(step == last)
    def _():
        small[...] = jnp.zeros_like(small)

        def back(tile, carry):
            rows = pl.ds(tile * TILE, TILE)
            grad = dn[rows, :]
            normal = xhat[rows, :]
            scaled = grad * gain_ref[...]
            first = jnp.mean(scaled, axis=1, keepdims=True)
            second = jnp.mean(scaled * normal, axis=1, keepdims=True)
            inverse = jnp.concatenate([scale[rows, :]] * 4, axis=1)
            top = g_h[rows, :].astype(F32) + g_l[rows, :].astype(F32)
            dn[rows, :] = inverse * (scaled - first - normal * second)
            small[0] += fold_rows(grad * normal)
            small[1] += fold_rows(grad)
            return carry

        lax.fori_loop(0, PIECE // TILE, back, 0)
        for part in range(PARTS):
            dx_refs[part][...] = g_refs[part][...] + dn[:, lanes(part)]
            out_refs[part][...] = acc[:, lanes(part)]


def feed(own, xs, gs, weights, b1, gain, bias, keep, chunk):
    piece = whole((PIECE, LANES))
    gpiece = pl.BlockSpec((PIECE, LANES), lambda i: (chunk, 0))
    weight = pl.BlockSpec((1, 512, 512), lambda i: (i, 0, 0))
    wide = pl.BlockSpec((PIECE, HID), lambda i: (chunk, i))
    narrow = pl.BlockSpec((PIECE, C), lambda i: (chunk, 0))
    rows = PIECE * CHUNKS
    shapes = [sds((PIECE, LANES))] * 8
    shapes += [sds((rows, 2048), BF16)] * 4 + [sds((rows, C), BF16)] * 4
    shapes += [sds((4, 8, HID)), sds((2, 8, C))]
    args = [own, *xs, *gs, *weights, b1, gain, bias]
    in_specs = [SMEM] + [piece] * 4 + [gpiece] * 4 + [weight] * 4
    in_specs += [pl.BlockSpec((1, 1, HID), lambda i: (i, 0, 0)), whole((1, C)), whole((1, C))]
    aliases = {}
    if keep is not None:
        for index, array in enumerate(keep):
            aliases[len(args)] = 8 + index
            args.append(array)
            in_specs.append(ANY)
    big = pltpu.VMEM((PIECE, C), F32)
    small = pltpu.VMEM((PIECE, C), BF16)
    return call(
        feed_body,
        shapes,
        in_specs,
        [piece] * 8
        + [wide] * 4
        + [narrow] * 4
        + [pl.BlockSpec((1, 8, HID), lambda i: (i, 0, 0)), whole((2, 8, C))],
        grid=(4,),
        scratch=[small] * 4 + [big, pltpu.VMEM((PIECE, LANES), F32), big, big],
        aliases=aliases,
        cost=(4 * 2 * 3 * PIECE * 512 * 2048, 40 * 10**6),
    )(*args)


def weight_body(hh, hl, ph, plo, nh, nl, gh, gl, *refs):
    b1s, smalls = refs[:CHUNKS], refs[CHUNKS : 2 * CHUNKS]
    out, n_h, n_l, g_h, g_l = refs[2 * CHUNKS :]
    step = pl.program_id(0)

    @pl.when(step == 0)
    def _():
        n_h[...] = nh[...].T
        n_l[...] = nl[...].T
        g_h[...] = gh[...].T
        g_l[...] = gl[...].T

    out[0, :C] = mm(n_h[...], ph[...]) + mm(n_l[...], ph[...]) + mm(n_h[...], plo[...])
    out[0, C : 2 * C] = mm(g_h[...], hh[...]) + mm(g_l[...], hh[...]) + mm(g_h[...], hl[...])
    first = b1s[0][0]
    norms = smalls[0][...]
    for chunk in range(1, CHUNKS):
        first = first + b1s[chunk][0]
        norms = norms + smalls[chunk][...]
    out[0, 2 * C : 2 * C + 8] = first
    tail = jnp.concatenate([norms[0], norms[1], jnp.zeros((8, 2 * LANES), F32)], axis=1)
    out[0, 2 * C + 8 :] = tail


def weight_grads(keep, b1s, smalls):
    rows = PIECE * CHUNKS
    wide = pl.BlockSpec((rows, HID), lambda i: (0, i))
    narrow = pl.BlockSpec((rows, C), lambda i: (0, 0), pipeline_mode=pl.Buffered(1))
    turned = pltpu.VMEM((C, rows), BF16)
    return call(
        weight_body,
        sds((4, 2 * C + 16, HID)),
        [wide] * 4
        + [narrow] * 4
        + [pl.BlockSpec((1, 8, HID), lambda i: (i, 0, 0))] * CHUNKS
        + [pl.BlockSpec((2, 8, LANES), lambda i: (0, 0, i))] * CHUNKS,
        pl.BlockSpec((1, 2 * C + 16, HID), lambda i: (i, 0, 0)),
        grid=(4,),
        scratch=[turned] * 4,
        cost=(2 * 2 * 3 * rows * 512 * 2048, 60 * 10**6),
    )(*keep, *b1s, *smalls)


def first_back_body(*refs):
    own_ref, pieces, f6_ref = refs[0], refs[1:5], refs[5]
    d_ref, dx_ref = refs[-2:]
    own = own_ref[0]
    table3 = f6_ref[...]
    for part in range(PARTS):
        base = (own ^ part) * SLABS
        for pair in range(SLABS // 2):
            slabs = (2 * pair, 2 * pair + 1)
            values = [pieces[part][s] for s in slabs]
            columns = jnp.concatenate([pad_rows(v) for v in values], axis=1)
            out = mm(table3, right3(columns))
            for index, s in enumerate(slabs):
                d_ref[base + s] = out[:, index * LANES : (index + 1) * LANES]
                dx_ref[base + s] = values[index]


def first_back(own, pieces, f6, keep, chunk):
    args = [own, *pieces, f6]
    in_specs = [SMEM] + [whole((SLABS, SMAX, LANES))] * 4 + [whole((128, 384))]
    aliases = {}
    if keep is not None:
        for index, array in enumerate(keep):
            aliases[len(args)] = index
            args.append(array)
            in_specs.append(ANY)
    return call(
        first_back_body,
        [sds((SMAX, LANES, LANES)), sds((SMAX, SMAX, LANES))],
        in_specs,
        [
            pl.BlockSpec((GROUP, LANES, LANES), lambda i: (chunk, 0, 0)),
            pl.BlockSpec((GROUP, SMAX, LANES), lambda i: (chunk, 0, 0)),
        ],
        grid=(1,),
        aliases=aliases,
        cost=(10**9, 5 * 10**6),
    )(*args)


def rows3(value):
    one, two = split2(value)
    return jnp.concatenate([one, one, two], axis=0)


def mix_back_body(re_ref, im_ref, a_ref, p_ref, o_ref, g3_ref, w1t, w2t, gt3_ref, dre, dim, dw1, dw2, db1, db2):
    @pl.when(pl.program_id(0) == 0)
    def _():
        for ref in (dw1, dw2, db1, db2):
            ref[...] = jnp.zeros_like(ref)

    for half in range(2):
        rows = pl.ds(half * TILE, TILE)
        dz = to_rows(mm(g3_ref[...], right3(gather_columns(re_ref, im_ref, 4 * half))))
        do = jnp.where(jnp.abs(o_ref[rows, :]) > SHRINK, dz, 0.0)
        pre = p_ref[rows, :]
        cdf, pdf = phi_pair(pre)
        dw2[...] += mm(rows3(pre * cdf), right3(do), TN)
        db2[...] += fold_rows(do)
        dp = mm(left3(do), w2t[...]) * (cdf + pre * pdf)
        dw1[...] += mm(rows3(a_ref[rows, :]), right3(dp), TN)
        db1[...] += fold_rows(dp)
        dx = mm(left3(dp), w1t[...])
        scatter_columns(dre, dim, 4 * half, mm(gt3_ref[...], right3(to_columns(dx))))


def mix_backward(d, a, p, o, g6, w1t, w2t, gt3):
    re = pl.BlockSpec((SMAX, 8, LANES), lambda j: (0, j, 0))
    im = pl.BlockSpec((SMAX, 8, LANES), lambda j: (0, 8 + j, 0))
    out = pl.BlockSpec((SMAX, 8, LANES), lambda j: (0, j, 0))
    rows = pl.BlockSpec((512, 256), lambda j: (j, 0))
    half = sds((SMAX, FREQ, LANES))
    return call(
        mix_back_body,
        [half, half, sds((256, 256)), sds((256, 256)), sds((8, 256)), sds((8, 256))],
        [
            re,
            im,
            rows,
            rows,
            rows,
            whole((128, 768)),
            whole((768, 256)),
            whole((768, 256)),
            whole((256, 384)),
        ],
        [out, out, whole((256, 256)), whole((256, 256)), whole((8, 256)), whole((8, 256))],
        grid=(8,),
        cost=(10**10, 3 * 10**7),
    )(d, d, a, p, o, g6, w1t, w2t, gt3)


def last_back_body(re_ref, im_ref, dx_ref, xhat_ref, gain_ref, ft3_ref, dn_ref, sums_ref, small):
    @pl.when(pl.program_id(0) == 0)
    def _():
        small[...] = jnp.zeros_like(small)

    gain = gain_ref[...]
    for pair in range(SLABS // 2):
        slabs = (2 * pair, 2 * pair + 1)
        columns = [jnp.concatenate([re_ref[s], im_ref[s]], axis=0) for s in slabs]
        out = mm(ft3_ref[...], right3(jnp.concatenate(columns, axis=1)))[:SMAX]
        for index, s in enumerate(slabs):
            grad = dx_ref[s] + out[:, index * LANES : (index + 1) * LANES]
            dn_ref[s] = grad
            normal = xhat_ref[s]
            product = grad * normal
            small[0] += fold_rows(product)
            small[1] += fold_rows(grad)
            sums_ref[0, pl.ds(s, 1), :] = jnp.sum(pad_rows(grad * gain).T, axis=0, keepdims=True)
            sums_ref[1, pl.ds(s, 1), :] = jnp.sum(pad_rows(product * gain).T, axis=0, keepdims=True)


def last_back(dre, dim, dx, xhat, gain, ft3):
    half = pl.BlockSpec((SLABS, FREQ, LANES), lambda i: (i, 0, 0))
    field = pl.BlockSpec((SLABS, SMAX, LANES), lambda i: (i, 0, 0))
    return call(
        last_back_body,
        [sds((SMAX, SMAX, LANES)), sds((2, SMAX, LANES)), sds((2, 8, LANES))],
        [half, half, field, field, whole((1, LANES)), whole((128, 384))],
        [field, pl.BlockSpec((2, SLABS, LANES), lambda i: (0, i, 0)), whole((2, 8, LANES))],
        grid=(STEPS,),
        cost=(2 * 10**9, 2 * 10**7),
    )(dre, dim, dx, xhat, gain, ft3)


def final_body(side_ref, dx_ref, dn_ref, xhat_ref, sums_ref, r_ref, gain_ref, out_ref):
    step = pl.program_id(0)
    side = side_ref[0]
    total = sums_ref[0] + sums_ref[1] + sums_ref[2] + sums_ref[3]
    inverse = r_ref[...]
    first = total[0] * (inverse * (1.0 / C))
    second = total[1] * (inverse * (1.0 / C))
    for slab in range(SLABS):
        row = slice(slab, slab + 1)
        normal = xhat_ref[slab]
        scaled = dn_ref[slab] * gain_ref[...]
        back = spread(inverse[row]) * scaled - spread(first[row]) - normal * spread(second[row])
        value = dx_ref[slab] + back
        out_ref[slab] = jnp.where(slab_mask(step * SLABS + slab, side), value, 0.0)


def final_stage(side, dx, dn, xhat, sums, r, gain):
    field = pl.BlockSpec((SLABS, SMAX, LANES), lambda i: (i, 0, 0))
    return call(
        final_body,
        sds((SMAX, SMAX, LANES)),
        [
            SMEM,
            field,
            field,
            field,
            pl.BlockSpec((PARTS, 2, SLABS, LANES), lambda i: (0, 0, i, 0)),
            pl.BlockSpec((SLABS, LANES), lambda i: (i, 0)),
            whole((1, LANES)),
        ],
        field,
        grid=(STEPS,),
        cost=(10**8, 2 * 10**7),
    )(side, dx, dn, xhat, sums, r, gain)


def make_output_body(chunk):
    def body(*refs):
        side_ref, own_ref = refs[:2]
        xs, outs, b2_ref, result = refs[2:6], refs[6:10], refs[10], refs[-1]
        side, own = side_ref[0], own_ref[0]
        for part in range(PARTS):
            base = (own ^ part) * SLABS
            for slab in range(SLABS):
                value = xs[part][slab] + outs[part][slab] + b2_ref[...]
                inside = slab_mask(chunk * GROUP + base + slab, side)
                result[base + slab] = jnp.where(inside, value, 0.0)

    return body


def output_stage(side, own, xs, outs, b2, keep, chunk):
    args = [side, own, *xs, *outs, b2]
    piece = whole((SLABS, SMAX, LANES))
    in_specs = [SMEM, SMEM] + [piece] * 8 + [whole((1, LANES))]
    aliases = {}
    if keep is not None:
        aliases[len(args)] = 0
        args.append(keep)
        in_specs.append(ANY)
    return call(
        make_output_body(chunk),
        sds((SMAX, SMAX, LANES)),
        in_specs,
        pl.BlockSpec((GROUP, SMAX, LANES), lambda i: (chunk, 0, 0)),
        grid=(1,),
        aliases=aliases,
        cost=(10**7, 6 * 10**6),
    )(*args)


def swap(value, axis, size, distance):
    return lax.ppermute(value, axis, [(i, i ^ distance) for i in range(size)])


def exchange(pieces):
    return [pieces[0]] + [swap(pieces[part], "blk", PARTS, part) for part in range(1, PARTS)]


def doubling_sum(value, size):
    distance = 1
    while distance < size:
        value = value + swap(value, "dp", size, distance)
        distance *= 2
    return value


def per_device(
    dp_size,
    block_input,
    cotangent,
    item_sides,
    item_modes,
    ln1_gain,
    ln1_bias,
    spec_w1,
    spec_b1,
    spec_w2,
    spec_b2,
    ln2_gain,
    ln2_bias,
    mlp_w1,
    mlp_b1,
    mlp_w2,
    mlp_b2,
):
    own = lax.axis_index("blk").astype(jnp.int32).reshape(1)
    cube = (SMAX, SMAX, LANES)
    x = block_input.reshape(cube)
    gain1, bias1 = ln1_gain.reshape(1, LANES), ln1_bias.reshape(1, LANES)

    stats = lax.all_gather(moments(item_sides, x), "blk", axis=0)
    *g_pieces, grad_b2 = cotangent_pieces(item_sides, own, cotangent.reshape(cube))
    gs = [piece.reshape(CHUNKS * PIECE, LANES) for piece in exchange(g_pieces)]
    vectors = lax.all_gather(jnp.concatenate([mlp_b1, ln2_gain, ln2_bias]), "blk", axis=0)
    b1_full = vectors[:, :HID].reshape(4, 1, HID)
    gain2 = vectors[:, HID : HID + LANES].reshape(1, C)
    bias2 = vectors[:, HID + LANES :].reshape(1, C)
    w1_full = lax.all_gather(mlp_w1, "blk", axis=0)
    w2_full = lax.all_gather(mlp_w2, "blk", axis=0)

    f6, g6, ft3, gt3, w1c, w2c, w1t, w2t = prepare(table(item_sides, item_modes), spec_w1, spec_w2)
    b, xn, xhat, r = first_stage(item_sides, x, stats, gain1, bias1, f6)
    bre, bim, a, p, o = mix_forward(
        b, g6, w1c, spec_b1.reshape(1, 256), w2c, spec_b2.reshape(1, 256), gt3
    )
    x1 = [last_stage(own, bre, bim, xn, ft3, chunk) for chunk in range(CHUNKS)]
    x1_in = [exchange(pieces) for pieces in x1]

    weights = split_weights(w1_full, w2_full)
    keep = None
    dx_in, out_in, b1s, smalls = [], [], [], []
    for chunk in range(CHUNKS):
        xs = [piece.reshape(PIECE, LANES) for piece in x1_in[chunk]]
        results = feed(own, xs, gs, weights, b1_full, gain2, bias2, keep, chunk)
        dx_in.append([v.reshape(SLABS, SMAX, LANES) for v in exchange(results[:4])])
        out_in.append(results[4:8])
        keep = results[8:16]
        b1s.append(results[16])
        smalls.append(results[17])
    out_in = [[v.reshape(SLABS, SMAX, LANES) for v in exchange(pieces)] for pieces in out_in]

    partial = weight_grads(keep, b1s, smalls)
    mine = lax.psum_scatter(partial, "blk", scatter_dimension=0, tiled=False)
    mine = lax.psum(mine, "dp")

    back = None
    for chunk in range(CHUNKS):
        back = first_back(own, dx_in[chunk], f6, back, chunk)
    d, dx = back
    dre, dim, dw1, dw2, db1, db2 = mix_backward(d, a, p, o, g6, w1t, w2t, gt3)
    dn, sums, small1 = last_back(dre, dim, dx, xhat, gain1, ft3)
    sums = lax.all_gather(sums, "blk", axis=0)
    input_grad = final_stage(item_sides, dx, dn, xhat, sums, r, gain1)

    block_output = None
    for chunk in range(CHUNKS):
        block_output = output_stage(
            item_sides, own, x1[chunk], out_in[chunk], mlp_b2.reshape(1, LANES), block_output, chunk
        )

    blocks = []
    for full in (dw1, dw2):
        for block in range(2):
            low, high = slice(block * 64, block * 64 + 64), slice(128 + block * 64, 192 + block * 64)
            blocks.append(full[low, low] + full[high, high])
            blocks.append(full[low, high] - full[high, low])
    packed = jnp.concatenate(
        [jnp.stack(blocks).reshape(-1), db1.sum(0), db2.sum(0), small1.sum(1).reshape(-1), grad_b2.sum(0)]
    )
    packed = doubling_sum(packed.reshape(-1, LANES), dp_size).reshape(-1)
    spec = packed[: 8 * 4096].reshape(2, 2, 2, 64, 64).transpose(0, 2, 1, 3, 4)
    rest = packed[8 * 4096 :]
    tail = mine[2 * C :]
    return (
        block_output.reshape(SMAX * SMAX, LANES),
        input_grad.reshape(SMAX * SMAX, LANES),
        rest[512:640],
        rest[640:768],
        spec[0],
        rest[:256].reshape(2, 2, 64),
        spec[1],
        rest[256:512].reshape(2, 2, 64),
        tail[8:, :LANES].sum(0),
        tail[8:, LANES : 2 * LANES].sum(0),
        mine[:C],
        tail[:8].sum(0),
        mine[C : 2 * C].T,
        rest[768:896],
    )


def solution(mesh):
    in_specs = (
        P("dp", "blk"),
        P("dp", "blk"),
        P("dp"),
        P("dp"),
        P("blk"),
        P("blk"),
        P(None, "blk", None, None),
        P(None, "blk", None),
        P(None, "blk", None, None),
        P(None, "blk", None),
        P("blk"),
        P("blk"),
        P(None, "blk"),
        P("blk"),
        P("blk", None),
        P("blk"),
    )
    out_specs = (
        P("dp", "blk"),
        P("dp", "blk"),
        P("blk"),
        P("blk"),
        P(None, "blk", None, None),
        P(None, "blk", None),
        P(None, "blk", None, None),
        P(None, "blk", None),
        P("blk"),
        P("blk"),
        P(None, "blk"),
        P("blk"),
        P("blk", None),
        P("blk"),
    )
    return jax.shard_map(
        functools.partial(per_device, mesh.shape["dp"]),
        mesh=mesh,
        in_specs=in_specs,
        out_specs=out_specs,
        check_vma=False,
    )
```

time: 1440 us -> 597 us (0.41)
  matrix products: 605 us -> 0 us
  waiting for transfers between devices: 528 us -> 130 us
  Pallas kernels: 0 us -> 293 us
  other arithmetic: 123 us -> 13 us
  local copies, waits for them, and re-layouts: 95.4 us -> 16.2 us
  starting transfers between devices: 0.29 us -> 33.2 us
  blocking collectives: 67.1 us -> 94.1 us
    dot_general x54 -> x0, matrix products: 605 us -> none  [the longest x48 350 us: contract(): return jnp.einsum(form, left, right, precision=lax.Precision.HIGHEST)]
    pallas_call x0 -> x22, Pallas kernels: none -> 293 us  [the longest x3 96.3 us: feed(): call(feed_body, shapes, in_specs, [piece] * 8 + [wide] * 4 + [narrow] * 4...]
    all_gather x2, waiting for transfers between devices: 212 us -> 0.01 us  [the longest x1 0.01 us: per_device(): w1_full = lax.all_gather(mlp_w1, 'blk', axis=0)]
    reduce_scatter x2 -> x1, waiting for transfers between devices: 206 us -> 0.02 us  [per_device(): mine = lax.psum_scatter(partial, 'blk', scatter_dimension=0, tiled=False)]
    all_gather x0 -> x3, blocking collectives: none -> 94.1 us  [the longest x1 76.4 us: per_device(): stats = lax.all_gather(moments(item_sides, x), 'blk', axis=0)]
    ppermute x0 -> x33, waiting for transfers between devices: none -> 86.5 us  [swap(): return lax.ppermute(value, axis, [(i, i ^ distance) for i in range(size)])]
    psum x5 -> x0, blocking collectives: 67.1 us -> none  [the longest x2 23.7 us: norm_forward(): total = lax.psum(jnp.sum(value, axis=1), 'blk')]
    psum x3 -> x1, waiting for transfers between devices: 109 us -> 42.2 us  [per_device(): mine = lax.psum(mine, 'dp')]
  transfers between devices with their start and end apart: 7 -> 37, of which waited for: 6 -> 12; matrix products, arithmetic and copies ran while one was open for 11% -> 3% of each run, Pallas kernels for 0% -> 37%
where the time goes in v1:
time: 597 us; the launch traced here: 595 us
  Pallas kernels  293 us (49%)
  waiting for transfers between devices  130 us (22%)
  blocking collectives  94.1 us (16%)
  starting transfers between devices  33.2 us (6%)
  local copies, waits for them, and re-layouts  16.2 us (3%)
  between operations  15.6 us (3%)
  other arithmetic  13 us (2%)
    pallas_call x3, Pallas kernels, feed(): call(feed_body, shapes, in_specs, [piece] * 8 + [wide] * 4 + [narrow] * 4...  96.3 us
    ppermute x33, waiting for transfers between devices, swap(): return lax.ppermute(value, axis, [(i, i ^ distance) for i in range(size)])  86.5 us
    all_gather x1, blocking collectives, per_device(): stats = lax.all_gather(moments(item_sides, x), 'blk', axis=0)  76.4 us
    psum x1, waiting for transfers between devices, per_device(): mine = lax.psum(mine, 'dp')  42.2 us
    pallas_call x1, Pallas kernels, weight_grads(): call(weight_body, sds((4, 2 * C + 16, HID)), [wide] * 4 + [narrow] * 4 +...  42.1 us
    ppermute x33, starting transfers between devices, swap(): return lax.ppermute(value, axis, [(i, i ^ distance) for i in range(size)])  33.1 us
    pallas_call x1, Pallas kernels, mix_forward(): call(mix_body, [half, half] + [sds((4096, 256))] * 3, [re, im, whole((128...  32.6 us
    pallas_call x1, Pallas kernels, mix_backward(): call(mix_back_body, [half, half, sds((256, 256)), sds((256, 256)), sds((8...  25.8 us
  transfers between devices with their start and end apart: 37, of which 12 were waited for; matrix products, arithmetic and copies ran while one was open for 3% of the time, Pallas kernels for 37%

profile of v1, /device:TPU:0, one launch (start us, length us, event | category | flops | bytes accessed | tf_op | source)
XLA Modules:
  0.0 594.9 jit_solution(18015416600889847530)
XLA Ops:
  9.4 6.1 %shard_map.268 = (f32[3,8,96,128]{3,2,1,0:T(8,128)}, f32[3,8,96,128]{3,2,1,0:T(8,128)}, f32[3,8,96,128]{3,2,1,0:T(8,128)}, f32[3,8,96,128]{3,2,1,0:T(8,128)}, f32[8,128]{1,0:T(8,128)}) custom-call(s32[1]{0:T(128)} %copy.96.side_ref.refs_0_, s32[1]{0:T(128)} %bitcast.own_ref.refs_0_.refs_1_, f32[96,96,128]{2,1,0:T(8,128)} %bitcast.101), custom_call_target="tpu_custom_call" | custom-call | flops 10000000 | bytes 10000000 | tf_op jit(solution)/shard_map/pallas_call | solution.py:225
  15.9 2.5 collective-permute-start.4
  20.6 1.7 multiply_select_fusion.f_ref
  22.3 2.8 shard_map.264
  25.1 8.8 %shard_map.263 = f32[2,96,128]{2,1,0:T(8,128)} custom-call(s32[1]{0:T(128)} %copy.96.side_ref.refs_0_, f32[96,96,128]{2,1,0:T(8,128)} %bitcast.102), custom_call_target="tpu_custom_call" | custom-call | flops 10000000 | bytes 5000000 | tf_op jit(solution)/shard_map/pallas_call | solution.py:196
  33.9 76.4 %all-gather = f32[8,96,128]{2,1,0:T(8,128)} all-gather(f32[2,96,128]{2,1,0:T(8,128)} %shard_map.263), channel_id=2, replica_groups=mesh['dp'=8,'blk'=4] {'blk'}, dimensions={0}, use_global_device_ids=true | all-gather | bytes 491520 | tf_op jit(solution)/shard_map/all_gather | solution.py:818
  110.3 12.7 %shard_map.265 = (f32[96,128,128]{2,1,0:T(8,128)}, f32[96,96,128]{2,1,0:T(8,128)}, f32[96,96,128]{2,1,0:T(8,128)}, f32[96,128]{1,0:T(8,128)}) custom-call(s32[1]{0:T(128)} %copy.96.side_ref.refs_0_, f32[96,96,128]{2,1,0:T(8,128)} %bitcast.103, f32[4,2,96,128]{3,2,1,0:T(8,128)} %bitcast.134, f32[1,128]{1,0:T(1,128)} %bitcast.140, f32[1,128]{1,0:T(1,128)} %bitcast.171, ...), custom_call_target="tpu_custom_call" | custom-call | flops 2000000000 | bytes 20000000 | tf_op jit(solution)/shard_map/pallas_call | solution.py:270
  123.0 32.6 %shard_map.266 = (f32[96,64,128]{2,1,0:T(8,128)}, f32[96,64,128]{2,1,0:T(8,128)}, f32[4096,256]{1,0:T(8,128)}, f32[4096,256]{1,0:T(8,128)}, f32[4096,256]{1,0:T(8,128)}) custom-call(f32[96,128,128]{2,1,0:T(8,128)} %get-tuple-element.122.re_ref.im_ref, f32[96,128,128]{2,1,0:T(8,128)} %get-tuple-element.122.re_ref.im_ref, ...), custom_call_target="tpu_custom_call" | custom-call | flops 10000000000 | bytes 30000000 | tf_op jit(solution)/shard_map/pallas_call | solution.py:350
  155.6 3.6 shard_map.271
  159.4 3.4 collective-permute-start.10
  162.9 10.6 %all-gather.5 = f32[4,1,768]{2,1,0:T(1,128)S(1)} all-gather(f32[1,1,768]{2,1,0:T(1,128)S(1)} %reshape.282), channel_id=5, replica_groups=mesh['dp'=8,'blk'=4] {'blk'}, dimensions={0}, use_global_device_ids=true | all-gather | bytes 15360 | tf_op jit(solution)/shard_map/all_gather | solution.py:821
  174.1 1.7 collective-permute-start.11
  175.8 3.6 shard_map.267
  179.3 3.6 shard_map.270
  183.6 7.3 %shard_map.269 = (bf16[4,512,512]{2,1,0:T(8,128)(2,1)}, bf16[4,512,512]{2,1,0:T(8,128)(2,1)}, bf16[4,512,512]{2,1,0:T(8,128)(2,1)}, bf16[4,512,512]{2,1,0:T(8,128)(2,1)}) custom-call(f32[4,512,512]{2,1,0:T(8,128)} %bitcast.105, f32[4,512,512]{2,1,0:T(8,128)} %bitcast.106), custom_call_target="tpu_custom_call" | custom-call | flops 10000000 | bytes 16000000 | tf_op jit(solution)/shard_map/pallas_call | solution.py:400
  191.6 1.8 collective-permute-start.7
  194.4 32.1 %shard_map.272 = (f32[768,128]{1,0:T(8,128)}, f32[768,128]{1,0:T(8,128)}, f32[768,128]{1,0:T(8,128)}, f32[768,128]{1,0:T(8,128)}, f32[768,128]{1,0:T(8,128)}, /*...) custom-call(s32[1]{0:T(128)} %bitcast.own_ref.refs_0_.refs_1_, ...), custom_call_target="tpu_custom_call" | custom-call | flops 19327352832 | bytes 40000000 | tf_op jit(solution)/shard_map/pallas_call | solution.py:523
  228.4 32.1 %shard_map.273 = (f32[768,128]{1,0:T(8,128)}, f32[768,128]{1,0:T(8,128)}, f32[768,128]{1,0:T(8,128)}, f32[768,128]{1,0:T(8,128)}, f32[768,128]{1,0:T(8,128)}, /*...) custom-call(s32[1]{0:T(128)} %bitcast.own_ref.refs_0_.refs_1_, ...), custom_call_target="tpu_custom_call", output_to_operand_aliasing={{8}: (16, {}), {9}: (17, {}), {10}: (18, {}), {11}: (19, {}... | custom-call | flops 19327352832 | bytes 40000000 | tf_op jit(solution)/shard_map/pallas_call | solution.py:523
  261.5 32.1 %shard_map.274 = (f32[768,128]{1,0:T(8,128)}, f32[768,128]{1,0:T(8,128)}, f32[768,128]{1,0:T(8,128)}, f32[768,128]{1,0:T(8,128)}, f32[768,128]{1,0:T(8,128)}, /*...) custom-call(s32[1]{0:T(128)} %bitcast.own_ref.refs_0_.refs_1_, ...), custom_call_target="tpu_custom_call", output_to_operand_aliasing={{8}: (16, {}), {9}: (17, {}), {10}: (18, {}), {11}: (19, {}... | custom-call | flops 19327352832 | bytes 40000000 | tf_op jit(solution)/shard_map/pallas_call | solution.py:523
  293.6 42.1 %shard_map.284 = f32[4,1040,512]{2,1,0:T(8,128)} custom-call(bf16[2304,2048]{1,0:T(8,128)(2,1)} %get-tuple-element.214.hh, bf16[2304,2048]{1,0:T(8,128)(2,1)} %get-tuple-element.215.hl, bf16[2304,2048]{1,0:T(8,128)(2,1)} %get-tuple-element.216.ph, bf16[2304,2048]{1,0:T(8,128)(2,1)} %get-tuple-element.217.plo, bf16[2304,512]{1,0:T(8,128)(2,1)} %get-tuple-element.218.nh, ...), custom_call_target="tpu_custom_call" | custom-call | flops 28991029248 | bytes 60000000 | tf_op jit(solution)/shard_map/pallas_call | solution.py:567
  341.0 8.2 %collective-permute-done.28 = f32[768,128]{1,0:T(8,128)S(1)} collective-permute-done((f32[768,128]{1,0:T(8,128)S(1)}, f32[768,128]{1,0:T(8,128)S(1)}, u32[]{:S(2)}, u32[]{:S(2)}) %collective-permute-start.28) | collective-permute-done | bytes 393248 | tf_op jit(solution)/shard_map/ppermute | solution.py:779
  350.2 6.0 %collective-permute-done.29 = f32[768,128]{1,0:T(8,128)S(1)} collective-permute-done((f32[768,128]{1,0:T(8,128)S(1)}, f32[768,128]{1,0:T(8,128)S(1)}, u32[]{:S(2)}, u32[]{:S(2)}) %collective-permute-start.29) | collective-permute-done | bytes 393248 | tf_op jit(solution)/shard_map/ppermute | solution.py:779
  356.1 1.9 collective-permute-start.23
  358.0 3.8 shard_map.278
  361.9 7.9 %collective-permute-done.25 = f32[768,128]{1,0:T(8,128)S(1)} collective-permute-done((f32[768,128]{1,0:T(8,128)}, f32[768,128]{1,0:T(8,128)S(1)}, u32[]{:S(2)}, u32[]{:S(2)}) %collective-permute-start.25) | collective-permute-done | bytes 393248 | tf_op jit(solution)/shard_map/ppermute | solution.py:779
  369.7 16.0 %collective-permute-done.26 = f32[768,128]{1,0:T(8,128)S(1)} collective-permute-done((f32[768,128]{1,0:T(8,128)S(1)}, f32[768,128]{1,0:T(8,128)S(1)}, u32[]{:S(2)}, u32[]{:S(2)}) %collective-permute-start.26) | collective-permute-done | bytes 393248 | tf_op jit(solution)/shard_map/ppermute | solution.py:779
  386.5 3.9 shard_map.279
  390.4 1.7 collective-permute-start.18
  392.1 11.4 %collective-permute-done.22 = f32[768,128]{1,0:T(8,128)S(1)} collective-permute-done((f32[768,128]{1,0:T(8,128)}, f32[768,128]{1,0:T(8,128)S(1)}, u32[]{:S(2)}, u32[]{:S(2)}) %collective-permute-start.22) | collective-permute-done | bytes 393248 | tf_op jit(solution)/shard_map/ppermute | solution.py:779
  403.4 1.6 collective-permute-start.19
  405.1 14.5 %collective-permute-done.23 = f32[768,128]{1,0:T(8,128)S(1)} collective-permute-done((f32[768,128]{1,0:T(8,128)}, f32[768,128]{1,0:T(8,128)S(1)}, u32[]{:S(2)}, u32[]{:S(2)}) %collective-permute-start.23) | collective-permute-done | bytes 393248 | tf_op jit(solution)/shard_map/ppermute | solution.py:779
  420.3 3.8 shard_map.280
  424.2 25.8 %shard_map.281 = (f32[96,64,128]{2,1,0:T(8,128)}, f32[96,64,128]{2,1,0:T(8,128)}, f32[256,256]{1,0:T(8,128)}, f32[256,256]{1,0:T(8,128)}, f32[8,256]{1,0:T(8,128)}, /*index=5*/f32[8,256]{1,0:T(8,128)}) custom-call(f32[96,128,128]{2,1,0:T(8,128)} %get-tuple-element.196.re_ref.im_ref, f32[96,128,128]{2,1,0:T(8,128)} %get-tuple-element.196.re_ref.im_ref, ...), custom_call_target="tpu_custom_call" | custom-call | flops 10000000000 | bytes 30000000 | tf_op jit(solution)/shard_map/pallas_call | solution.py:653
  458.1 13.1 %shard_map.282 = (f32[96,96,128]{2,1,0:T(8,128)}, f32[2,96,128]{2,1,0:T(8,128)}, f32[2,8,128]{2,1,0:T(8,128)}) custom-call(f32[96,64,128]{2,1,0:T(8,128)} %get-tuple-element.202.re_ref, f32[96,64,128]{2,1,0:T(8,128)} %get-tuple-element.203.im_ref, f32[96,96,128]{2,1,0:T(8,128)} %get-tuple-element.195.dx_ref, f32[96,96,128]{2,1,0:T(8,128)} %get-tuple-element.204.xhat_ref, ...), custom_call_target="tpu_custom_call" | custom-call | flops 2000000000 | bytes 20000000 | tf_op jit(solution)/shard_map/pallas_call | solution.py:697
  473.0 1.9 collective-permute-start.20
  478.7 5.8 collective-permute-done.20
  484.5 1.8 collective-permute-start.31
  486.3 3.2 shard_map.275.refs_11_
  489.6 3.4 collective-permute-done.17
  493.7 3.2 shard_map.276.refs_11_
  496.9 5.5 collective-permute-done.13
  502.4 6.6 %collective-permute-done.14 = f32[768,128]{1,0:T(8,128)S(1)} collective-permute-done((f32[768,128]{1,0:T(8,128)S(1)}, f32[768,128]{1,0:T(8,128)S(1)}, u32[]{:S(2)}, u32[]{:S(2)}) %collective-permute-start.14) | collective-permute-done | bytes 393248 | tf_op jit(solution)/shard_map/ppermute | solution.py:779
  509.7 3.2 shard_map.277
  513.0 3.2 collective-permute-start.32
  516.2 7.1 %all-gather.4 = f32[8,96,128]{2,1,0:T(8,128)} all-gather(f32[2,96,128]{2,1,0:T(8,128)S(1)} %copy-done.21), channel_id=6, replica_groups=mesh['dp'=8,'blk'=4] {'blk'}, dimensions={0}, use_global_device_ids=true | all-gather | bytes 491520 | tf_op jit(solution)/shard_map/all_gather | solution.py:859
  523.3 13.0 %shard_map.283 = f32[96,96,128]{2,1,0:T(8,128)} custom-call(s32[1]{0:T(128)} %copy.96.side_ref.refs_0_, f32[96,96,128]{2,1,0:T(8,128)} %get-tuple-element.195.dx_ref, f32[96,96,128]{2,1,0:T(8,128)} %get-tuple-element.205.dn_ref, f32[96,96,128]{2,1,0:T(8,128)} %get-tuple-element.204.xhat_ref, f32[4,2,96,128]{3,2,1,0:T(8,128)} %bitcast.108, ...), custom_call_target="tpu_custom_call" | custom-call | flops 100000000 | bytes 20000000 | tf_op jit(solution)/shard_map/pallas_call | solution.py:725
  539.6 42.2 %all-reduce.2.cloned.1.call-done = f32[1040,512]{1,0:T(8,128)} async-done(((f32[1040,512]{1,0:T(8,128)}), f32[1040,512]{1,0:T(8,128)}) %all-reduce.2.cloned.1.call-update) | async-done | bytes 2129936 | tf_op jit(solution)/shard_map/psum | solution.py:851
  581.9 2.7 slice_bitcast_fusion
  (201 shorter events, 39.5 us)
Async XLA Ops:
  7.2 176.3 %all-gather.9.cloned.1.call-start = ((), (), s32[]{:S(2)}) async-start(), calls=%async_computation.3 | async-start | bytes 5242880 | tf_op jit(solution)/shard_map/all_gather | solution.py:825
  7.9 175.6 %all-gather.11.cloned.1.call-start = ((), (), s32[]{:S(2)}) async-start(), calls=%async_computation.4 | async-start | bytes 5242880 | tf_op jit(solution)/shard_map/all_gather | solution.py:826
  8.7 462.6 %reduce-scatter.2.cloned.1.call-start = ((), (), s32[]{:S(2)}) async-start(), calls=%async_computation.1 | async-start | bytes 10649600 | tf_op jit(solution)/shard_map/reduce_scatter | solution.py:850
  15.5 176.0 %collective-permute-start.3 = (f32[3,8,96,128]{3,2,1,0:T(8,128)}, f32[3,8,96,128]{3,2,1,0:T(8,128)S(1)}, u32[]{:S(2)}, u32[]{:S(2)}) collective-permute-start(f32[3,8,96,128]{3,2,1,0:T(8,128)} %get-tuple-element.136), channel_id=1, source_target_pairs={{0,1},{1,0},{2,3},{3,2},{4,5},{5,4},{6,7},{7,6},{8,9},{9,8},{10,11... | collective-permute-start | bytes 3538952 | tf_op jit(solution)/shard_map/ppermute | solution.py:779
  15.9 175.6 %collective-permute-start.4 = (f32[3,8,96,128]{3,2,1,0:T(8,128)}, f32[3,8,96,128]{3,2,1,0:T(8,128)S(1)}, u32[]{:S(2)}, u32[]{:S(2)}) collective-permute-start(f32[3,8,96,128]{3,2,1,0:T(8,128)} %get-tuple-element.137), channel_id=1, source_target_pairs={{0,2},{1,3},{2,0},{3,1},{4,6},{5,7},{6,4},{7,5},{8,10},{9,11},{10,... | collective-permute-start | bytes 3538952 | tf_op jit(solution)/shard_map/ppermute | solution.py:779
  18.5 174.9 %collective-permute-start.5 = (f32[3,8,96,128]{3,2,1,0:T(8,128)}, f32[3,8,96,128]{3,2,1,0:T(8,128)S(1)}, u32[]{:S(2)}, u32[]{:S(2)}) collective-permute-start(f32[3,8,96,128]{3,2,1,0:T(8,128)} %get-tuple-element.138), channel_id=1, source_target_pairs={{0,3},{1,2},{2,1},{3,0},{4,7},{5,6},{6,5},{7,4},{8,11},{9,10},{10,... | collective-permute-start | bytes 3538952 | tf_op jit(solution)/shard_map/ppermute | solution.py:779
  159.2 14.9 %collective-permute-start.9 = (f32[8,96,128]{2,1,0:T(8,128)}, f32[8,96,128]{2,1,0:T(8,128)S(1)}, u32[]{:S(2)}, u32[]{:S(2)}) collective-permute-start(f32[8,96,128]{2,1,0:T(8,128)} %get-tuple-element.148.refs_3_), channel_id=1, source_target_pairs={{0,1},{1,0},{2,3},{3,2},{4,5},{5,4},{6,7},{7,6},{8,9},{9,8},{10,11... | collective-permute-start | bytes 1179656 | tf_op jit(solution)/shard_map/ppermute | solution.py:779
  159.4 31.4 %collective-permute-start.10 = (f32[8,96,128]{2,1,0:T(8,128)}, f32[8,96,128]{2,1,0:T(8,128)}, u32[]{:S(2)}, u32[]{:S(2)}) collective-permute-start(f32[8,96,128]{2,1,0:T(8,128)} %get-tuple-element.149.refs_4_), channel_id=1, source_target_pairs={{0,2},{1,3},{2,0},{3,1},{4,6},{5,7},{6,4},{7,5},{8,10},{9,11},{10,... | collective-permute-start | bytes 1179656 | tf_op jit(solution)/shard_map/ppermute | solution.py:779
  174.1 17.1 %collective-permute-start.11 = (f32[8,96,128]{2,1,0:T(8,128)}, f32[8,96,128]{2,1,0:T(8,128)}, u32[]{:S(2)}, u32[]{:S(2)}) collective-permute-start(f32[8,96,128]{2,1,0:T(8,128)} %get-tuple-element.150.refs_5_), channel_id=1, source_target_pairs={{0,3},{1,2},{2,1},{3,0},{4,7},{5,6},{6,5},{7,4},{8,11},{9,10},{10,... | collective-permute-start | bytes 1179656 | tf_op jit(solution)/shard_map/ppermute | solution.py:779
  190.9 69.6 %collective-permute-start = (f32[8,96,128]{2,1,0:T(8,128)S(1)}, f32[8,96,128]{2,1,0:T(8,128)S(1)}, u32[]{:S(2)}, u32[]{:S(2)}) collective-permute-start(f32[8,96,128]{2,1,0:T(8,128)S(1)} %copy-done), channel_id=1, source_target_pairs={{0,1},{1,0},{2,3},{3,2},{4,5},{5,4},{6,7},{7,6},{8,9},{9,8},{10,11... | collective-permute-start | bytes 1179656 | tf_op jit(solution)/shard_map/ppermute | solution.py:779
  191.2 69.4 %collective-permute-start.1 = (f32[8,96,128]{2,1,0:T(8,128)S(1)}, f32[8,96,128]{2,1,0:T(8,128)S(1)}, u32[]{:S(2)}, u32[]{:S(2)}) collective-permute-start(f32[8,96,128]{2,1,0:T(8,128)S(1)} %copy-done.1), channel_id=1, source_target_pairs={{0,2},{1,3},{2,0},{3,1},{4,6},{5,7},{6,4},{7,5},{8,10},{9,11},{10,... | collective-permute-start | bytes 1179656 | tf_op jit(solution)/shard_map/ppermute | solution.py:779
  191.5 35.0 %collective-permute-start.6 = (f32[8,96,128]{2,1,0:T(8,128)S(1)}, f32[8,96,128]{2,1,0:T(8,128)S(1)}, u32[]{:S(2)}, u32[]{:S(2)}) collective-permute-start(f32[8,96,128]{2,1,0:T(8,128)S(1)} %copy-done.3), channel_id=1, source_target_pairs={{0,1},{1,0},{2,3},{3,2},{4,5},{5,4},{6,7},{7,6},{8,9},{9,8},{10,11... | collective-permute-start | bytes 1179656 | tf_op jit(solution)/shard_map/ppermute | solution.py:779
  191.6 35.9 %collective-permute-start.7 = (f32[8,96,128]{2,1,0:T(8,128)S(1)}, f32[8,96,128]{2,1,0:T(8,128)S(1)}, u32[]{:S(2)}, u32[]{:S(2)}) collective-permute-start(f32[8,96,128]{2,1,0:T(8,128)S(1)} %copy-done.4), channel_id=1, source_target_pairs={{0,2},{1,3},{2,0},{3,1},{4,6},{5,7},{6,4},{7,5},{8,10},{9,11},{10,... | collective-permute-start | bytes 1179656 | tf_op jit(solution)/shard_map/ppermute | solution.py:779
  193.4 34.1 %collective-permute-start.8 = (f32[8,96,128]{2,1,0:T(8,128)S(1)}, f32[8,96,128]{2,1,0:T(8,128)S(1)}, u32[]{:S(2)}, u32[]{:S(2)}) collective-permute-start(f32[8,96,128]{2,1,0:T(8,128)S(1)} %copy-done.5), channel_id=1, source_target_pairs={{0,3},{1,2},{2,1},{3,0},{4,7},{5,6},{6,5},{7,4},{8,11},{9,10},{10,... | collective-permute-start | bytes 1179656 | tf_op jit(solution)/shard_map/ppermute | solution.py:779
  194.4 32.1 %copy-start.2 = (f32[8,96,128]{2,1,0:T(8,128)S(1)}, f32[8,96,128]{2,1,0:T(8,128)}, u32[]{:S(2)}) copy-start(f32[8,96,128]{2,1,0:T(8,128)} %get-tuple-element.134.refs_5_) | copy-start | bytes 1179652
  226.6 34.0 %collective-permute-start.2 = (f32[8,96,128]{2,1,0:T(8,128)S(1)}, f32[8,96,128]{2,1,0:T(8,128)S(1)}, u32[]{:S(2)}, u32[]{:S(2)}) collective-permute-start(f32[8,96,128]{2,1,0:T(8,128)S(1)} %copy-done.2), channel_id=1, source_target_pairs={{0,3},{1,2},{2,1},{3,0},{4,7},{5,6},{6,5},{7,4},{8,11},{9,10},{10,... | collective-permute-start | bytes 1179656 | tf_op jit(solution)/shard_map/ppermute | solution.py:779
  335.8 22.2 %copy-start.22 = (f32[8,128]{1,0:T(8,128)S(1)}, f32[8,128]{1,0:T(8,128)}, u32[]{:S(2)}) copy-start(f32[8,128]{1,0:T(8,128)} %get-tuple-element.213) | copy-start | bytes 12292
  335.8 246.0 %all-reduce.2.cloned.1.call-start = ((), (), s32[]{:S(2)}) async-start(), calls=%async_computation.2 | async-start | bytes 4259840 | tf_op jit(solution)/shard_map/psum | solution.py:851
  336.7 3.2 collective-permute-start.24
  336.9 3.9 collective-permute-start.27
  337.2 12.0 %collective-permute-start.28 = (f32[768,128]{1,0:T(8,128)S(1)}, f32[768,128]{1,0:T(8,128)S(1)}, u32[]{:S(2)}, u32[]{:S(2)}) collective-permute-start(f32[768,128]{1,0:T(8,128)S(1)} %copy-done.36), channel_id=1, source_target_pairs={{0,2},{1,3},{2,0},{3,1},{4,6},{5,7},{6,4},{7,5},{8,10},{9,11},{10,... | collective-permute-start | bytes 1179656 | tf_op jit(solution)/shard_map/ppermute | solution.py:779
  338.2 17.9 %collective-permute-start.29 = (f32[768,128]{1,0:T(8,128)S(1)}, f32[768,128]{1,0:T(8,128)S(1)}, u32[]{:S(2)}, u32[]{:S(2)}) collective-permute-start(f32[768,128]{1,0:T(8,128)S(1)} %copy-done.35), channel_id=1, source_target_pairs={{0,3},{1,2},{2,1},{3,0},{4,7},{5,6},{6,5},{7,4},{8,11},{9,10},{10,... | collective-permute-start | bytes 1179656 | tf_op jit(solution)/shard_map/ppermute | solution.py:779
  338.8 30.9 %collective-permute-start.25 = (f32[768,128]{1,0:T(8,128)}, f32[768,128]{1,0:T(8,128)S(1)}, u32[]{:S(2)}, u32[]{:S(2)}) collective-permute-start(f32[768,128]{1,0:T(8,128)} %get-tuple-element.185), channel_id=1, source_target_pairs={{0,2},{1,3},{2,0},{3,1},{4,6},{5,7},{6,4},{7,5},{8,10},{9,11},{10,... | collective-permute-start | bytes 1179656 | tf_op jit(solution)/shard_map/ppermute | solution.py:779
  339.9 46.2 %copy-start.10 = (f32[768,128]{1,0:T(8,128)}, f32[768,128]{1,0:T(8,128)S(1)}, u32[]{:S(2)}) copy-start(f32[768,128]{1,0:T(8,128)S(1)} %collective-permute-done.24) | copy-start | bytes 1179652
  339.9 45.8 %collective-permute-start.26 = (f32[768,128]{1,0:T(8,128)S(1)}, f32[768,128]{1,0:T(8,128)S(1)}, u32[]{:S(2)}, u32[]{:S(2)}) collective-permute-start(f32[768,128]{1,0:T(8,128)S(1)} %copy-done.37), channel_id=1, source_target_pairs={{0,3},{1,2},{2,1},{3,0},{4,7},{5,6},{6,5},{7,4},{8,11},{9,10},{10,... | collective-permute-start | bytes 1179656 | tf_op jit(solution)/shard_map/ppermute | solution.py:779
  340.8 17.2 %copy-start.47 = (f32[768,128]{1,0:T(8,128)}, f32[768,128]{1,0:T(8,128)S(1)}, u32[]{:S(2)}) copy-start(f32[768,128]{1,0:T(8,128)S(1)} %collective-permute-done.27) | copy-start | bytes 1179652
  340.8 49.5 %collective-permute-start.21 = (f32[768,128]{1,0:T(8,128)}, f32[768,128]{1,0:T(8,128)S(1)}, u32[]{:S(2)}, u32[]{:S(2)}) collective-permute-start(f32[768,128]{1,0:T(8,128)} %get-tuple-element.180), channel_id=1, source_target_pairs={{0,1},{1,0},{2,3},{3,2},{4,5},{5,4},{6,7},{7,6},{8,9},{9,8},{10,11... | collective-permute-start | bytes 1179656 | tf_op jit(solution)/shard_map/ppermute | solution.py:779
  349.2 54.2 %collective-permute-start.22 = (f32[768,128]{1,0:T(8,128)}, f32[768,128]{1,0:T(8,128)S(1)}, u32[]{:S(2)}, u32[]{:S(2)}) collective-permute-start(f32[768,128]{1,0:T(8,128)} %get-tuple-element.181), channel_id=1, source_target_pairs={{0,2},{1,3},{2,0},{3,1},{4,6},{5,7},{6,4},{7,5},{8,10},{9,11},{10,... | collective-permute-start | bytes 1179656 | tf_op jit(solution)/shard_map/ppermute | solution.py:779
  356.1 63.4 %collective-permute-start.23 = (f32[768,128]{1,0:T(8,128)}, f32[768,128]{1,0:T(8,128)S(1)}, u32[]{:S(2)}, u32[]{:S(2)}) collective-permute-start(f32[768,128]{1,0:T(8,128)} %get-tuple-element.182), channel_id=1, source_target_pairs={{0,3},{1,2},{2,1},{3,0},{4,7},{5,6},{6,5},{7,4},{8,11},{9,10},{10,... | collective-permute-start | bytes 1179656 | tf_op jit(solution)/shard_map/ppermute | solution.py:779
  369.7 16.4 %copy-start.14 = (f32[768,128]{1,0:T(8,128)}, f32[768,128]{1,0:T(8,128)S(1)}, u32[]{:S(2)}) copy-start(f32[768,128]{1,0:T(8,128)S(1)} %collective-permute-done.25) | copy-start | bytes 1179652
  369.7 103.2 %collective-permute-start.15 = (f32[768,128]{1,0:T(8,128)}, f32[768,128]{1,0:T(8,128)S(1)}, u32[]{:S(2)}, u32[]{:S(2)}) collective-permute-start(f32[768,128]{1,0:T(8,128)} %get-tuple-element.172), channel_id=1, source_target_pairs={{0,1},{1,0},{2,3},{3,2},{4,5},{5,4},{6,7},{7,6},{8,9},{9,8},{10,11... | collective-permute-start | bytes 1179656 | tf_op jit(solution)/shard_map/ppermute | solution.py:779
  385.7 89.2 %collective-permute-start.16 = (f32[768,128]{1,0:T(8,128)}, f32[768,128]{1,0:T(8,128)S(1)}, u32[]{:S(2)}, u32[]{:S(2)}) collective-permute-start(f32[768,128]{1,0:T(8,128)} %get-tuple-element.173), channel_id=1, source_target_pairs={{0,2},{1,3},{2,0},{3,1},{4,6},{5,7},{6,4},{7,5},{8,10},{9,11},{10,... | collective-permute-start | bytes 1179656 | tf_op jit(solution)/shard_map/ppermute | solution.py:779
  386.5 17.0 %copy-start.32 = (f32[768,128]{1,0:T(8,128)S(1)}, f32[768,128]{1,0:T(8,128)}, u32[]{:S(2)}) copy-start(f32[768,128]{1,0:T(8,128)} %get-tuple-element.177) | copy-start | bytes 1179652
  390.4 29.2 %copy-start.11 = (f32[768,128]{1,0:T(8,128)}, f32[768,128]{1,0:T(8,128)S(1)}, u32[]{:S(2)}) copy-start(f32[768,128]{1,0:T(8,128)S(1)} %collective-permute-done.21) | copy-start | bytes 1179652
  390.4 84.7 %collective-permute-start.18 = (f32[768,128]{1,0:T(8,128)}, f32[768,128]{1,0:T(8,128)S(1)}, u32[]{:S(2)}, u32[]{:S(2)}) collective-permute-start(f32[768,128]{1,0:T(8,128)} %get-tuple-element.176), channel_id=1, source_target_pairs={{0,1},{1,0},{2,3},{3,2},{4,5},{5,4},{6,7},{7,6},{8,9},{9,8},{10,11... | collective-permute-start | bytes 1179656 | tf_op jit(solution)/shard_map/ppermute | solution.py:779
  403.4 72.3 %collective-permute-start.19 = (f32[768,128]{1,0:T(8,128)S(1)}, f32[768,128]{1,0:T(8,128)S(1)}, u32[]{:S(2)}, u32[]{:S(2)}) collective-permute-start(f32[768,128]{1,0:T(8,128)S(1)} %copy-done.32), channel_id=1, source_target_pairs={{0,2},{1,3},{2,0},{3,1},{4,6},{5,7},{6,4},{7,5},{8,10},{9,11},{10,... | collective-permute-start | bytes 1179656 | tf_op jit(solution)/shard_map/ppermute | solution.py:779
  458.1 16.9 %copy-start.33 = (f32[768,128]{1,0:T(8,128)S(1)}, f32[768,128]{1,0:T(8,128)}, u32[]{:S(2)}) copy-start(f32[768,128]{1,0:T(8,128)} %get-tuple-element.174) | copy-start | bytes 1179652
  458.1 20.5 %copy-start.34 = (f32[768,128]{1,0:T(8,128)S(1)}, f32[768,128]{1,0:T(8,128)}, u32[]{:S(2)}) copy-start(f32[768,128]{1,0:T(8,128)} %get-tuple-element.170) | copy-start | bytes 1179652
  472.0 6.5 %collective-permute-start.30 = (f32[263,128]{1,0:T(8,128)S(1)}, f32[263,128]{1,0:T(8,128)S(1)}, u32[]{:S(2)}, u32[]{:S(2)}) collective-permute-start(f32[263,128]{1,0:T(8,128)S(1)} %bitcast.109), channel_id=1, source_target_pairs={{0,4},{4,0},{8,12},{12,8},{16,20},{20,16},{24,28},{28,24},{1,5},{5... | collective-permute-start | bytes 403976 | tf_op jit(solution)/shard_map/ppermute | solution.py:779
  473.0 19.9 %copy-start.6 = (f32[768,128]{1,0:T(8,128)}, f32[768,128]{1,0:T(8,128)S(1)}, u32[]{:S(2)}) copy-start(f32[768,128]{1,0:T(8,128)S(1)} %collective-permute-done.15) | copy-start | bytes 1179652
  473.0 11.5 %collective-permute-start.20 = (f32[768,128]{1,0:T(8,128)S(1)}, f32[768,128]{1,0:T(8,128)S(1)}, u32[]{:S(2)}, u32[]{:S(2)}) collective-permute-start(f32[768,128]{1,0:T(8,128)S(1)} %copy-done.31), channel_id=1, source_target_pairs={{0,3},{1,2},{2,1},{3,0},{4,7},{5,6},{6,5},{7,4},{8,11},{9,10},{10,... | collective-permute-start | bytes 1179656 | tf_op jit(solution)/shard_map/ppermute | solution.py:779
  474.9 18.0 %copy-start.7 = (f32[768,128]{1,0:T(8,128)}, f32[768,128]{1,0:T(8,128)S(1)}, u32[]{:S(2)}) copy-start(f32[768,128]{1,0:T(8,128)S(1)} %collective-permute-done.16) | copy-start | bytes 1179652
  474.9 18.0 %collective-permute-start.17 = (f32[768,128]{1,0:T(8,128)S(1)}, f32[768,128]{1,0:T(8,128)S(1)}, u32[]{:S(2)}, u32[]{:S(2)}) collective-permute-start(f32[768,128]{1,0:T(8,128)S(1)} %copy-done.33), channel_id=1, source_target_pairs={{0,3},{1,2},{2,1},{3,0},{4,7},{5,6},{6,5},{7,4},{8,11},{9,10},{10,... | collective-permute-start | bytes 1179656 | tf_op jit(solution)/shard_map/ppermute | solution.py:779
  475.0 21.8 %collective-permute-start.12 = (f32[768,128]{1,0:T(8,128)}, f32[768,128]{1,0:T(8,128)S(1)}, u32[]{:S(2)}, u32[]{:S(2)}) collective-permute-start(f32[768,128]{1,0:T(8,128)} %get-tuple-element.168), channel_id=1, source_target_pairs={{0,1},{1,0},{2,3},{3,2},{4,5},{5,4},{6,7},{7,6},{8,9},{9,8},{10,11... | collective-permute-start | bytes 1179656 | tf_op jit(solution)/shard_map/ppermute | solution.py:779
  475.8 26.6 %collective-permute-start.13 = (f32[768,128]{1,0:T(8,128)}, f32[768,128]{1,0:T(8,128)S(1)}, u32[]{:S(2)}, u32[]{:S(2)}) collective-permute-start(f32[768,128]{1,0:T(8,128)} %get-tuple-element.169), channel_id=1, source_target_pairs={{0,2},{1,3},{2,0},{3,1},{4,6},{5,7},{6,4},{7,5},{8,10},{9,11},{10,... | collective-permute-start | bytes 1179656 | tf_op jit(solution)/shard_map/ppermute | solution.py:779
  478.5 30.4 %collective-permute-start.14 = (f32[768,128]{1,0:T(8,128)S(1)}, f32[768,128]{1,0:T(8,128)S(1)}, u32[]{:S(2)}, u32[]{:S(2)}) collective-permute-start(f32[768,128]{1,0:T(8,128)S(1)} %copy-done.34), channel_id=1, source_target_pairs={{0,3},{1,2},{2,1},{3,0},{4,7},{5,6},{6,5},{7,4},{8,11},{9,10},{10,... | collective-permute-start | bytes 1179656 | tf_op jit(solution)/shard_map/ppermute | solution.py:779
  484.5 28.4 %collective-permute-start.31 = (f32[263,128]{1,0:T(8,128)S(1)}, f32[263,128]{1,0:T(8,128)S(1)}, u32[]{:S(2)}, u32[]{:S(2)}) collective-permute-start(f32[263,128]{1,0:T(8,128)S(1)} %bitcast_add_fusion), channel_id=1, source_target_pairs={{0,8},{4,12},{8,0},{12,4},{16,24},{20,28},{24,16},{28,20},{1,9},{5... | collective-permute-start | bytes 403976 | tf_op jit(solution)/shard_map/ppermute | solution.py:779
  513.0 23.3 %collective-permute-start.32 = (f32[263,128]{1,0:T(8,128)S(1)}, f32[263,128]{1,0:T(8,128)S(1)}, u32[]{:S(2)}, u32[]{:S(2)}) collective-permute-start(f32[263,128]{1,0:T(8,128)S(1)} %fusion.15), channel_id=1, source_target_pairs={{0,16},{4,20},{8,24},{12,28},{16,0},{20,4},{24,8},{28,12},{1,17},{... | collective-permute-start | bytes 403976 | tf_op jit(solution)/shard_map/ppermute | solution.py:779
  (39 other events, 207.0 us)
Sparse Core Ops, SparseCore 0:
  9.6 59.7 all-gather.8
  71.0 48.2 all-gather.10
  335.9 118.4 reduce-scatter.1
  471.4 110.4 all-reduce.1

commit v2 on v1

v2 whole, which is shorter than its diff:
```python
import functools
import math

import jax
import jax.numpy as jnp
from jax import lax
from jax.experimental import pallas as pl
from jax.experimental.pallas import tpu as pltpu
from jax.sharding import PartitionSpec as P

C = 512
MODES = 32
SMAX = 96
LANES = 128
FREQ = 64
PARTS = 4
CHUNKS = 3
SLABS = SMAX // (PARTS * CHUNKS)
PIECE = SLABS * SMAX
GROUP = PARTS * SLABS
STEPS = SMAX // SLABS
STAGE = 24
THIRDS = STAGE // SLABS
WIDTH = 8
TILE = 256
SUB = 768
HID = 512
PACK = 4 * FREQ + 8

EPS = 1e-05
SHRINK = 0.01
F32 = jnp.float32
BF16 = jnp.bfloat16
NN = (((1,), (0,)), ((), ()))
NT = (((1,), (1,)), ((), ()))
TN = (((0,), (0,)), ((), ()))
LIMIT = 56 * 1024 * 1024


def mm(left, right, dims=NN):
    return lax.dot_general(left, right, dims, preferred_element_type=F32)


def split2(value):
    high = value.astype(BF16)
    return high, (value - high.astype(F32)).astype(BF16)


def split3(value):
    high = value.astype(BF16)
    rest = value - high.astype(F32)
    mid = rest.astype(BF16)
    return high, mid, (rest - mid.astype(F32)).astype(BF16)


def left6(value):
    one, two, three = split3(value)
    return jnp.concatenate([one, one, two, one, two, three], axis=1)


def right6(value):
    one, two, three = split3(value)
    return jnp.concatenate([one, two, one, three, two, one], axis=0)


def left3(value):
    one, two = split2(value)
    return jnp.concatenate([one, one, two], axis=1)


def right3(value):
    one, two = split2(value)
    return jnp.concatenate([one, two, one], axis=0)


def phi_pair(value):
    cdf = 0.5 + 0.5 * lax.erf(value * math.sqrt(0.5))
    pdf = jnp.exp(value * value * -0.5) * (1.0 / math.sqrt(2.0 * math.pi))
    return cdf, pdf


def pad_rows(value):
    return jnp.concatenate([value, jnp.zeros((LANES - SMAX, value.shape[1]), F32)], axis=0)


def fold_rows(value):
    return jnp.sum(value.reshape(-1, 8, value.shape[-1]), axis=0)


def spread8(rows):
    one, two, three = split3(rows)
    parts = [value.astype(F32) for value in (one, two, three)]
    left = jnp.concatenate(parts + [jnp.zeros_like(rows)], axis=0).astype(BF16)
    index = lax.broadcasted_iota(jnp.int32, (32, SLABS * LANES), 0)
    lane = lax.broadcasted_iota(jnp.int32, (32, SLABS * LANES), 1)
    pick = (index % SLABS == lane // LANES) & (index < 3 * SLABS)
    return mm(left, jnp.where(pick, 1.0, 0.0).astype(BF16), TN)


def slab_of(wide, slab):
    return wide[:SMAX, slab * LANES : (slab + 1) * LANES]


def us(time):
    return (int(time * 1e9), int(time * 3e6))


def call(body, out_shape, in_specs, out_specs, grid=(), scratch=(), aliases=None, cost=None):
    flops, moved = cost or (0, 0)
    return pl.pallas_call(
        body,
        out_shape=out_shape,
        grid=grid,
        in_specs=in_specs,
        out_specs=out_specs,
        scratch_shapes=list(scratch),
        input_output_aliases=aliases or {},
        compiler_params=pltpu.CompilerParams(vmem_limit_bytes=LIMIT),
        cost_estimate=pl.CostEstimate(flops=flops, bytes_accessed=moved, transcendentals=0),
    )


SMEM = pl.BlockSpec(memory_space=pltpu.SMEM)
VMEM = pl.BlockSpec(memory_space=pltpu.VMEM)
ANY = pl.BlockSpec(memory_space=pl.ANY)


def whole(shape):
    zeros = (0,) * len(shape)
    return pl.BlockSpec(shape, lambda *_: zeros)


def sds(shape, dtype=F32):
    return jax.ShapeDtypeStruct(shape, dtype)


def table(item_sides, item_modes):
    row = lax.broadcasted_iota(jnp.int32, (LANES, LANES), 0)
    cell = lax.broadcasted_iota(jnp.int32, (LANES, LANES), 1)
    index = row % FREQ
    frequency = index - (MODES - 1)
    extent = item_sides[0]
    phase = frequency * cell % extent
    keep = (jnp.abs(frequency) < item_modes[0]) & (cell < extent) & (index < 2 * MODES - 1)
    length = extent.astype(F32)
    angle = 2.0 * math.pi * phase.astype(F32) / length
    wave = jnp.where(row < FREQ, jnp.cos(angle), -jnp.sin(angle)) * lax.rsqrt(length)
    return jnp.where(keep, wave, jnp.zeros_like(wave))


def big_weight(weight, out):
    out[...] = jnp.zeros_like(out)
    for block in range(2):
        rows = pl.ds(block * 64, 64)
        later = pl.ds(128 + block * 64, 64)
        out[rows, rows] = weight[0, block]
        out[rows, later] = weight[1, block]
        out[later, rows] = -weight[1, block]
        out[later, later] = weight[0, block]


def prepare_body(f_ref, w1_ref, w2_ref, f6, g6, ft3, gt3, w1c, w2c, w1t, w2t, big):
    forward = f_ref[...]
    turned = jnp.concatenate([-forward[FREQ:], forward[:FREQ]], axis=0)
    f6[...] = left6(forward)
    g6[...] = left6(jnp.concatenate([forward, turned], axis=1))
    back = forward.T
    ft3[...] = left3(back)
    gt3[...] = left3(jnp.concatenate([back, turned.T], axis=0))
    for source, straight, across in ((w1_ref, w1c, w1t), (w2_ref, w2c, w2t)):
        big_weight(source, big)
        straight[...] = right6(big[...])
        across[...] = right3(big[...].T)


def prepare(forward, spec_w1, spec_w2):
    shapes = [
        sds((128, 768), BF16),
        sds((128, 1536), BF16),
        sds((128, 384), BF16),
        sds((256, 384), BF16),
        sds((1536, 256), BF16),
        sds((1536, 256), BF16),
        sds((768, 256), BF16),
        sds((768, 256), BF16),
    ]
    return call(
        prepare_body,
        shapes,
        [VMEM] * 3,
        [VMEM] * 8,
        scratch=[pltpu.VMEM((256, 256), F32)],
        cost=us(3),
    )(forward, spec_w1, spec_w2)


def slab_mask(first, side):
    cell = lax.broadcasted_iota(jnp.int32, (SMAX, LANES), 0)
    return (cell < side) & (first < side)


def moments_body(side_ref, x_ref, b1_ref, gain_ref, bias_ref, out_ref):
    step = pl.program_id(0)
    side = side_ref[0]

    @pl.when(step == 0)
    def _():
        vectors = [b1_ref[...], gain_ref[...], bias_ref[...], jnp.zeros((2, LANES), F32)]
        out_ref[2 * STEPS] = jnp.concatenate(vectors, axis=0)

    for slab in range(STAGE):
        inside = slab_mask(step * STAGE + slab, side)
        value = pad_rows(jnp.where(inside, x_ref[slab], 0.0)).T
        mean = jnp.sum(value, axis=0, keepdims=True) * (1.0 / LANES)
        centered = value - mean
        block, row = step * THIRDS + slab // SLABS, pl.ds(slab % SLABS, 1)
        out_ref[block, row, :] = mean
        out_ref[STEPS + block, row, :] = jnp.sum(centered * centered, axis=0, keepdims=True)


def moments(side, x, b1, gain, bias):
    return call(
        moments_body,
        sds((2 * STEPS + 1, SLABS, LANES)),
        [
            SMEM,
            pl.BlockSpec((STAGE, SMAX, LANES), lambda i: (i, 0, 0)),
            whole((4, LANES)),
            whole((1, LANES)),
            whole((1, LANES)),
        ],
        whole((2 * STEPS + 1, SLABS, LANES)),
        grid=(SMAX // STAGE,),
        cost=us(6),
    )(side, x, b1, gain, bias)


def cotangent_body(side_ref, g_ref, out_ref, total):
    chunk = pl.program_id(0)
    side = side_ref[0]

    @pl.when(chunk == 0)
    def _():
        total[...] = jnp.zeros_like(total)

    carry = jnp.zeros((8, LANES), F32)
    for part in range(PARTS):
        for slab in range(SLABS):
            first = part * SLABS + slab
            value = jnp.where(slab_mask(chunk * GROUP + first, side), g_ref[first], 0.0)
            out_ref[part, 0, slab] = value
            carry = carry + fold_rows(value)
    total[...] += carry


def cotangent_pieces(side, g):
    return call(
        cotangent_body,
        [sds((PARTS, CHUNKS, SLABS, SMAX, LANES)), sds((8, LANES))],
        [SMEM, pl.BlockSpec((GROUP, SMAX, LANES), lambda i: (i, 0, 0))],
        [
            pl.BlockSpec((PARTS, 1, SLABS, SMAX, LANES), lambda i: (0, i, 0, 0, 0)),
            whole((8, LANES)),
        ],
        grid=(CHUNKS,),
        cost=us(5),
    )(side, g)


def row_stats(means, totals):
    mean = (means[0] + means[1] + means[2] + means[3]) * (1.0 / PARTS)
    total = totals[0] + totals[1] + totals[2] + totals[3]
    for part in range(PARTS):
        gap = means[part] - mean
        total = total + LANES * (gap * gap)
    spread_ = total * (1.0 / C) + EPS
    inverse = lax.rsqrt(spread_)
    inverse = inverse * (1.5 - 0.5 * spread_ * inverse * inverse)
    return mean, inverse


def first_body(side_ref, x_ref, *refs):
    stats = refs[:PARTS]
    gain_ref, bias_ref, f6_ref, b_ref, xn_ref, xhat_ref, r_ref = refs[PARTS:]
    step = pl.program_id(0)
    side = side_ref[0]
    gain, bias = gain_ref[...], bias_ref[...]
    for third in range(THIRDS):
        block = step * THIRDS + third
        mean, inverse = row_stats([ref[block] for ref in stats], [ref[STEPS + block] for ref in stats])
        r_ref[pl.ds(third * SLABS, SLABS), :] = inverse
        means, scales = spread8(mean), spread8(inverse)
        for pair in range(SLABS // 2):
            columns = []
            for inner in (2 * pair, 2 * pair + 1):
                slab = third * SLABS + inner
                value = jnp.where(slab_mask(step * STAGE + slab, side), x_ref[slab], 0.0)
                centered = value - slab_of(means, inner)
                normal = centered * slab_of(scales, inner)
                normed = normal * gain + bias
                xhat_ref[slab] = normal
                xn_ref[slab] = value + normed
                columns.append(pad_rows(normed))
            out = mm(f6_ref[...], right6(jnp.concatenate(columns, axis=1)))
            b_ref[slab - 1] = out[:, :LANES]
            b_ref[slab] = out[:, LANES:]


def first_stage(side, x, stats, gain, bias, f6):
    field = pl.BlockSpec((STAGE, SMAX, LANES), lambda i: (i, 0, 0))
    return call(
        first_body,
        [sds((SMAX, LANES, LANES)), sds((SMAX, SMAX, LANES)), sds((SMAX, SMAX, LANES)), sds((SMAX, LANES))],
        [SMEM, field]
        + [whole((2 * STEPS + 1, SLABS, LANES))] * PARTS
        + [whole((1, LANES)), whole((1, LANES)), whole((128, 768))],
        [
            pl.BlockSpec((STAGE, LANES, LANES), lambda i: (i, 0, 0)),
            field,
            field,
            pl.BlockSpec((STAGE, LANES), lambda i: (i, 0)),
        ],
        grid=(SMAX // STAGE,),
        cost=us(3),
    )(side, x, *stats, gain, bias, f6)


def gather_columns(re_ref, im_ref, first):
    zeros = jnp.zeros((LANES - SMAX, LANES), F32)
    re, im = [ref.reshape(SMAX * WIDTH, LANES) for ref in (re_ref, im_ref)]
    columns = []
    for j in range(first, first + 4):
        rows = pl.ds(j, SMAX, stride=WIDTH)
        columns.append(jnp.concatenate([re[rows, :], zeros, im[rows, :], zeros], axis=0))
    return jnp.concatenate(columns, axis=1)


def to_rows(out):
    rows = []
    for j in range(4):
        lanes = slice(j * LANES, (j + 1) * LANES)
        rows.append(jnp.concatenate([out[:FREQ, lanes], out[FREQ:, lanes]], axis=1))
    return jnp.concatenate(rows, axis=0)


def to_columns(rows):
    columns = []
    for j in range(4):
        part = rows[j * FREQ : (j + 1) * FREQ]
        columns.append(jnp.concatenate([part[:, :LANES], part[:, LANES:]], axis=0))
    return jnp.concatenate(columns, axis=1)


def scatter_columns(re_ref, im_ref, first, out):
    re, im = [ref.reshape(SMAX * WIDTH, LANES) for ref in (re_ref, im_ref)]
    for j in range(4):
        lanes = slice(j * LANES, (j + 1) * LANES)
        rows = pl.ds(first + j, SMAX, stride=WIDTH)
        re[rows, :] = out[:SMAX, lanes]
        im[rows, :] = out[LANES : LANES + SMAX, lanes]


def shrink(value):
    return jnp.where(
        value > SHRINK,
        value - SHRINK,
        jnp.where(value < -SHRINK, value + SHRINK, jnp.zeros_like(value)),
    )


def mix_body(re_ref, im_ref, g6_ref, w1_ref, b1_ref, w2_ref, b2_ref, gt3_ref, bre, bim, a_out, p_out, o_out):
    for half in range(WIDTH // 4):
        rows = pl.ds(half * TILE, TILE)
        spectrum = to_rows(mm(g6_ref[...], right6(gather_columns(re_ref, im_ref, 4 * half))))
        a_out[rows, :] = spectrum
        pre = mm(left6(spectrum), w1_ref[...]) + b1_ref[...]
        p_out[rows, :] = pre
        cdf = 0.5 + 0.5 * lax.erf(pre * math.sqrt(0.5))
        out = mm(left6(pre * cdf), w2_ref[...]) + b2_ref[...]
        o_out[rows, :] = out
        scatter_columns(bre, bim, 4 * half, mm(gt3_ref[...], right3(to_columns(shrink(out)))))


def mix_forward(b, g6, w1c, bias1, w2c, bias2, gt3):
    count = FREQ // WIDTH
    re = pl.BlockSpec((SMAX, WIDTH, LANES), lambda j: (0, j, 0))
    im = pl.BlockSpec((SMAX, WIDTH, LANES), lambda j: (0, count + j, 0))
    out = pl.BlockSpec((SMAX, WIDTH, LANES), lambda j: (0, j, 0))
    rows = pl.BlockSpec((WIDTH * FREQ, 256), lambda j: (j, 0))
    half = sds((SMAX, FREQ, LANES))
    return call(
        mix_body,
        [half, half] + [sds((4096, 256))] * 3,
        [
            re,
            im,
            whole((128, 1536)),
            whole((1536, 256)),
            whole((1, 256)),
            whole((1536, 256)),
            whole((1, 256)),
            whole((256, 384)),
        ],
        [out, out, rows, rows, rows],
        grid=(count,),
        cost=us(4),
    )(b, b, g6, w1c, bias1, w2c, bias2, gt3)


def last_body(own_ref, re_ref, im_ref, xn_ref, ft3_ref, *refs):
    full = refs[-1]
    outs = refs[-1 - PARTS : -1] if len(refs) > PARTS else None
    tip = None if outs else refs[-2]
    own = own_ref[0]
    for part in range(PARTS):
        base = (own ^ part) * SLABS
        for pair in range(SLABS // 2):
            slabs = (base + 2 * pair, base + 2 * pair + 1)
            columns = [jnp.concatenate([re_ref[s], im_ref[s]], axis=0) for s in slabs]
            out = mm(ft3_ref[...], right3(jnp.concatenate(columns, axis=1)))[:SMAX]
            for index, s in enumerate(slabs):
                value = xn_ref[s] + out[:, index * LANES : (index + 1) * LANES]
                full[s] = value
                if outs:
                    outs[part][2 * pair + index] = value
                else:
                    tip[own ^ part, 2 * pair + index] = value


def last_stage(own, bre, bim, xn, ft3, keep, chunk):
    half = pl.BlockSpec((GROUP, FREQ, LANES), lambda i: (chunk, 0, 0))
    field = pl.BlockSpec((GROUP, SMAX, LANES), lambda i: (chunk, 0, 0))
    args = [own, bre, bim, xn, ft3]
    in_specs = [SMEM, half, half, field, whole((128, 384))]
    aliases = {}
    piece = (SLABS, SMAX, LANES)
    pieces = [piece] * PARTS if chunk < CHUNKS - 1 else [(PARTS,) + piece]
    if keep is not None:
        aliases[len(args)] = len(pieces)
        args.append(keep)
        in_specs.append(ANY)
    *pieces, full = call(
        last_body,
        [sds(shape) for shape in pieces] + [sds((SMAX, SMAX, LANES))],
        in_specs,
        [whole(shape) for shape in pieces] + [field],
        grid=(1,),
        aliases=aliases,
        cost=us(3.5),
    )(*args)
    return pieces, full


def weights_body(own_ref, *refs):
    step = pl.program_id(0)
    own = own_ref[0]
    one, two = refs[0:2], refs[2:4]
    far = refs[4:6]
    w1h, w1l, w2h, w2l = refs[6:]

    def emit(first, second):
        for part in range(PARTS):
            source = pl.ds(pl.multiple_of((own ^ part) * LANES, LANES), LANES)
            target = slice(part * LANES, (part + 1) * LANES)
            w1h[0, target, :], w1l[0, target, :] = split2(first(source))
            w2h[0, :, target], w2l[0, :, target] = split2(second(source))

    for index in range(2):

        @pl.when(step == index)
        def _(index=index):
            emit(lambda rows: one[index][rows, :], lambda lanes: two[index][:, lanes])

        @pl.when(step == 2 + index)
        def _(index=index):
            ref = far[index]
            depth = ref.shape[0] // PARTS

            def rows_of(rows):
                first = pl.multiple_of(rows.start // ref.shape[2], depth)
                return ref[pl.ds(first, depth), 0].reshape(LANES, 512)

            emit(rows_of, lambda lanes: ref[:, 1, :, lanes].reshape(512, LANES))


def split_weights(own, one, two, far):
    block = pl.BlockSpec((1, 512, 512), lambda i: (i, 0, 0))
    return call(
        weights_body,
        [sds((4, 512, 512), BF16)] * 4,
        [SMEM] + [whole((512, 512))] * 4 + [whole(far[0].shape)] * 2,
        [block] * 4,
        grid=(4,),
        cost=us(7),
    )(own, *one, *two, *far)


def row_mean(parts):
    total = parts[0] + parts[1] + parts[2] + parts[3]
    return jnp.sum(total, axis=1, keepdims=True) * (1.0 / C)


def part_lanes(part):
    return slice(part * LANES, (part + 1) * LANES)


def norm_tiles(load, vectors, n_h, n_l, nh, nl, xhat, scale):
    def norm(tile, carry):
        rows = pl.ds(tile * TILE, TILE)
        values = [load(part, rows) for part in range(PARTS)]
        mean = row_mean(values)
        centered = [value - mean for value in values]
        spread_ = row_mean([value * value for value in centered]) + EPS
        inverse = lax.rsqrt(spread_)
        inverse = inverse * (1.5 - 0.5 * spread_ * inverse * inverse)
        scale[rows, :] = jnp.broadcast_to(inverse, (TILE, LANES))
        for part in range(PARTS):
            lanes = part_lanes(part)
            normal = centered[part] * inverse
            xhat[rows, lanes] = normal
            gain, bias = vectors[part][0, 4:5, :], vectors[part][0, 5:6, :]
            high, low = split2(normal * gain + bias)
            n_h[rows, lanes] = high
            n_l[rows, lanes] = low
            nh[rows, lanes] = high
            nl[rows, lanes] = low
        return carry

    lax.fori_loop(0, PIECE // TILE, norm, 0)


def bias_of(vectors, step):
    row = jnp.zeros((4, LANES), F32)
    for part in range(PARTS):
        row = jnp.where(step == part, vectors[part][0, 0:4, :], row)
    return jnp.concatenate([row[i : i + 1] for i in range(4)], axis=1)


def grad_tiles(own, g_ref, vectors, dn, xhat, scale, store, small):
    small[...] = jnp.zeros_like(small)

    def back(tile, carry):
        rows = pl.ds(tile * TILE, TILE)
        inverse = scale[rows, :]
        scaled, normals = [], []
        for part in range(PARTS):
            lanes = part_lanes(part)
            grad = dn[rows, lanes]
            normal = xhat[rows, lanes]
            small[0, :, lanes] += fold_rows(grad * normal)
            small[1, :, lanes] += fold_rows(grad)
            scaled.append(grad * vectors[part][0, 4:5, :])
            normals.append(normal)
        first = row_mean(scaled)
        second = row_mean([s * n for s, n in zip(scaled, normals)])
        for part in range(PARTS):
            delta = inverse * (scaled[part] - first - normals[part] * second)
            store(part, rows, g_ref[own ^ part, rows, :] + delta)
        return carry

    lax.fori_loop(0, PIECE // TILE, back, 0)


def split_cotangent(own, g_ref, g_h, g_l):
    for part in range(PARTS):
        lanes = part_lanes(part)
        g_h[:, lanes], g_l[:, lanes] = split2(g_ref[own ^ part])


def product3(high, low, w_h, w_l, dims=NN):
    return mm(high, w_h[0], dims) + mm(low, w_h[0], dims) + mm(high, w_l[0], dims)


def add_to(ref, step, value):
    @pl.when(step == 0)
    def _():
        ref[...] = value

    @pl.when(step > 0)
    def _():
        ref[...] += value


def feed_body(*refs):
    own = refs[0][0]
    x_refs, g_ref = refs[1:5], refs[5]
    w1h, w1l, w2h, w2l = refs[6:10]
    vectors = refs[10:14]
    refs = refs[len(refs) - 21 :]
    hh, hl, nh, nl, out_ref, ph, plo = refs[0:7]
    dx_refs, db1, small = refs[7:11], refs[11], refs[12]
    n_h, n_l, g_h, g_l, xhat, scale, dn, acc = refs[13:21]
    step = pl.program_id(0)

    @pl.when(step == 0)
    def _():
        norm_tiles(lambda part, rows: x_refs[part][rows, :], vectors, n_h, n_l, nh, nl, xhat, scale)
        split_cotangent(own, g_ref, g_h, g_l)

    pre = product3(n_h[...], n_l[...], w1h, w1l) + bias_of(vectors, step)
    dh = product3(g_h[...], g_l[...], w2h, w2l, NT)
    cdf, pdf = phi_pair(pre)
    high, low = split2(pre * cdf)
    hh[...] = high
    hl[...] = low
    grad = dh * (cdf + pre * pdf)
    add_to(acc, step, product3(high, low, w2h, w2l))
    high, low = split2(grad)
    ph[...] = high
    plo[...] = low
    db1[0] = fold_rows(grad)
    add_to(dn, step, product3(high, low, w1h, w1l, NT))

    @pl.when(step == pl.num_programs(0) - 1)
    def _():
        for part in range(PARTS):
            out_ref[own ^ part, 0] = acc[:, part_lanes(part)]

        def store(part, rows, value):
            dx_refs[part][rows, :] = value

        grad_tiles(own, g_ref, vectors, dn, xhat, scale, store, small)


def forward_body(*refs):
    own = refs[0][0]
    x_ref = refs[1]
    w1h, w1l, w2h, w2l = refs[2:6]
    vectors = refs[6:10]
    hh, hl, nh, nl, out_ref, slope, xhat, scale, n_h, n_l, acc = refs[len(refs) - 11 :]
    step = pl.program_id(0)

    @pl.when(step == 0)
    def _():
        norm_tiles(lambda part, rows: x_ref[own ^ part, rows, :], vectors, n_h, n_l, nh, nl, xhat, scale)

    pre = product3(n_h[...], n_l[...], w1h, w1l) + bias_of(vectors, step)
    cdf, pdf = phi_pair(pre)
    slope[...] = cdf + pre * pdf
    high, low = split2(pre * cdf)
    hh[...] = high
    hl[...] = low
    add_to(acc, step, product3(high, low, w2h, w2l))

    @pl.when(step == pl.num_programs(0) - 1)
    def _():
        for part in range(PARTS):
            out_ref[own ^ part, 0] = acc[:, part_lanes(part)]


def backward_body(*refs):
    own = refs[0][0]
    g_ref, w1h, w1l, w2h, w2l, slope, xhat, scale = refs[1:9]
    vectors = refs[9:13]
    ph, plo, dx_ref, db1, small, g_h, g_l, dn = refs[len(refs) - 8 :]
    step = pl.program_id(0)

    @pl.when(step == 0)
    def _():
        split_cotangent(own, g_ref, g_h, g_l)

    grad = product3(g_h[...], g_l[...], w2h, w2l, NT) * slope[...]
    high, low = split2(grad)
    ph[...] = high
    plo[...] = low
    db1[0] = fold_rows(grad)
    add_to(dn, step, product3(high, low, w1h, w1l, NT))

    @pl.when(step == pl.num_programs(0) - 1)
    def _():

        def store(part, rows, value):
            dx_ref[own ^ part, rows, :] = value

        grad_tiles(own, g_ref, vectors, dn, xhat, scale, store, small)


def feed_call(body, head, heads, weights, stats, local, keep, kinds, chunk, cost):
    rows = PIECE * CHUNKS
    specs = {
        "x": (sds((PIECE, LANES)), whole((PIECE, LANES))),
        "g": (None, pl.BlockSpec((PARTS, PIECE, LANES), lambda i: (0, chunk, 0))),
        "out": (
            sds((PARTS, CHUNKS - 1, PIECE, LANES)),
            pl.BlockSpec((PARTS, 1, PIECE, LANES), lambda i: (0, chunk, 0, 0)),
        ),
        "last": (sds((PARTS, 1, PIECE, LANES)), whole((PARTS, 1, PIECE, LANES))),
        "wide": (sds((rows, 2048), BF16), pl.BlockSpec((PIECE, HID), lambda i: (chunk, i))),
        "narrow": (sds((rows, C), BF16), pl.BlockSpec((PIECE, C), lambda i: (chunk, 0))),
        "slope": (sds((PIECE, 2048)), pl.BlockSpec((PIECE, HID), lambda i: (0, i))),
        "four": (sds((PARTS, PIECE, LANES)), whole((PARTS, PIECE, LANES))),
        "full": (sds((PIECE, C)), whole((PIECE, C))),
        "db1": (sds((4, 8, HID)), pl.BlockSpec((1, 8, HID), lambda i: (i, 0, 0))),
        "small": (sds((2, 8, C)), whole((2, 8, C))),
    }
    weight = pl.BlockSpec((1, 512, 512), lambda i: (i, 0, 0))
    vector = pl.BlockSpec((1, SLABS, LANES), lambda i: (2 * STEPS, 0, 0))
    args = [*head, *weights, *(value for _, value in local), *stats]
    in_specs = [SMEM] + [specs[kind][1] for kind in heads] + [weight] * 4
    in_specs += [specs[kind][1] for kind, _ in local] + [vector] * 4
    aliases = {}
    for index, array in enumerate(keep or ()):
        aliases[len(args)] = index
        args.append(array)
        in_specs.append(ANY)
    bf, big = pltpu.VMEM((PIECE, C), BF16), pltpu.VMEM((PIECE, C), F32)
    scratch = {
        "feed": [bf] * 4 + [big, pltpu.VMEM((PIECE, LANES), F32), big, big],
        "fore": [bf, bf, big],
        "back": [bf, bf, big],
    }[kinds]
    outs = {
        "feed": ["wide"] * 2 + ["narrow"] * 2 + ["out", "wide", "wide"] + ["x"] * 4 + ["db1", "small"],
        "fore": ["wide"] * 2 + ["narrow"] * 2 + ["last", "slope", "full", "x"],
        "back": ["wide", "wide", "four", "db1", "small"],
    }[kinds]
    return call(
        body,
        [specs[kind][0] for kind in outs],
        in_specs,
        [specs[kind][1] for kind in outs],
        grid=(4,),
        scratch=scratch,
        aliases=aliases,
        cost=us(cost),
    )(*args)


def feed(own, xs, g, weights, stats, keep, chunk):
    head, heads = [own, *xs, g], ["x"] * 4 + ["g"]
    return feed_call(feed_body, head, heads, weights, stats, [], keep, "feed", chunk, 28)


def feed_forward(own, x, weights, stats, keep, chunk):
    return feed_call(forward_body, [own, x], ["four"], weights, stats, [], keep, "fore", chunk, 18)


def feed_backward(own, g, weights, local, stats, keep, chunk):
    local = list(zip(("slope", "full", "x"), local))
    return feed_call(backward_body, [own, g], ["g"], weights, stats, local, keep, "back", chunk, 1)


def weight_body(own_ref, place_ref, th, tl, *refs):
    send, held, t_h, t_l = refs[-4:]
    step = pl.program_id(0)
    own, place = own_ref[0], place_ref[0]

    @pl.when(step == 0)
    def _():
        if len(refs) == 6:
            t_h[...] = refs[0][...].T
            t_l[...] = refs[1][...].T
        else:
            for part in range(PARTS):
                high, low = split2(refs[0][own ^ part])
                t_h[part_lanes(part), :] = high.T
                t_l[part_lanes(part), :] = low.T

    out = mm(t_h[...], th[...]) + mm(t_l[...], th[...]) + mm(t_h[...], tl[...])
    count, depth = send.shape[1], send.shape[2]

    def store(ref):
        for index in range(count):
            part, inner = divmod(index, count // PARTS)
            apart = ((own ^ part) * (count // PARTS) + inner) ^ place
            where = (apart & 1) * (count // 2) + (apart >> 1)
            ref[0, where] = out[index * depth : (index + 1) * depth]

    @pl.when(step < 2)
    def _():
        store(send)

    @pl.when(step >= 2)
    def _():
        store(held)


def weight_grads(own, place, dp_size, left, th, tl):
    rows = PIECE * CHUNKS
    wide = pl.BlockSpec((rows, HID), lambda i: (0, (i % 2) * 2 + 1 - i // 2))
    block = (1, dp_size, C // dp_size, HID)
    shape = sds((2,) + block[1:])
    return call(
        weight_body,
        [shape, shape],
        [SMEM, SMEM]
        + [wide] * 2
        + [pl.BlockSpec(v.shape, lambda i, n=v.ndim: (0,) * n, pipeline_mode=pl.Buffered(1)) for v in left],
        [
            pl.BlockSpec(block, lambda i: (jnp.minimum(i, 1), 0, 0, 0)),
            pl.BlockSpec(block, lambda i: (jnp.maximum(i - 2, 0), 0, 0, 0)),
        ],
        grid=(4,),
        scratch=[pltpu.VMEM((C, rows), BF16)] * 2,
        cost=us(20),
    )(own, place, th, tl, *left)


def assemble_body(place_ref, near2, far2, near1, far1, w1_ref, w2_ref, turned):
    place = place_ref[0]
    half, depth = near1.shape[0], near1.shape[1]
    for side, (first, second) in enumerate(((near1, near2), (far1, far2))):
        for index in range(half):
            rows = pl.ds(pl.multiple_of((place ^ (2 * index + side)) * depth, depth), depth)
            w1_ref[rows, :] = first[index]
            turned[rows, :] = second[index]
    w2_ref[...] = turned[...].T


def assemble(place, near2, far2, near1, far1):
    return call(
        assemble_body,
        [sds((C, HID)), sds((HID, C))],
        [SMEM] + [VMEM] * 4,
        [VMEM] * 2,
        scratch=[pltpu.VMEM((C, HID), F32)],
        cost=us(3),
    )(place, near2, far2, near1, far1)


def first_back_body(*refs):
    own_ref, f6_ref, first = refs[:3]
    d_ref, dx_ref = refs[-2:]
    own = own_ref[0]
    pieces = refs[2 : 2 + PARTS] if len(first.shape) == 3 else None
    table3 = f6_ref[...]
    for part in range(PARTS):
        base = (own ^ part) * SLABS if pieces else part * SLABS
        for pair in range(SLABS // 2):
            slabs = (2 * pair, 2 * pair + 1)
            values = [pieces[part][s] if pieces else first[part, s] for s in slabs]
            columns = jnp.concatenate([pad_rows(v) for v in values], axis=1)
            out = mm(table3, right3(columns))
            for index, s in enumerate(slabs):
                d_ref[base + s] = out[:, index * LANES : (index + 1) * LANES]
                dx_ref[base + s] = values[index]


def first_back(own, pieces, f6, keep, chunk):
    args = [own, f6, *pieces]
    in_specs = [SMEM, whole((128, 384))] + [whole(piece.shape) for piece in pieces]
    aliases = {}
    if keep is not None:
        for index, array in enumerate(keep):
            aliases[len(args)] = index
            args.append(array)
            in_specs.append(ANY)
    return call(
        first_back_body,
        [sds((SMAX, LANES, LANES)), sds((SMAX, SMAX, LANES))],
        in_specs,
        [
            pl.BlockSpec((GROUP, LANES, LANES), lambda i: (chunk, 0, 0)),
            pl.BlockSpec((GROUP, SMAX, LANES), lambda i: (chunk, 0, 0)),
        ],
        grid=(1,),
        aliases=aliases,
        cost=us(4),
    )(*args)


def rows3(value):
    one, two = split2(value)
    return jnp.concatenate([one, one, two], axis=0)


def mix_back_body(*refs):
    re_ref, im_ref, a_ref, p_ref, o_ref, g3_ref, w1t, w2t, gt3_ref = refs[:9]
    sums = refs[-4:]
    dw1, dw2, db1, db2 = sums
    if len(refs) == 15:
        dre, dim = refs[9:11]
    else:
        gb_ref = refs[13]
        dre, dim, pack = refs[14:17]

    @pl.when(pl.program_id(0) == 0)
    def _():
        for index, ref in enumerate(sums):
            ref[...] = jnp.zeros_like(ref) if len(refs) == 15 else refs[9 + index][...]

    for half in range(WIDTH // 4):
        rows = pl.ds(half * TILE, TILE)
        dz = to_rows(mm(g3_ref[...], right3(gather_columns(re_ref, im_ref, 4 * half))))
        do = jnp.where(jnp.abs(o_ref[rows, :]) > SHRINK, dz, 0.0)
        pre = p_ref[rows, :]
        cdf, pdf = phi_pair(pre)
        dw2[...] += mm(rows3(pre * cdf), right3(do), TN)
        db2[...] += fold_rows(do)
        dp = mm(left3(do), w2t[...]) * (cdf + pre * pdf)
        dw1[...] += mm(rows3(a_ref[rows, :]), right3(dp), TN)
        db1[...] += fold_rows(dp)
        dx = mm(left3(dp), w1t[...])
        scatter_columns(dre, dim, 4 * half, mm(gt3_ref[...], right3(to_columns(dx))))

    if len(refs) == 15:
        return

    @pl.when(pl.program_id(0) == pl.num_programs(0) - 1)
    def _():
        low = lax.broadcasted_iota(jnp.int32, (FREQ, LANES), 1) < FREQ
        for index, ref in enumerate((dw1, dw2)):
            full = ref[...]
            same = full[:LANES, :LANES] + full[LANES:, LANES:]
            cross = full[:LANES, LANES:] - full[LANES:, :LANES]
            for inner, value in enumerate((same, cross)):
                rows = pl.ds((2 * index + inner) * FREQ, FREQ)
                pack[rows, :] = jnp.where(low, value[:FREQ], value[FREQ:])
        sums = [jnp.sum(ref[...], axis=0, keepdims=True) for ref in (db1, db2)]
        lines = [sums[0][:, :LANES], sums[0][:, LANES:], sums[1][:, :LANES], sums[1][:, LANES:]]
        lines.append(jnp.sum(gb_ref[...], axis=0, keepdims=True))
        pack[4 * FREQ : 4 * FREQ + 8] = jnp.concatenate(lines + [jnp.zeros((3, LANES), F32)], axis=0)


def mix_backward(d, a, p, o, g6, w1t, w2t, gt3, carry, grad_b2):
    count = FREQ // WIDTH
    skip = 0 if carry is None else count // 2
    re = pl.BlockSpec((SMAX, WIDTH, LANES), lambda j: (0, skip + j, 0))
    im = pl.BlockSpec((SMAX, WIDTH, LANES), lambda j: (0, count + skip + j, 0))
    out = pl.BlockSpec((SMAX, WIDTH, LANES), lambda j: (0, j, 0))
    rows = pl.BlockSpec((WIDTH * FREQ, 256), lambda j: (skip + j, 0))
    half = sds((SMAX, FREQ // 2, LANES))
    args = [d, d, a, p, o, g6, w1t, w2t, gt3]
    in_specs = [re, im, rows, rows, rows, whole((128, 768))]
    in_specs += [whole((768, 256)), whole((768, 256)), whole((256, 384))]
    sums = [(256, 256), (256, 256), (8, 256), (8, 256)]
    shapes, out_specs, scratch = [half, half], [out, out], []
    if carry is None:
        shapes += [sds(shape) for shape in sums]
        out_specs += [whole(shape) for shape in sums]
    else:
        args += [*carry, grad_b2]
        in_specs += [whole(shape) for shape in sums] + [whole((8, LANES))]
        shapes.append(sds((PACK, LANES)))
        out_specs.append(whole((PACK, LANES)))
        scratch = [pltpu.VMEM(shape, F32) for shape in sums]
    return call(
        mix_back_body, shapes, in_specs, out_specs, grid=(count // 2,), scratch=scratch, cost=us(13)
    )(*args)


def last_back_body(re0, re1, im0, im1, dx_ref, xhat_ref, gain_ref, ft3_ref, pack_ref, *refs):
    b1_refs, norm_refs = refs[:CHUNKS], refs[CHUNKS : 2 * CHUNKS]
    dn_ref, pack = refs[2 * CHUNKS : 2 * CHUNKS + 2]
    sums, small = refs[-1 - PARTS : -1], refs[-1]
    step = pl.program_id(0)

    @pl.when(step == 0)
    def _():
        small[...] = jnp.zeros_like(small)
        norms = norm_refs[0][...]
        for ref in norm_refs[1:]:
            norms = norms + ref[...]
        norms = [jnp.sum(norms[i], axis=0, keepdims=True) for i in range(2)]
        for part in range(PARTS):
            total = b1_refs[0][part]
            for ref in b1_refs[1:]:
                total = total + ref[part]
            total = jnp.sum(total, axis=0, keepdims=True)
            lines = [total[:, part_lanes(i)] for i in range(4)]
            lines += [value[:, part_lanes(part)] for value in norms]
            lines.append(jnp.zeros((2, LANES), F32))
            sums[part][2 * STEPS] = jnp.concatenate(lines, axis=0)

    gain = gain_ref[...]
    for pair in range(STAGE // 2):
        slabs = (2 * pair, 2 * pair + 1)
        columns = [jnp.concatenate([re0[s], re1[s], im0[s], im1[s]], axis=0) for s in slabs]
        out = mm(ft3_ref[...], right3(jnp.concatenate(columns, axis=1)))[:SMAX]
        for index, s in enumerate(slabs):
            grad = dx_ref[s] + out[:, index * LANES : (index + 1) * LANES]
            dn_ref[s] = grad
            product = grad * xhat_ref[s]
            small[0] += fold_rows(product)
            small[1] += fold_rows(grad)
            for which, value in enumerate((grad, product)):
                row = jnp.sum(pad_rows(value * gain).T, axis=0, keepdims=True)
                for ref in sums:
                    block = which * STEPS + step * THIRDS + s // SLABS
                    ref[block, pl.ds(s % SLABS, 1), :] = row

    @pl.when(step == pl.num_programs(0) - 1)
    def _():
        pack[...] = pack_ref[...]
        for index in range(2):
            where = pl.ds(4 * FREQ + 5 + index, 1)
            pack[where, :] = jnp.sum(small[index], axis=0, keepdims=True)


def last_back(quarters, dx, xhat, gain, ft3, pack, b1s, norms):
    half = pl.BlockSpec((STAGE, FREQ // 2, LANES), lambda i: (i, 0, 0))
    field = pl.BlockSpec((STAGE, SMAX, LANES), lambda i: (i, 0, 0))
    shape = (2 * STEPS + 1, SLABS, LANES)
    return call(
        last_back_body,
        [sds((SMAX, SMAX, LANES)), sds((PACK, LANES))] + [sds(shape)] * PARTS,
        [half] * 4
        + [field, field, whole((1, LANES)), whole((128, 384)), whole((PACK, LANES))]
        + [whole((4, 8, HID))] * CHUNKS
        + [whole((2, 8, C))] * CHUNKS,
        [field, whole((PACK, LANES))] + [whole(shape)] * PARTS,
        grid=(SMAX // STAGE,),
        scratch=[pltpu.VMEM((2, 8, LANES), F32)],
        cost=us(13),
    )(*quarters, dx, xhat, gain, ft3, pack, *b1s, *norms)


def final_body(side_ref, dx_ref, dn_ref, xhat_ref, r_ref, gain_ref, *refs):
    sums, out_ref = refs[:PARTS], refs[PARTS]
    step = pl.program_id(0)
    side = side_ref[0]
    for third in range(THIRDS):
        block = step * THIRDS + third
        inverse = r_ref[pl.ds(third * SLABS, SLABS), :]
        total = [sum(ref[which * STEPS + block] for ref in sums) for which in range(2)]
        first = total[0] * (inverse * (1.0 / C))
        second = total[1] * (inverse * (1.0 / C))
        wide = [spread8(value) for value in (inverse, first, second)]
        for inner in range(SLABS):
            slab = third * SLABS + inner
            scaled = dn_ref[slab] * gain_ref[...]
            scale, shift, slope = [slab_of(value, inner) for value in wide]
            value = dx_ref[slab] + (scale * scaled - shift - xhat_ref[slab] * slope)
            out_ref[slab] = jnp.where(slab_mask(step * STAGE + slab, side), value, 0.0)


def final_stage(side, dx, dn, xhat, sums, r, gain):
    field = pl.BlockSpec((STAGE, SMAX, LANES), lambda i: (i, 0, 0))
    return call(
        final_body,
        sds((SMAX, SMAX, LANES)),
        [SMEM, field, field, field, pl.BlockSpec((STAGE, LANES), lambda i: (i, 0)), whole((1, LANES))]
        + [whole((2 * STEPS + 1, SLABS, LANES))] * PARTS,
        field,
        grid=(SMAX // STAGE,),
        cost=us(13),
    )(side, dx, dn, xhat, r, gain, *sums)


def output_body(side_ref, x_ref, y_ref, tip_ref, b2_ref, out_ref):
    step = pl.program_id(0)
    side = side_ref[0]
    for part in range(PARTS):
        for inner in range(SLABS):
            slab = part * SLABS + inner
            branch = jnp.where(step < CHUNKS - 1, y_ref[part, 0, inner], tip_ref[part, inner])
            value = x_ref[slab] + branch + b2_ref[...]
            out_ref[slab] = jnp.where(slab_mask(step * GROUP + slab, side), value, 0.0)


def output_stage(side, x1, y, tip, b2):
    field = pl.BlockSpec((GROUP, SMAX, LANES), lambda i: (i, 0, 0))
    early = pl.BlockSpec(
        (PARTS, 1, SLABS, SMAX, LANES), lambda i: (0, jnp.minimum(i, CHUNKS - 2), 0, 0, 0)
    )
    return call(
        output_body,
        sds((SMAX, SMAX, LANES)),
        [SMEM, field, early, whole((PARTS, SLABS, SMAX, LANES)), whole((1, LANES))],
        field,
        grid=(CHUNKS,),
        cost=us(5),
    )(side, x1, y, tip, b2)


def swap(value, axis, size, distance):
    return lax.ppermute(value, axis, [(i, i ^ distance) for i in range(size)])


def exchange(pieces):
    return [pieces[0]] + [swap(pieces[part], "blk", PARTS, part) for part in range(1, PARTS)]


def after(value, *others):
    return lax.optimization_barrier((value, *others))[0]


def scatter_one(send, held, size):
    half = size // 2
    got = held + swap(send, "blk", PARTS, 1)
    gate = yield got
    mine = got[:, :half] + swap(after(got[:, half:], gate), "dp", size, 1)
    yield mine
    yield mine[0] + swap(mine[1], "blk", PARTS, 2)


def scatter_two(send, held, size):
    half, cut = size // 2, send.shape[2] // 2
    got = held + swap(send, "blk", PARTS, 1)
    yield got
    one = got[:, :half, :cut] + swap(got[:, half:, :cut], "dp", size, 1)
    two = got[0, :, cut:] + swap(got[1, :, cut:], "blk", PARTS, 2)
    yield one, two
    one = one[0] + swap(one[1], "blk", PARTS, 2)
    two = two[:half] + swap(two[half:], "dp", size, 1)
    yield one, two
    yield jnp.concatenate([one, two], axis=1)


def scatter_last(mine, size, gate):
    total = after(mine[0], gate)
    for index in range(1, size // 2):
        total = total + swap(mine[index], "dp", size, 2 * index)
    return total


def gather_near(piece, size, gate):
    return jnp.stack([after(piece, gate)] + [swap(piece, "dp", size, 2 * index) for index in range(1, size // 2)])


def per_device(
    dp_size,
    block_input,
    cotangent,
    item_sides,
    item_modes,
    ln1_gain,
    ln1_bias,
    spec_w1,
    spec_b1,
    spec_w2,
    spec_b2,
    ln2_gain,
    ln2_bias,
    mlp_w1,
    mlp_b1,
    mlp_w2,
    mlp_b2,
):
    own = lax.axis_index("blk").astype(jnp.int32).reshape(1)
    place = lax.axis_index("dp").astype(jnp.int32).reshape(1)
    cube = (SMAX, SMAX, LANES)
    x = block_input.reshape(cube)
    gain1, bias1 = ln1_gain.reshape(1, LANES), ln1_bias.reshape(1, LANES)

    depth = C // dp_size
    share = jnp.stack([lax.dynamic_slice_in_dim(w, place[0] * depth, depth) for w in (mlp_w1, mlp_w2)])
    share = swap(share, "blk", PARTS, 2)

    moment = moments(
        item_sides, x, mlp_b1.reshape(4, LANES), ln2_gain.reshape(1, LANES), ln2_bias.reshape(1, LANES)
    )
    stats = exchange([moment] * PARTS)
    f6, g6, ft3, gt3, w1c, w2c, w1t, w2t = prepare(table(item_sides, item_modes), spec_w1, spec_w2)
    g_parts, grad_b2 = cotangent_pieces(item_sides, after(cotangent.reshape(cube), f6, *stats[1:]))
    g = lax.all_to_all(g_parts, "blk", 0, 0).reshape(PARTS, CHUNKS * PIECE, LANES)
    far = lax.all_gather(after(share, moment), "dp", axis=0)
    mlp_w1, mlp_w2, _ = lax.optimization_barrier((mlp_w1, mlp_w2, stats[3]))
    one = [mlp_w1, swap(mlp_w1, "blk", PARTS, 1)]
    two = [mlp_w2, swap(mlp_w2, "blk", PARTS, 1)]

    b, xn, xhat, r = first_stage(item_sides, after(x, g_parts), stats, gain1, bias1, f6)
    bre, bim, a, p, o = mix_forward(
        b, g6, w1c, spec_b1.reshape(1, 256), w2c, spec_b2.reshape(1, 256), gt3
    )
    far = after(far, bre)
    far = [far, swap(far, "blk", PARTS, 1)]
    x1, x1_in = None, []
    for chunk in range(CHUNKS):
        field = after(xn, g, *x1_in[0]) if chunk == CHUNKS - 1 else xn
        pieces, x1 = last_stage(own, bre, bim, field, ft3, x1, chunk)
        if chunk < CHUNKS - 1:
            x1_in.append(exchange(pieces))
    x1_last = lax.all_to_all(pieces[0].reshape(PARTS, PIECE, LANES), "blk", 0, 0)

    weights = split_weights(own, one, two, far)
    keep, dx_in, b1s, norms = None, [], [], []

    def take(results):
        dx_in.append([v.reshape(SLABS, SMAX, LANES) for v in exchange(results[:4])])
        b1s.append(results[4])
        norms.append(results[5])

    xs = [[piece.reshape(PIECE, LANES) for piece in pieces] for pieces in x1_in]
    xs[0][0] = after(xs[0][0], x1)
    for chunk in range(CHUNKS - 1):
        results = feed(own, xs[chunk], g, weights, stats, keep, chunk)
        keep = results[:7]
        take(results[7:])
    branch = lax.all_to_all(keep[4], "blk", 0, 0)
    results = feed_forward(own, after(x1_last, *dx_in[0]), weights, stats, keep[:4], CHUNKS - 1)
    hh, hl, nh, nl = results[:4]
    tip = results[4]
    send2, held2 = weight_grads(own, place, dp_size, [g], hh, hl)
    chain2 = scatter_one(send2, held2, dp_size)
    local = list(results[5:])
    got2 = chain2.send(None)
    local[1] = after(local[1], held2)
    results = feed_backward(own, g, weights, local, stats, keep[5:], CHUNKS - 1)
    ph, plo, dx_last = results[:3]
    dx_in.append([lax.all_to_all(dx_last, "blk", 0, 0).reshape(PARTS, SLABS, SMAX, LANES)])
    b1s.append(results[3])
    norms.append(results[4])

    chain1 = scatter_two(*weight_grads(own, place, dp_size, [nh, nl], after(ph, got2, branch, *dx_in[1]), plo), dp_size)

    mine2 = chain2.send(ph)
    dx_in[0][0] = after(dx_in[0][0], mine2, *dx_in[2])
    back = first_back(own, dx_in[0], f6, None, 0)
    back = first_back(own, dx_in[1], f6, back, 1)
    dx_in[2][0] = after(dx_in[2][0], chain1.send(None))
    d, dx = first_back(own, dx_in[2], f6, back, 2)
    tip = lax.all_to_all(after(tip, d), "blk", 0, 0)
    mine2 = chain2.send(None)
    early = mix_backward(after(d, mine2), a, p, o, g6, w1t, w2t, gt3, None, None)
    second = scatter_last(after(mine2, d), dp_size, early[0])
    d_late = after(d, second, *chain1.send(None))
    late = mix_backward(d_late, a, p, o, g6, w1t, w2t, gt3, early[2:], grad_b2)
    near2 = gather_near(after(second, early[0]), dp_size, late[0])
    dx_last = after(dx, near2, tip, *chain1.send(None))
    quarters = [early[0], late[0], early[1], late[1]]
    dn, pack, *sums = last_back(quarters, dx_last, xhat, gain1, ft3, late[2], b1s, norms)
    first = scatter_last(chain1.send(None), dp_size, dn)
    sums = exchange([after(value, first) for value in sums])
    far2 = swap(after(near2, *sums[1:]), "dp", dp_size, 1)
    input_grad = final_stage(item_sides, dx, dn, xhat, sums, r, gain1)
    tail = sums[0][-1] + sums[1][-1] + sums[2][-1] + sums[3][-1]
    pack = jnp.concatenate([pack, tail], axis=0)
    near1 = gather_near(first, dp_size, input_grad)
    pack = after(pack, input_grad) + swap(pack, "dp", dp_size, 1)
    block_output = output_stage(
        item_sides,
        after(x1, input_grad, near1),
        branch.reshape(PARTS, CHUNKS - 1, SLABS, SMAX, LANES),
        tip.reshape(PARTS, SLABS, SMAX, LANES),
        mlp_b2.reshape(1, LANES),
    )
    distance = 2
    while distance < dp_size:
        pack = pack + swap(pack, "dp", dp_size, distance)
        distance *= 2
    far1 = swap(near1, "dp", dp_size, 1)
    w1_grad, w2_grad = assemble(place, near2, far2, near1, far1)

    spec = pack[: 4 * FREQ].reshape(2, 2, FREQ, 2, FREQ).transpose(0, 1, 3, 2, 4)
    rest = pack[4 * FREQ :]
    return (
        block_output.reshape(SMAX * SMAX, LANES),
        input_grad.reshape(SMAX * SMAX, LANES),
        rest[5],
        rest[6],
        spec[0],
        rest[0:2].reshape(2, 2, 64),
        spec[1],
        rest[2:4].reshape(2, 2, 64),
        rest[12],
        rest[13],
        w1_grad,
        rest[8:12].reshape(HID),
        w2_grad,
        rest[4],
    )


def solution(mesh):
    in_specs = (
        P("dp", "blk"),
        P("dp", "blk"),
        P("dp"),
        P("dp"),
        P("blk"),
        P("blk"),
        P(None, "blk", None, None),
        P(None, "blk", None),
        P(None, "blk", None, None),
        P(None, "blk", None),
        P("blk"),
        P("blk"),
        P(None, "blk"),
        P("blk"),
        P("blk", None),
        P("blk"),
    )
    out_specs = (
        P("dp", "blk"),
        P("dp", "blk"),
        P("blk"),
        P("blk"),
        P(None, "blk", None, None),
        P(None, "blk", None),
        P(None, "blk", None, None),
        P(None, "blk", None),
        P("blk"),
        P("blk"),
        P(None, "blk"),
        P("blk"),
        P("blk", None),
        P("blk"),
    )
    return jax.shard_map(
        functools.partial(per_device, mesh.shape["dp"]),
        mesh=mesh,
        in_specs=in_specs,
        out_specs=out_specs,
        check_vma=False,
    )
```

time: 597 us -> 436 us (0.73)
  waiting for transfers between devices: 130 us -> 34.8 us
  blocking collectives: 94.1 us -> 0 us
  starting transfers between devices: 33.2 us -> 75.2 us
  Pallas kernels: 293 us -> 282 us
    all_gather x3 -> x0, blocking collectives: 94.1 us -> none  [the longest x1 76.4 us: per_device(): stats = lax.all_gather(moments(item_sides, x), 'blk', axis=0)]
    ppermute x33 -> x47, waiting for transfers between devices: 86.5 us -> 34.8 us  [swap(): return lax.ppermute(value, axis, [(i, i ^ distance) for i in range(size)])]
    psum x1 -> x0, waiting for transfers between devices: 42.2 us -> none  [per_device(): mine = lax.psum(mine, 'dp')]
    all_to_all x0 -> x5, starting transfers between devices: none -> 23 us  [the longest x1 5.05 us: per_device(): lax.all_to_all(g_parts, 'blk', 0, 0).reshape(PARTS, CHUNKS * PIECE, LANES)]
    ppermute x33 -> x47, starting transfers between devices: 33.1 us -> 52.1 us  [swap(): return lax.ppermute(value, axis, [(i, i ^ distance) for i in range(size)])]
    pallas_call x15 -> x17, Pallas kernels: 220 us -> 219 us  [the longest x4 98.9 us: feed_call(): call(body, [specs[kind][0] for kind in outs], in_specs, [specs[kind][1] f...]
  transfers between devices with their start and end apart: 37 -> 53, of which waited for: 12 -> 10; matrix products, arithmetic and copies ran while one was open for 3% -> 3% of each run, Pallas kernels for 37% -> 64%
where the time goes in v2:
time: 436 us; the launch traced here: 429 us
  Pallas kernels  282 us (65%)
  starting transfers between devices  75.2 us (17%)
  waiting for transfers between devices  34.8 us (8%)
  between operations  16.3 us (4%)
  local copies, waits for them, and re-layouts  11.8 us (3%)
  other arithmetic  8.63 us (2%)
    pallas_call x4, Pallas kernels, feed_call(): call(body, [specs[kind][0] for kind in outs], in_specs, [specs[kind][1] f...  98.9 us
    ppermute x47, starting transfers between devices, swap(): return lax.ppermute(value, axis, [(i, i ^ distance) for i in range(size)])  52.1 us
    pallas_call x2, Pallas kernels, weight_grads(): call(weight_body, [shape, shape], [SMEM, SMEM] + [wide] * 2 + [pl.BlockSp...  44.2 us
    ppermute x47, waiting for transfers between devices, swap(): return lax.ppermute(value, axis, [(i, i ^ distance) for i in range(size)])  34.8 us
    pallas_call x1, Pallas kernels, mix_forward(): call(mix_body, [half, half] + [sds((4096, 256))] * 3, [re, im, whole((128...  28.4 us
    pallas_call x2, Pallas kernels, mix_backward(): call(mix_back_body, shapes, in_specs, out_specs, grid=(count // 2,), scra...  24.4 us
    pallas_call x3, Pallas kernels, last_stage(): call(last_body, [sds(shape) for shape in pieces] + [sds((SMAX, SMAX, LANE...  13.1 us
    pallas_call x3, Pallas kernels, first_back(): call(first_back_body, [sds((SMAX, LANES, LANES)), sds((SMAX, SMAX, LANES)...  11.7 us
  transfers between devices with their start and end apart: 53, of which 10 were waited for; matrix products, arithmetic and copies ran while one was open for 3% of the time, Pallas kernels for 64%

profile of v2, /device:TPU:0, one launch (start us, length us, event | category | flops | bytes accessed | tf_op | source)
XLA Modules:
  0.0 428.5 jit_solution(6113906174641887837)
XLA Ops:
  8.3 3.0 collective-permute-start.8
  11.9 4.9 %shard_map.264.refs_0_.refs_10_.refs_6_.refs_9_ = f32[25,8,128]{2,1,0:T(8,128)} custom-call(s32[1]{0:T(128)} %copy.72.side_ref, f32[96,96,128]{2,1,0:T(8,128)} %bitcast.119, f32[4,128]{1,0:T(4,128)} %bitcast.131, f32[1,128]{1,0:T(1,128)} %bitcast.132, f32[1,128]{1,0:T(1,128)} %bitcast.133), custom_call_target="tpu_custom_call" | custom-call | flops 6000000000 | bytes 18000000 | tf_op jit(solution)/shard_map/pallas_call | solution.py:222
  22.7 2.8 shard_map.263
  26.0 5.8 %shard_map.265 = (f32[4,3,8,96,128]{4,3,2,1,0:T(8,128)}, f32[8,128]{1,0:T(8,128)}) custom-call(s32[1]{0:T(128)} %copy.72.side_ref, f32[96,96,128]{2,1,0:T(8,128)} %bitcast.118), custom_call_target="tpu_custom_call" | custom-call | flops 5000000000 | bytes 15000000 | tf_op jit(solution)/shard_map/pallas_call | solution.py:257
  31.8 5.1 %all-to-all-start = ((f32[4,3,8,96,128]{4,3,2,1,0:T(8,128)}), f32[4,3,8,96,128]{4,3,2,1,0:T(8,128)}, u32[]{:S(2)}, u32[]{:S(2)}) async-start(f32[4,3,8,96,128]{4,3,2,1,0:T(8,128)} %get-tuple-element.148), calls=%async_computation | async-start | bytes 9437184 | tf_op jit(solution)/shard_map/all_to_all | solution.py:1146
  38.2 10.6 %shard_map.266 = (f32[96,128,128]{2,1,0:T(8,128)}, f32[96,96,128]{2,1,0:T(8,128)}, f32[96,96,128]{2,1,0:T(8,128)}, f32[96,128]{1,0:T(8,128)}) custom-call(s32[1]{0:T(128)} %copy.72.side_ref, f32[96,96,128]{2,1,0:T(8,128)} %bitcast.120, f32[25,8,128]{2,1,0:T(8,128)} %shard_map.264.refs_0_.refs_10_.refs_6_.refs_9_, f32[25,8,128]{2,1,0:T(8,128)} %copy-done.9, ...), custom_call_target="tpu_custom_call" | custom-call | flops 3000000000 | bytes 9000000 | tf_op jit(solution)/shard_map/pallas_call | solution.py:311
  48.7 28.4 %shard_map.267 = (f32[96,64,128]{2,1,0:T(8,128)}, f32[96,64,128]{2,1,0:T(8,128)}, f32[4096,256]{1,0:T(8,128)}, f32[4096,256]{1,0:T(8,128)}, f32[4096,256]{1,0:T(8,128)}) custom-call(f32[96,128,128]{2,1,0:T(8,128)} %get-tuple-element.150.re_ref.im_ref, f32[96,128,128]{2,1,0:T(8,128)} %get-tuple-element.150.re_ref.im_ref, ...), custom_call_target="tpu_custom_call" | custom-call | flops 4000000000 | bytes 12000000 | tf_op jit(solution)/shard_map/pallas_call | solution.py:391
  77.7 4.3 %shard_map.268 = (f32[8,96,128]{2,1,0:T(8,128)}, f32[8,96,128]{2,1,0:T(8,128)}, f32[8,96,128]{2,1,0:T(8,128)}, f32[8,96,128]{2,1,0:T(8,128)}, f32[96,96,128]{2,1,0:T(8,128)}) custom-call(s32[1]{0:T(128)} %bitcast.own_ref.refs_0_, f32[96,64,128]{2,1,0:T(8,128)} %get-tuple-element.155.re_ref, f32[96,64,128]{2,1,0:T(8,128)} %get-tuple-element.156.im_ref, ...), custom_call_target="tpu_custom_call" | custom-call | flops 3500000000 | bytes 10500000 | tf_op jit(solution)/shard_map/pallas_call | solution.py:442
  82.6 2.0 collective-permute-start.4
  85.6 4.2 shard_map.269
  89.8 9.7 %collective-permute-done.4 = f32[8,96,128]{2,1,0:T(8,128)S(1)} collective-permute-done((f32[8,96,128]{2,1,0:T(8,128)}, f32[8,96,128]{2,1,0:T(8,128)S(1)}, u32[]{:S(2)}, u32[]{:S(2)}) %collective-permute-start.4) | collective-permute-done | bytes 393248 | tf_op jit(solution)/shard_map/ppermute | solution.py:1067
  100.3 6.8 %collective-permute-done.5 = f32[8,96,128]{2,1,0:T(8,128)} collective-permute-done((f32[8,96,128]{2,1,0:T(8,128)}, f32[8,96,128]{2,1,0:T(8,128)}, u32[]{:S(2)}, u32[]{:S(2)}) %collective-permute-start.5) | collective-permute-done | bytes 393248 | tf_op jit(solution)/shard_map/ppermute | solution.py:1067
  107.7 4.5 %shard_map.270 = (f32[4,8,96,128]{3,2,1,0:T(8,128)}, f32[96,96,128]{2,1,0:T(8,128)}) custom-call(s32[1]{0:T(128)} %bitcast.own_ref.refs_0_, f32[96,64,128]{2,1,0:T(8,128)} %get-tuple-element.155.re_ref, f32[96,64,128]{2,1,0:T(8,128)} %get-tuple-element.156.im_ref, f32[96,96,128]{2,1,0:T(8,128)} %get-tuple-element.163.xn_ref, ...), custom_call_target="tpu_custom_call", output_to_operand_aliasing={{1}: (5, {})} | custom-call | flops 3500000000 | bytes 10500000 | tf_op jit(solution)/shard_map/pallas_call | solution.py:442
  112.2 4.0 all-to-all-start.1
  116.3 1.8 collective-permute-start.15
  118.1 7.7 %shard_map.271 = (bf16[4,512,512]{2,1,0:T(8,128)(2,1)}, bf16[4,512,512]{2,1,0:T(8,128)(2,1)}, bf16[4,512,512]{2,1,0:T(8,128)(2,1)}, bf16[4,512,512]{2,1,0:T(8,128)(2,1)}) custom-call(s32[1]{0:T(128)} %bitcast.own_ref.refs_0_, f32[512,512]{1,0:T(8,128)} %refs_0_, f32[512,512]{1,0:T(8,128)} %collective-permute-done.6.refs_1_, f32[512,512]{1,0:T(8,128)} %refs_2_, ...), custom_call_target="tpu_custom_call" | custom-call | flops 7000000000 | bytes 21000000 | tf_op jit(solution)/shard_map/pallas_call | solution.py:488
  125.9 30.7 %shard_map.272 = (bf16[2304,2048]{1,0:T(8,128)(2,1)}, bf16[2304,2048]{1,0:T(8,128)(2,1)}, bf16[2304,512]{1,0:T(8,128)(2,1)}, bf16[2304,512]{1,0:T(8,128)(2,1)}, ...) custom-call(s32[1]{0:T(128)} %bitcast.own_ref.refs_0_, ...), custom_call_target="tpu_custom_call" | custom-call | flops 28000000000 | bytes 84000000 | tf_op jit(solution)/shard_map/pallas_call | solution.py:717
  159.2 30.7 %shard_map.273 = (bf16[2304,2048]{1,0:T(8,128)(2,1)}, bf16[2304,2048]{1,0:T(8,128)(2,1)}, bf16[2304,512]{1,0:T(8,128)(2,1)}, bf16[2304,512]{1,0:T(8,128)(2,1)}, ...) custom-call(s32[1]{0:T(128)} %bitcast.own_ref.refs_0_, ...), custom_call_target="tpu_custom_call", output_to_operand_aliasing={{0}: (14, {}), {1}: (15, {}), {2}: (16, {}), {3}: (17, {}),... | custom-call | flops 28000000000 | bytes 84000000 | tf_op jit(solution)/shard_map/pallas_call | solution.py:717
  191.1 4.8 %all-to-all-start.3 = ((f32[4,2,768,128]{3,2,1,0:T(8,128)}), f32[4,2,768,128]{3,2,1,0:T(8,128)}, u32[]{:S(2)}, u32[]{:S(2)}) async-start(f32[4,2,768,128]{3,2,1,0:T(8,128)} %get-tuple-element.209), calls=%async_computation.3 | async-start | bytes 6291456 | tf_op jit(solution)/shard_map/all_to_all | solution.py:1180
  196.0 20.1 %shard_map.274 = (bf16[2304,2048]{1,0:T(8,128)(2,1)}, bf16[2304,2048]{1,0:T(8,128)(2,1)}, bf16[2304,512]{1,0:T(8,128)(2,1)}, bf16[2304,512]{1,0:T(8,128)(2,1)}, ...) custom-call(s32[1]{0:T(128)} %bitcast.own_ref.refs_0_, ...), custom_call_target="tpu_custom_call", output_to_operand_aliasing={{0}: (10, {}), {1}: (11, {}), {2}: (12, {}), {3}: (13, {})} | custom-call | flops 17999998976 | bytes 54000000 | tf_op jit(solution)/shard_map/pallas_call | solution.py:717
  216.1 22.2 %shard_map.275 = (f32[2,8,64,512]{3,2,1,0:T(8,128)}, f32[2,8,64,512]{3,2,1,0:T(8,128)}) custom-call(s32[1]{0:T(128)} %bitcast.own_ref.refs_0_, s32[1]{0:T(128)} %bitcast.27.place_ref, bf16[2304,2048]{1,0:T(8,128)(2,1)} %get-tuple-element.199.th, bf16[2304,2048]{1,0:T(8,128)(2,1)} %get-tuple-element.200.tl, f32[4,2304,128]{2,1,0:T(8,128)} %bitcast.10.refs_5_.refs_0_.refs_1_), custom_call_target="tpu_custom_call" | custom-call | flops 20000000000 | bytes 60000000 | tf_op jit(solution)/shard_map/pallas_call | solution.py:783
  238.9 1.9 collective-permute-start.18
  240.8 17.5 %shard_map.276 = (bf16[2304,2048]{1,0:T(8,128)(2,1)}, bf16[2304,2048]{1,0:T(8,128)(2,1)}, f32[4,768,128]{2,1,0:T(8,128)}, f32[4,8,512]{2,1,0:T(8,128)}, f32[2,8,512]{2,1,0:T(8,128)}) custom-call(s32[1]{0:T(128)} %bitcast.own_ref.refs_0_, f32[4,2304,128]{2,1,0:T(8,128)} %bitcast.10.refs_5_.refs_0_.refs_1_, ...), custom_call_target="tpu_custom_call", output_to_operand_aliasing={{0}: (13, {}), {1}: (14, {})} | custom-call | flops 1000000000 | bytes 3000000 | tf_op jit(solution)/shard_map/pallas_call | solution.py:717
  259.0 4.6 %all-to-all-start.2 = ((f32[4,768,128]{2,1,0:T(8,128)}), f32[4,768,128]{2,1,0:T(8,128)}, u32[]{:S(2)}, u32[]{:S(2)}) async-start(f32[4,768,128]{2,1,0:T(8,128)} %get-tuple-element.206), calls=%async_computation.2 | async-start | bytes 3145728 | tf_op jit(solution)/shard_map/all_to_all | solution.py:1191
  263.6 1.8 collective-permute-start.21
  265.3 22.0 %shard_map.277 = (f32[2,8,64,512]{3,2,1,0:T(8,128)}, f32[2,8,64,512]{3,2,1,0:T(8,128)}) custom-call(s32[1]{0:T(128)} %bitcast.own_ref.refs_0_, s32[1]{0:T(128)} %bitcast.27.place_ref, bf16[2304,2048]{1,0:T(8,128)(2,1)} %get-tuple-element.214.th, bf16[2304,2048]{1,0:T(8,128)(2,1)} %get-tuple-element.215.tl, bf16[2304,512]{1,0:T(8,128)(2,1)} %get-tuple-element.216.refs_0_, ...), custom_call_target="tpu_custom_call" | custom-call | flops 20000000000 | bytes 60000000 | tf_op jit(solution)/shard_map/pallas_call | solution.py:783
  289.4 1.7 collective-permute-start.22
  291.2 3.9 shard_map.278
  295.0 4.0 shard_map.279
  299.0 4.0 collective-permute-done.22
  303.9 2.1 add.91
  307.7 3.9 shard_map.280
  314.7 4.6 %all-to-all-start.4 = ((f32[4,1,768,128]{3,2,1,0:T(8,128)}), f32[4,1,768,128]{3,2,1,0:T(8,128)}, u32[]{:S(2)}, u32[]{:S(2)}) async-start(f32[4,1,768,128]{3,2,1,0:T(8,128)} %get-tuple-element.250), calls=%async_computation.4 | async-start | bytes 3145728 | tf_op jit(solution)/shard_map/all_to_all | solution.py:1203
  321.0 2.6 collective-permute-start.25
  323.6 12.1 %shard_map.281 = (f32[96,32,128]{2,1,0:T(8,128)}, f32[96,32,128]{2,1,0:T(8,128)}, f32[256,256]{1,0:T(8,128)}, f32[256,256]{1,0:T(8,128)}, f32[8,256]{1,0:T(8,128)}, /*index=5*/f32[8,256]{1,0:T(8,128)}) custom-call(f32[96,128,128]{2,1,0:T(8,128)} %get-tuple-element.238.refs_0_.refs_1_, f32[96,128,128]{2,1,0:T(8,128)} %get-tuple-element.238.refs_0_.refs_1_, ...), custom_call_target="tpu_custom_call" | custom-call | flops 12999999488 | bytes 39000000 | tf_op jit(solution)/shard_map/pallas_call | solution.py:937
  335.9 2.8 collective-permute-start.30
  341.7 1.9 collective-permute-start.31
  344.1 12.4 %shard_map.282 = (f32[96,32,128]{2,1,0:T(8,128)}, f32[96,32,128]{2,1,0:T(8,128)}, f32[264,128]{1,0:T(8,128)}) custom-call(f32[96,128,128]{2,1,0:T(8,128)} %get-tuple-element.238.refs_0_.refs_1_, f32[96,128,128]{2,1,0:T(8,128)} %get-tuple-element.238.refs_0_.refs_1_, f32[4096,256]{1,0:T(8,128)} %get-tuple-element.230.refs_2_, ...), custom_call_target="tpu_custom_call" | custom-call | flops 12999999488 | bytes 39000000 | tf_op jit(solution)/shard_map/pallas_call | solution.py:937
  357.6 2.5 collective-permute-start.35
  360.2 10.3 %shard_map.283 = (f32[96,96,128]{2,1,0:T(8,128)}, f32[264,128]{1,0:T(8,128)}, f32[25,8,128]{2,1,0:T(8,128)}, f32[25,8,128]{2,1,0:T(8,128)}, f32[25,8,128]{2,1,0:T(8,128)}, /*index=5*/f32[25,8,128]{2,1,0:T(8,128)}) custom-call(f32[96,32,128]{2,1,0:T(8,128)} %get-tuple-element.235.re0, f32[96,32,128]{2,1,0:T(8,128)} %get-tuple-element.244.re1, ...), custom_call_target="tpu_custom_call" | custom-call | flops 12999999488 | bytes 39000000 | tf_op jit(solution)/shard_map/pallas_call | solution.py:994
  372.6 2.9 collective-permute-start.41
  381.2 9.3 %shard_map.284 = f32[96,96,128]{2,1,0:T(8,128)} custom-call(s32[1]{0:T(128)} %copy.72.side_ref, f32[96,96,128]{2,1,0:T(8,128)} %get-tuple-element.251.dx_ref, f32[96,96,128]{2,1,0:T(8,128)} %get-tuple-element.260.dn_ref, f32[96,96,128]{2,1,0:T(8,128)} %get-tuple-element.252.xhat_ref, f32[96,128]{1,0:T(8,128)} %get-tuple-element.261.r_ref, ...), custom_call_target="tpu_custom_call" | custom-call | flops 12999999488 | bytes 39000000 | tf_op jit(solution)/shard_map/pallas_call | solution.py:1029
  390.5 1.8 collective-permute-start.43
  394.4 2.0 collective-permute-done.43
  396.4 2.9 collective-permute-start.44
  399.4 6.4 %shard_map.285 = f32[96,96,128]{2,1,0:T(8,128)} custom-call(s32[1]{0:T(128)} %copy.72.side_ref, f32[96,96,128]{2,1,0:T(8,128)} %get-tuple-element.272.x_ref, f32[4,2,8,96,128]{4,3,2,1,0:T(8,128)} %bitcast.55.y_ref, f32[4,8,96,128]{3,2,1,0:T(8,128)} %bitcast.56.tip_ref, f32[1,128]{1,0:T(1,128)} %bitcast.138), custom_call_target="tpu_custom_call" | custom-call | flops 5000000000 | bytes 15000000 | tf_op jit(solution)/shard_map/pallas_call | solution.py:1056
  409.2 8.1 %collective-permute-done.46.far1 = f32[4,64,512]{2,1,0:T(8,128)S(1)} collective-permute-done((f32[4,64,512]{2,1,0:T(8,128)S(1)}, f32[4,64,512]{2,1,0:T(8,128)S(1)}, u32[]{:S(2)}, u32[]{:S(2)}) %collective-permute-start.46) | collective-permute-done | bytes 524320 | tf_op jit(solution)/shard_map/ppermute | solution.py:1067
  418.2 3.2 shard_map.286
  (177 shorter events, 45.0 us)
Async XLA Ops:
  7.2 70.0 %all-gather.3.cloned.1.call-start = ((), (), s32[]{:S(2)}) async-start(), calls=%async_computation.5 | async-start | bytes 2359296 | tf_op jit(solution)/shard_map/all_gather | solution.py:1147
  8.3 9.3 %collective-permute-start.8 = (f32[2,64,512]{2,1,0:T(8,128)S(1)}, f32[2,64,512]{2,1,0:T(8,128)S(1)}, u32[]{:S(2)}, u32[]{:S(2)}) collective-permute-start(f32[2,64,512]{2,1,0:T(8,128)S(1)} %pad_maximum_fusion.2), channel_id=1, source_target_pairs={{0,2},{1,3},{2,0},{3,1},{4,6},{5,7},{6,4},{7,5},{8,10},{9,11},{10,... | collective-permute-start | bytes 786440 | tf_op jit(solution)/shard_map/ppermute | solution.py:1067
  18.3 7.2 %collective-permute-start.2 = (f32[25,8,128]{2,1,0:T(8,128)}, f32[25,8,128]{2,1,0:T(8,128)S(1)}, u32[]{:S(2)}, u32[]{:S(2)}) collective-permute-start(f32[25,8,128]{2,1,0:T(8,128)} %shard_map.264.refs_0_.refs_10_.refs_6_.refs_9_), channel_id=1, source_target_pairs={{0,3},{1,2},{2,1},{3,0},{4,7},{5,6},{6,5},{7,4},{8,11},{9,10},{10,... | collective-permute-start | bytes 307208 | tf_op jit(solution)/shard_map/ppermute | solution.py:1067
  18.7 7.3 %collective-permute-start.1 = (f32[25,8,128]{2,1,0:T(8,128)}, f32[25,8,128]{2,1,0:T(8,128)S(1)}, u32[]{:S(2)}, u32[]{:S(2)}) collective-permute-start(f32[25,8,128]{2,1,0:T(8,128)} %shard_map.264.refs_0_.refs_10_.refs_6_.refs_9_), channel_id=1, source_target_pairs={{0,2},{1,3},{2,0},{3,1},{4,6},{5,7},{6,4},{7,5},{8,10},{9,11},{10,... | collective-permute-start | bytes 307208 | tf_op jit(solution)/shard_map/ppermute | solution.py:1067
  31.8 75.9 %all-to-all-start = ((f32[4,3,8,96,128]{4,3,2,1,0:T(8,128)}), f32[4,3,8,96,128]{4,3,2,1,0:T(8,128)}, u32[]{:S(2)}, u32[]{:S(2)}) async-start(f32[4,3,8,96,128]{4,3,2,1,0:T(8,128)} %get-tuple-element.148), calls=%async_computation | async-start | bytes 9437184 | tf_op jit(solution)/shard_map/all_to_all | solution.py:1146
  77.2 40.9 %collective-permute-start.9 = (f32[8,2,64,512]{3,2,1,0:T(8,128)}, f32[8,2,64,512]{3,2,1,0:T(8,128)}, u32[]{:S(2)}, u32[]{:S(2)}) collective-permute-start(f32[8,2,64,512]{3,2,1,0:T(8,128)} %bitcast.121), channel_id=1, source_target_pairs={{0,1},{1,0},{2,3},{3,2},{4,5},{5,4},{6,7},{7,6},{8,9},{9,8},{10,11... | collective-permute-start | bytes 6291464 | tf_op jit(solution)/shard_map/ppermute | solution.py:1067
  82.1 34.2 %collective-permute-start.6 = (f32[512,512]{1,0:T(8,128)S(1)}, f32[512,512]{1,0:T(8,128)}, u32[]{:S(2)}, u32[]{:S(2)}) collective-permute-start(f32[512,512]{1,0:T(8,128)S(1)} %copy-done.10), channel_id=1, source_target_pairs={{0,1},{1,0},{2,3},{3,2},{4,5},{5,4},{6,7},{7,6},{8,9},{9,8},{10,11... | collective-permute-start | bytes 3145736 | tf_op jit(solution)/shard_map/ppermute | solution.py:1067
  82.5 35.6 %collective-permute-start.7 = (f32[512,512]{1,0:T(8,128)}, f32[512,512]{1,0:T(8,128)}, u32[]{:S(2)}, u32[]{:S(2)}) collective-permute-start(f32[512,512]{1,0:T(8,128)} %refs_2_), channel_id=1, source_target_pairs={{0,1},{1,0},{2,3},{3,2},{4,5},{5,4},{6,7},{7,6},{8,9},{9,8},{10,11... | collective-permute-start | bytes 3145736 | tf_op jit(solution)/shard_map/ppermute | solution.py:1067
  82.6 16.9 %collective-permute-start.4 = (f32[8,96,128]{2,1,0:T(8,128)}, f32[8,96,128]{2,1,0:T(8,128)S(1)}, u32[]{:S(2)}, u32[]{:S(2)}) collective-permute-start(f32[8,96,128]{2,1,0:T(8,128)} %get-tuple-element.161), channel_id=1, source_target_pairs={{0,2},{1,3},{2,0},{3,1},{4,6},{5,7},{6,4},{7,5},{8,10},{9,11},{10,... | collective-permute-start | bytes 1179656 | tf_op jit(solution)/shard_map/ppermute | solution.py:1067
  84.6 22.5 %collective-permute-start.5 = (f32[8,96,128]{2,1,0:T(8,128)}, f32[8,96,128]{2,1,0:T(8,128)}, u32[]{:S(2)}, u32[]{:S(2)}) collective-permute-start(f32[8,96,128]{2,1,0:T(8,128)} %get-tuple-element.162), channel_id=1, source_target_pairs={{0,3},{1,2},{2,1},{3,0},{4,7},{5,6},{6,5},{7,4},{8,11},{9,10},{10,... | collective-permute-start | bytes 1179656 | tf_op jit(solution)/shard_map/ppermute | solution.py:1067
  100.3 56.8 %collective-permute-start.13 = (f32[8,96,128]{2,1,0:T(8,128)}, f32[8,96,128]{2,1,0:T(8,128)S(1)}, u32[]{:S(2)}, u32[]{:S(2)}) collective-permute-start(f32[8,96,128]{2,1,0:T(8,128)} %get-tuple-element.183), channel_id=1, source_target_pairs={{0,1},{1,0},{2,3},{3,2},{4,5},{5,4},{6,7},{7,6},{8,9},{9,8},{10,11... | collective-permute-start | bytes 1179656 | tf_op jit(solution)/shard_map/ppermute | solution.py:1067
  107.1 51.4 %collective-permute-start.14 = (f32[8,96,128]{2,1,0:T(8,128)}, f32[8,96,128]{2,1,0:T(8,128)}, u32[]{:S(2)}, u32[]{:S(2)}) collective-permute-start(f32[8,96,128]{2,1,0:T(8,128)} %get-tuple-element.184), channel_id=1, source_target_pairs={{0,2},{1,3},{2,0},{3,1},{4,6},{5,7},{6,4},{7,5},{8,10},{9,11},{10,... | collective-permute-start | bytes 1179656 | tf_op jit(solution)/shard_map/ppermute | solution.py:1067
  112.2 77.7 %all-to-all-start.1 = ((f32[4,768,128]{2,1,0:T(8,128)}), f32[4,768,128]{2,1,0:T(8,128)S(1)}, u32[]{:S(2)}, u32[]{:S(2)}) async-start(f32[4,768,128]{2,1,0:T(8,128)} %bitcast.108), calls=%async_computation.1 | async-start | bytes 3145728 | tf_op jit(solution)/shard_map/all_to_all | solution.py:1164
  116.3 42.2 %collective-permute-start.15 = (f32[8,96,128]{2,1,0:T(8,128)}, f32[8,96,128]{2,1,0:T(8,128)S(1)}, u32[]{:S(2)}, u32[]{:S(2)}) collective-permute-start(f32[8,96,128]{2,1,0:T(8,128)} %get-tuple-element.185), channel_id=1, source_target_pairs={{0,3},{1,2},{2,1},{3,0},{4,7},{5,6},{6,5},{7,4},{8,11},{9,10},{10,... | collective-permute-start | bytes 1179656 | tf_op jit(solution)/shard_map/ppermute | solution.py:1067
  156.5 39.4 %collective-permute-start.10 = (f32[768,128]{1,0:T(8,128)}, f32[768,128]{1,0:T(8,128)S(1)}, u32[]{:S(2)}, u32[]{:S(2)}) collective-permute-start(f32[768,128]{1,0:T(8,128)} %get-tuple-element.178), channel_id=1, source_target_pairs={{0,1},{1,0},{2,3},{3,2},{4,5},{5,4},{6,7},{7,6},{8,9},{9,8},{10,11... | collective-permute-start | bytes 1179656 | tf_op jit(solution)/shard_map/ppermute | solution.py:1067
  157.0 39.0 %collective-permute-start.11 = (f32[768,128]{1,0:T(8,128)}, f32[768,128]{1,0:T(8,128)S(1)}, u32[]{:S(2)}, u32[]{:S(2)}) collective-permute-start(f32[768,128]{1,0:T(8,128)} %get-tuple-element.179), channel_id=1, source_target_pairs={{0,2},{1,3},{2,0},{3,1},{4,6},{5,7},{6,4},{7,5},{8,10},{9,11},{10,... | collective-permute-start | bytes 1179656 | tf_op jit(solution)/shard_map/ppermute | solution.py:1067
  157.0 38.9 %collective-permute-start.12 = (f32[768,128]{1,0:T(8,128)}, f32[768,128]{1,0:T(8,128)S(1)}, u32[]{:S(2)}, u32[]{:S(2)}) collective-permute-start(f32[768,128]{1,0:T(8,128)} %get-tuple-element.180), channel_id=1, source_target_pairs={{0,3},{1,2},{2,1},{3,0},{4,7},{5,6},{6,5},{7,4},{8,11},{9,10},{10,... | collective-permute-start | bytes 1179656 | tf_op jit(solution)/shard_map/ppermute | solution.py:1067
  191.1 67.9 %all-to-all-start.3 = ((f32[4,2,768,128]{3,2,1,0:T(8,128)}), f32[4,2,768,128]{3,2,1,0:T(8,128)}, u32[]{:S(2)}, u32[]{:S(2)}) async-start(f32[4,2,768,128]{3,2,1,0:T(8,128)} %get-tuple-element.209), calls=%async_computation.3 | async-start | bytes 6291456 | tf_op jit(solution)/shard_map/all_to_all | solution.py:1180
  238.3 20.0 %collective-permute-start.16 = (f32[2,8,64,512]{3,2,1,0:T(8,128)}, f32[2,8,64,512]{3,2,1,0:T(8,128)S(1)}, u32[]{:S(2)}, u32[]{:S(2)}) collective-permute-start(f32[2,8,64,512]{3,2,1,0:T(8,128)} %get-tuple-element.208), channel_id=1, source_target_pairs={{0,1},{1,0},{2,3},{3,2},{4,5},{5,4},{6,7},{7,6},{8,9},{9,8},{10,11... | collective-permute-start | bytes 6291464 | tf_op jit(solution)/shard_map/ppermute | solution.py:1067
  238.9 24.6 %collective-permute-start.17 = (f32[768,128]{1,0:T(8,128)}, f32[768,128]{1,0:T(8,128)}, u32[]{:S(2)}, u32[]{:S(2)}) collective-permute-start(f32[768,128]{1,0:T(8,128)} %get-tuple-element.211), channel_id=1, source_target_pairs={{0,1},{1,0},{2,3},{3,2},{4,5},{5,4},{6,7},{7,6},{8,9},{9,8},{10,11... | collective-permute-start | bytes 1179656 | tf_op jit(solution)/shard_map/ppermute | solution.py:1067
  238.9 24.6 %collective-permute-start.18 = (f32[768,128]{1,0:T(8,128)}, f32[768,128]{1,0:T(8,128)}, u32[]{:S(2)}, u32[]{:S(2)}) collective-permute-start(f32[768,128]{1,0:T(8,128)} %get-tuple-element.212), channel_id=1, source_target_pairs={{0,2},{1,3},{2,0},{3,1},{4,6},{5,7},{6,4},{7,5},{8,10},{9,11},{10,... | collective-permute-start | bytes 1179656 | tf_op jit(solution)/shard_map/ppermute | solution.py:1067
  240.8 22.8 %collective-permute-start.19 = (f32[768,128]{1,0:T(8,128)S(1)}, f32[768,128]{1,0:T(8,128)}, u32[]{:S(2)}, u32[]{:S(2)}) collective-permute-start(f32[768,128]{1,0:T(8,128)S(1)} %copy-done.21), channel_id=1, source_target_pairs={{0,3},{1,2},{2,1},{3,0},{4,7},{5,6},{6,5},{7,4},{8,11},{9,10},{10,... | collective-permute-start | bytes 1179656 | tf_op jit(solution)/shard_map/ppermute | solution.py:1067
  259.0 30.4 %all-to-all-start.2 = ((f32[4,768,128]{2,1,0:T(8,128)}), f32[4,768,128]{2,1,0:T(8,128)}, u32[]{:S(2)}, u32[]{:S(2)}) async-start(f32[4,768,128]{2,1,0:T(8,128)} %get-tuple-element.206), calls=%async_computation.2 | async-start | bytes 3145728 | tf_op jit(solution)/shard_map/all_to_all | solution.py:1191
  263.6 25.6 %collective-permute-start.21 = (f32[2,4,64,512]{3,2,1,0:T(8,128)S(1)}, f32[2,4,64,512]{3,2,1,0:T(8,128)S(1)}, u32[]{:S(2)}, u32[]{:S(2)}) collective-permute-start(f32[2,4,64,512]{3,2,1,0:T(8,128)S(1)} %slice.150), channel_id=1, source_target_pairs={{0,4},{4,0},{8,12},{12,8},{16,20},{20,16},{24,28},{28,24},{1,5},{5... | collective-permute-start | bytes 3145736 | tf_op jit(solution)/shard_map/ppermute | solution.py:1067
  287.4 16.5 %collective-permute-start.20 = (f32[2,8,64,512]{3,2,1,0:T(8,128)}, f32[2,8,64,512]{3,2,1,0:T(8,128)}, u32[]{:S(2)}, u32[]{:S(2)}) collective-permute-start(f32[2,8,64,512]{3,2,1,0:T(8,128)} %get-tuple-element.219), channel_id=1, source_target_pairs={{0,1},{1,0},{2,3},{3,2},{4,5},{5,4},{6,7},{7,6},{8,9},{9,8},{10,11... | collective-permute-start | bytes 6291464 | tf_op jit(solution)/shard_map/ppermute | solution.py:1067
  289.4 13.6 %collective-permute-start.22 = (f32[4,64,512]{2,1,0:T(8,128)S(1)}, f32[4,64,512]{2,1,0:T(8,128)S(1)}, u32[]{:S(2)}, u32[]{:S(2)}) collective-permute-start(f32[4,64,512]{2,1,0:T(8,128)S(1)} %slice_bitcast_fusion.2), channel_id=1, source_target_pairs={{0,2},{1,3},{2,0},{3,1},{4,6},{5,7},{6,4},{7,5},{8,10},{9,11},{10,... | collective-permute-start | bytes 1572872 | tf_op jit(solution)/shard_map/ppermute | solution.py:1067
  311.7 28.7 %collective-permute-start.26 = (f32[2,4,32,512]{3,2,1,0:T(8,128)}, f32[2,4,32,512]{3,2,1,0:T(8,128)}, u32[]{:S(2)}, u32[]{:S(2)}) collective-permute-start(f32[2,4,32,512]{3,2,1,0:T(8,128)} %slice.154), channel_id=1, source_target_pairs={{0,4},{4,0},{8,12},{12,8},{16,20},{20,16},{24,28},{28,24},{1,5},{5... | collective-permute-start | bytes 1572872 | tf_op jit(solution)/shard_map/ppermute | solution.py:1067
  313.4 28.2 %collective-permute-start.27 = (f32[8,32,512]{2,1,0:T(8,128)}, f32[8,32,512]{2,1,0:T(8,128)S(1)}, u32[]{:S(2)}, u32[]{:S(2)}) collective-permute-start(f32[8,32,512]{2,1,0:T(8,128)} %slice_bitcast_fusion), channel_id=1, source_target_pairs={{0,2},{1,3},{2,0},{3,1},{4,6},{5,7},{6,4},{7,5},{8,10},{9,11},{10,... | collective-permute-start | bytes 1572872 | tf_op jit(solution)/shard_map/ppermute | solution.py:1067
  314.7 45.5 %all-to-all-start.4 = ((f32[4,1,768,128]{3,2,1,0:T(8,128)}), f32[4,1,768,128]{3,2,1,0:T(8,128)}, u32[]{:S(2)}, u32[]{:S(2)}) async-start(f32[4,1,768,128]{3,2,1,0:T(8,128)} %get-tuple-element.250), calls=%async_computation.4 | async-start | bytes 3145728 | tf_op jit(solution)/shard_map/all_to_all | solution.py:1203
  319.3 16.4 %collective-permute-start.23 = (f32[64,512]{1,0:T(8,128)S(1)}, f32[64,512]{1,0:T(8,128)S(1)}, u32[]{:S(2)}, u32[]{:S(2)}) collective-permute-start(f32[64,512]{1,0:T(8,128)S(1)} %get-tuple-element.282), channel_id=1, source_target_pairs={{0,8},{4,12},{8,0},{12,4},{16,24},{20,28},{24,16},{28,20},{1,9},{5... | collective-permute-start | bytes 393224 | tf_op jit(solution)/shard_map/ppermute | solution.py:1067
  321.0 14.7 %collective-permute-start.25 = (f32[64,512]{1,0:T(8,128)S(1)}, f32[64,512]{1,0:T(8,128)S(1)}, u32[]{:S(2)}, u32[]{:S(2)}) collective-permute-start(f32[64,512]{1,0:T(8,128)S(1)} %get-tuple-element.283), channel_id=1, source_target_pairs={{0,24},{4,28},{8,16},{12,20},{16,8},{20,12},{24,0},{28,4},{1,25},{... | collective-permute-start | bytes 393224 | tf_op jit(solution)/shard_map/ppermute | solution.py:1067
  323.6 12.3 %collective-permute-start.24 = (f32[64,512]{1,0:T(8,128)S(1)}, f32[64,512]{1,0:T(8,128)S(1)}, u32[]{:S(2)}, u32[]{:S(2)}) collective-permute-start(f32[64,512]{1,0:T(8,128)S(1)} %get-tuple-element.284), channel_id=1, source_target_pairs={{0,16},{4,20},{8,24},{12,28},{16,0},{20,4},{24,8},{28,12},{1,17},{... | collective-permute-start | bytes 393224 | tf_op jit(solution)/shard_map/ppermute | solution.py:1067
  335.9 20.5 %collective-permute-start.30 = (f32[64,512]{1,0:T(8,128)S(1)}, f32[64,512]{1,0:T(8,128)S(1)}, u32[]{:S(2)}, u32[]{:S(2)}) collective-permute-start(f32[64,512]{1,0:T(8,128)S(1)} %add_add_fusion.1), channel_id=1, source_target_pairs={{0,24},{4,28},{8,16},{12,20},{16,8},{20,12},{24,0},{28,4},{1,25},{... | collective-permute-start | bytes 393224 | tf_op jit(solution)/shard_map/ppermute | solution.py:1067
  338.8 17.7 %collective-permute-start.29 = (f32[64,512]{1,0:T(8,128)S(1)}, f32[64,512]{1,0:T(8,128)S(1)}, u32[]{:S(2)}, u32[]{:S(2)}) collective-permute-start(f32[64,512]{1,0:T(8,128)S(1)} %add_add_fusion.1), channel_id=1, source_target_pairs={{0,16},{4,20},{8,24},{12,28},{16,0},{20,4},{24,8},{28,12},{1,17},{... | collective-permute-start | bytes 393224 | tf_op jit(solution)/shard_map/ppermute | solution.py:1067
  339.1 17.4 %collective-permute-start.28 = (f32[64,512]{1,0:T(8,128)S(1)}, f32[64,512]{1,0:T(8,128)S(1)}, u32[]{:S(2)}, u32[]{:S(2)}) collective-permute-start(f32[64,512]{1,0:T(8,128)S(1)} %add_add_fusion.1), channel_id=1, source_target_pairs={{0,8},{4,12},{8,0},{12,4},{16,24},{20,28},{24,16},{28,20},{1,9},{5... | collective-permute-start | bytes 393224 | tf_op jit(solution)/shard_map/ppermute | solution.py:1067
  341.7 14.9 %collective-permute-start.31 = (f32[4,32,512]{2,1,0:T(8,128)S(1)}, f32[4,32,512]{2,1,0:T(8,128)S(1)}, u32[]{:S(2)}, u32[]{:S(2)}) collective-permute-start(f32[4,32,512]{2,1,0:T(8,128)S(1)} %slice_bitcast_fusion.4), channel_id=1, source_target_pairs={{0,2},{1,3},{2,0},{3,1},{4,6},{5,7},{6,4},{7,5},{8,10},{9,11},{10,... | collective-permute-start | bytes 786440 | tf_op jit(solution)/shard_map/ppermute | solution.py:1067
  343.6 13.0 %collective-permute-start.32 = (f32[4,32,512]{2,1,0:T(8,128)S(1)}, f32[4,32,512]{2,1,0:T(8,128)S(1)}, u32[]{:S(2)}, u32[]{:S(2)}) collective-permute-start(f32[4,32,512]{2,1,0:T(8,128)S(1)} %slice.160), channel_id=1, source_target_pairs={{0,4},{4,0},{8,12},{12,8},{16,20},{20,16},{24,28},{28,24},{1,5},{5... | collective-permute-start | bytes 786440 | tf_op jit(solution)/shard_map/ppermute | solution.py:1067
  356.7 13.9 %collective-permute-start.33 = (f32[64,512]{1,0:T(8,128)S(1)}, f32[64,512]{1,0:T(8,128)S(1)}, u32[]{:S(2)}, u32[]{:S(2)}) collective-permute-start(f32[64,512]{1,0:T(8,128)S(1)} %get-tuple-element.278), channel_id=1, source_target_pairs={{0,8},{4,12},{8,0},{12,4},{16,24},{20,28},{24,16},{28,20},{1,9},{5... | collective-permute-start | bytes 393224 | tf_op jit(solution)/shard_map/ppermute | solution.py:1067
  357.6 12.9 %collective-permute-start.35 = (f32[64,512]{1,0:T(8,128)S(1)}, f32[64,512]{1,0:T(8,128)S(1)}, u32[]{:S(2)}, u32[]{:S(2)}) collective-permute-start(f32[64,512]{1,0:T(8,128)S(1)} %get-tuple-element.280), channel_id=1, source_target_pairs={{0,24},{4,28},{8,16},{12,20},{16,8},{20,12},{24,0},{28,4},{1,25},{... | collective-permute-start | bytes 393224 | tf_op jit(solution)/shard_map/ppermute | solution.py:1067
  360.1 10.5 %collective-permute-start.34 = (f32[64,512]{1,0:T(8,128)S(1)}, f32[64,512]{1,0:T(8,128)S(1)}, u32[]{:S(2)}, u32[]{:S(2)}) collective-permute-start(f32[64,512]{1,0:T(8,128)S(1)} %get-tuple-element.281), channel_id=1, source_target_pairs={{0,16},{4,20},{8,24},{12,28},{16,0},{20,4},{24,8},{28,12},{1,17},{... | collective-permute-start | bytes 393224 | tf_op jit(solution)/shard_map/ppermute | solution.py:1067
  370.9 7.1 %collective-permute-start.38 = (f32[25,8,128]{2,1,0:T(8,128)}, f32[25,8,128]{2,1,0:T(8,128)S(1)}, u32[]{:S(2)}, u32[]{:S(2)}) collective-permute-start(f32[25,8,128]{2,1,0:T(8,128)} %get-tuple-element.270), channel_id=1, source_target_pairs={{0,3},{1,2},{2,1},{3,0},{4,7},{5,6},{6,5},{7,4},{8,11},{9,10},{10,... | collective-permute-start | bytes 307208 | tf_op jit(solution)/shard_map/ppermute | solution.py:1067
  372.6 20.3 %collective-permute-start.41 = (f32[64,512]{1,0:T(8,128)S(1)}, f32[64,512]{1,0:T(8,128)S(1)}, u32[]{:S(2)}, u32[]{:S(2)}) collective-permute-start(f32[64,512]{1,0:T(8,128)S(1)} %add_add_fusion), channel_id=1, source_target_pairs={{0,24},{4,28},{8,16},{12,20},{16,8},{20,12},{24,0},{28,4},{1,25},{... | collective-permute-start | bytes 393224 | tf_op jit(solution)/shard_map/ppermute | solution.py:1067
  375.5 17.3 %collective-permute-start.40 = (f32[64,512]{1,0:T(8,128)S(1)}, f32[64,512]{1,0:T(8,128)S(1)}, u32[]{:S(2)}, u32[]{:S(2)}) collective-permute-start(f32[64,512]{1,0:T(8,128)S(1)} %add_add_fusion), channel_id=1, source_target_pairs={{0,16},{4,20},{8,24},{12,28},{16,0},{20,4},{24,8},{28,12},{1,17},{... | collective-permute-start | bytes 393224 | tf_op jit(solution)/shard_map/ppermute | solution.py:1067
  375.8 17.0 %collective-permute-start.39 = (f32[64,512]{1,0:T(8,128)S(1)}, f32[64,512]{1,0:T(8,128)S(1)}, u32[]{:S(2)}, u32[]{:S(2)}) collective-permute-start(f32[64,512]{1,0:T(8,128)S(1)} %add_add_fusion), channel_id=1, source_target_pairs={{0,8},{4,12},{8,0},{12,4},{16,24},{20,28},{24,16},{28,20},{1,9},{5... | collective-permute-start | bytes 393224 | tf_op jit(solution)/shard_map/ppermute | solution.py:1067
  379.6 10.9 %collective-permute-start.42 = (f32[272,128]{1,0:T(8,128)S(1)}, f32[272,128]{1,0:T(8,128)S(1)}, u32[]{:S(2)}, u32[]{:S(2)}) collective-permute-start(f32[272,128]{1,0:T(8,128)S(1)} %pad_maximum_fusion.3), channel_id=1, source_target_pairs={{0,4},{4,0},{8,12},{12,8},{16,20},{20,16},{24,28},{28,24},{1,5},{5... | collective-permute-start | bytes 417800 | tf_op jit(solution)/shard_map/ppermute | solution.py:1067
  392.3 16.9 %collective-permute-start.45 = (f32[4,64,512]{2,1,0:T(8,128)S(1)}, f32[4,64,512]{2,1,0:T(8,128)S(1)}, u32[]{:S(2)}, u32[]{:S(2)}) collective-permute-start(f32[4,64,512]{2,1,0:T(8,128)S(1)} %pad_maximum_fusion.near2), channel_id=1, source_target_pairs={{0,4},{4,0},{8,12},{12,8},{16,20},{20,16},{24,28},{28,24},{1,5},{5... | collective-permute-start | bytes 1572872 | tf_op jit(solution)/shard_map/ppermute | solution.py:1067
  392.9 24.5 %collective-permute-start.46 = (f32[4,64,512]{2,1,0:T(8,128)S(1)}, f32[4,64,512]{2,1,0:T(8,128)S(1)}, u32[]{:S(2)}, u32[]{:S(2)}) collective-permute-start(f32[4,64,512]{2,1,0:T(8,128)S(1)} %pad_maximum_fusion.1.near1), channel_id=1, source_target_pairs={{0,4},{4,0},{8,12},{12,8},{16,20},{20,16},{24,28},{28,24},{1,5},{5... | collective-permute-start | bytes 1572872 | tf_op jit(solution)/shard_map/ppermute | solution.py:1067
  396.4 9.4 %collective-permute-start.44 = (f32[272,128]{1,0:T(8,128)S(1)}, f32[272,128]{1,0:T(8,128)S(1)}, u32[]{:S(2)}, u32[]{:S(2)}) collective-permute-start(f32[272,128]{1,0:T(8,128)S(1)} %add.109), channel_id=1, source_target_pairs={{0,16},{4,20},{8,24},{12,28},{16,0},{20,4},{24,8},{28,12},{1,17},{... | collective-permute-start | bytes 417800 | tf_op jit(solution)/shard_map/ppermute | solution.py:1067
  (31 other events, 258.4 us)
Sparse Core Ops, SparseCore 0:
  18.4 50.7 all-gather.2
